TPU v7x, 32 devices: a whole 2x2x4 slice. The times are simulated.
32 devices in a mesh: row: 8 (over y, x, core), col: 4 (over z).
Axes of the slice: x: 2, y: 2, z: 4, core: 2. Of those that a mesh axis runs over, the one named last changes fastest.
Arguments:
- trial_vectors: bfloat16 [6144, 256], P(('row', 'col')), may hold values from -6 to 6
- h_blocks: bfloat16 [4, 8, 12, 64, 8, 128], P('col', None, None, None, 'row'), may hold values from -0.1875 to 0.1875
- block_col: int32 [4, 8, 12, 8, 2], P('col', 'row'), may hold values from 0 to 2
- block_count: int32 [4, 8, 12, 8], P('col', 'row'), may hold values from 0 to 2, as said below
- center: float32 [1], replicated, may hold values from -0.5 to 0.5
- half_width: float32 [1], replicated, may hold values from 1.5 to 2.5
Outputs:
- filtered: float32 [6144, 256], P(('row', 'col'))
Inputs may be any that keep to these rules, and one draw needn't show every extreme that they name: Only the first block_count slots of a block row and source domain hold blocks. In every column group one row domain has all 2 slots used in every block row for every source domain.
All inputs are finite; a program needn't handle non-finite values.
Results may differ from a plain program's by a relative error of at most 0.019.
Values may be sent and summed in bfloat16 or wider, within the bound.
No kernel may reach another device: no remote copies, remote signals or barrier semaphores. Data moves between devices by JAX's collectives and lax.ppermute only.
A program may use at most 64 MiB of HBM per device.

v0:
```python
import jax
import jax.numpy as jnp
from jax import lax
from jax.sharding import PartitionSpec as P

BLOCK = 64
VECTORS = 256
PER = 2
DEGREE = 6
BLOCK_ROWS = 3


def body(trial_vectors, h_blocks, block_col, block_count, center, half_width):
    arrived = lax.all_to_all(h_blocks, "row", split_axis=1, concat_axis=4, tiled=True)
    row_count = lax.axis_size("row")
    col_count = lax.axis_size("col")
    domain = BLOCK_ROWS * col_count
    filled = (
        lax.broadcasted_iota(jnp.int32, (domain, row_count, PER), 2) < block_count[0, 0][:, :, None]
    )
    shaped = arrived[0, 0].reshape(domain, BLOCK, row_count, PER, BLOCK)
    blocks = jnp.where(filled[:, None, :, :, None], shaped, jnp.zeros((), jnp.bfloat16))
    blocks = blocks.reshape(col_count, BLOCK_ROWS, BLOCK, row_count * PER * BLOCK)
    sources = lax.broadcasted_iota(jnp.int32, (domain, row_count, PER), 1)
    columns = (sources * BLOCK_ROWS + block_col[0, 0]).reshape(
        col_count, BLOCK_ROWS, row_count * PER
    )
    centre_value = center[0]
    half_value = half_width[0]

    def operator(current):
        gathered = lax.all_gather(current, "row", axis=0, tiled=True).reshape(
            row_count * BLOCK_ROWS, BLOCK, VECTORS
        )

        def group_rows(entries):
            group_blocks, group_columns = entries
            picked = gathered[group_columns].reshape(BLOCK_ROWS, row_count * PER * BLOCK, VECTORS)
            return jnp.einsum(
                "rak,rkv->rav", group_blocks, picked, preferred_element_type=jnp.float32
            )

        partial_value = lax.map(group_rows, (blocks, columns)).reshape(domain * BLOCK, VECTORS)
        owned = lax.psum_scatter(
            partial_value.astype(jnp.bfloat16), "col", scatter_dimension=0, tiled=True
        ).astype(jnp.float32)
        return owned

    previous = trial_vectors.astype(jnp.float32)
    current = (operator(trial_vectors) - centre_value * previous) / half_value
    for degree_step in range(DEGREE - 1):
        product = operator(current.astype(jnp.bfloat16))
        following = 2.0 * (product - centre_value * current) / half_value - previous
        previous, current = (current, following)
    return current


def solution(mesh):
    in_specs = (
        P(("row", "col"), None),
        P("col", None, None, None, "row", None),
        P("col", "row", None, None, None),
        P("col", "row", None, None),
        P(),
        P(),
    )
    out_specs = P(("row", "col"), None)
    return jax.shard_map(body, mesh=mesh, in_specs=in_specs, out_specs=out_specs, check_vma=False)
```

profile of v0, /device:TPU:0, one launch (start us, length us, event | category | flops | bytes accessed | tf_op | source)
XLA Modules:
  0.0 303.4 jit_solution(4536157744505953639)
XLA Ops:
  6.5 5.3 %all-to-all-start = ((bf16[1,8,12,64,1,128]{5,3,4,2,0,1:T(8,128)(2,1)}), bf16[1,8,12,64,1,128]{5,3,4,2,0,1:T(8,128)(2,1)S(1)}, u32[]{:S(2)}, u32[]{:S(2)}) async-start(bf16[1,8,12,64,1,128]{5,3,4,2,0,1:T(8,128)(2,1)} %bitcast.176), calls=%async_computation | async-start | bytes 3145728 | tf_op jit(solution)/shard_map/all_to_all | solution.py:14
  12.9 26.2 %all_gather.18 = bf16[1536,256]{1,0:T(8,128)(2,1)} all-gather(bf16[192,256]{1,0:T(8,128)(2,1)S(1)} %copy-done), channel_id=1, replica_groups=mesh['row'=8,'col'=4] {'row'}, dimensions={0}, use_global_device_ids=true | all-gather | bytes 884736 | tf_op jit(solution)/shard_map/all_gather | solution.py:32
  39.1 2.4 copy.27
  41.5 2.5 reshape_squeeze.3
  45.0 11.8 %while.60 = (s32[]{:T(128)}, bf16[4,3,64,256]{3,2,1,0:T(8,128)(2,1)}, bf16[4,3,64,1024]{3,2,1,0:T(8,128)(2,1)S(1)}, s32[4,3,16]{2,0,1:T(4,128)S(1)}, bf16[24,64,256]{2,1,0:T(8,128)(2,1)}, /*index=5*/s32[]{:T(128)}) while((s32[]{:T(128)}, bf16[4,3,64,256]{3,2,1,0:T(8,128)(2,1)}, bf16[4,3,64,1024]{3,2,1,0:T(8,128)(2,1)S(1)}, ...), condition=%wide.region_1.2_spmd, body=%wide.region_0.1_spmd.sunk | while | flops 100664464 | bytes 5314761 | solution.py:43
  45.1 1.8 gather_fusion
  48.0 1.8 gather_fusion
  49.8 1.0 fusion.70
  51.0 1.8 gather_fusion
  52.8 1.0 fusion.70
  53.9 1.8 gather_fusion
  55.7 1.0 fusion.70
  58.1 19.9 %reduce-scatter.7.cloned.1.call-done = bf16[192,256]{1,0:T(8,128)(2,1)} async-done(((bf16[768,256]{1,0:T(8,128)(2,1)}), bf16[192,256]{1,0:T(8,128)(2,1)}) %reduce-scatter.7.cloned.1.call-update) | async-done | bytes 98320 | tf_op jit(solution)/shard_map/reduce_scatter | solution.py:44
  78.9 11.4 %all_gather.19 = bf16[1536,256]{1,0:T(8,128)(2,1)} all-gather(bf16[192,256]{1,0:T(8,128)(2,1)S(1)} %fusion.33), channel_id=1, replica_groups=mesh['row'=8,'col'=4] {'row'}, dimensions={0}, use_global_device_ids=true | all-gather | bytes 884736 | tf_op jit(solution)/shard_map/all_gather | solution.py:32
  91.1 11.8 %while.61 = (s32[]{:T(128)}, bf16[4,3,64,256]{3,2,1,0:T(8,128)(2,1)}, bf16[4,3,64,1024]{3,2,1,0:T(8,128)(2,1)S(1)}, s32[4,3,16]{2,0,1:T(4,128)S(1)}, bf16[24,64,256]{2,1,0:T(8,128)(2,1)}, /*index=5*/s32[]{:T(128)}) while((s32[]{:T(128)}, bf16[4,3,64,256]{3,2,1,0:T(8,128)(2,1)}, bf16[4,3,64,1024]{3,2,1,0:T(8,128)(2,1)S(1)}, ...), condition=%wide.region_4.5_spmd, body=%wide.region_3.4_spmd.sunk | while | flops 100664464 | bytes 5314761 | solution.py:43
  91.2 1.8 gather_fusion.1
  93.0 1.0 fusion.74
  94.1 1.8 gather_fusion.1
  95.9 1.0 fusion.74
  97.1 1.8 gather_fusion.1
  98.9 1.0 fusion.74
  100.0 1.8 gather_fusion.1
  102.9 18.2 %reduce-scatter.9.cloned.1.call-done = bf16[192,256]{1,0:T(8,128)(2,1)} async-done(((bf16[768,256]{1,0:T(8,128)(2,1)}), bf16[192,256]{1,0:T(8,128)(2,1)}) %reduce-scatter.9.cloned.1.call-update) | async-done | bytes 98320 | tf_op jit(solution)/shard_map/reduce_scatter | solution.py:44
  122.1 11.4 %all_gather.20 = bf16[1536,256]{1,0:T(8,128)(2,1)} all-gather(bf16[192,256]{1,0:T(8,128)(2,1)S(1)} %fusion.34), channel_id=1, replica_groups=mesh['row'=8,'col'=4] {'row'}, dimensions={0}, use_global_device_ids=true | all-gather | bytes 884736 | tf_op jit(solution)/shard_map/all_gather | solution.py:32
  134.3 11.8 %while.62 = (s32[]{:T(128)}, bf16[4,3,64,256]{3,2,1,0:T(8,128)(2,1)}, bf16[4,3,64,1024]{3,2,1,0:T(8,128)(2,1)S(1)}, s32[4,3,16]{2,0,1:T(4,128)S(1)}, bf16[24,64,256]{2,1,0:T(8,128)(2,1)}, /*index=5*/s32[]{:T(128)}) while((s32[]{:T(128)}, bf16[4,3,64,256]{3,2,1,0:T(8,128)(2,1)}, bf16[4,3,64,1024]{3,2,1,0:T(8,128)(2,1)S(1)}, ...), condition=%wide.region_7.8_spmd, body=%wide.region_6.7_spmd.sunk | while | flops 100664464 | bytes 5314761 | solution.py:43
  134.4 1.8 gather_fusion.2
  136.2 1.0 fusion.78
  137.4 1.8 gather_fusion.2
  140.3 1.8 gather_fusion.2
  142.1 1.0 fusion.78
  143.2 1.8 gather_fusion.2
  146.1 18.3 %reduce-scatter.11.cloned.1.call-done = bf16[192,256]{1,0:T(8,128)(2,1)} async-done(((bf16[768,256]{1,0:T(8,128)(2,1)}), bf16[192,256]{1,0:T(8,128)(2,1)}) %reduce-scatter.11.cloned.1.call-update) | async-done | bytes 98320 | tf_op jit(solution)/shard_map/reduce_scatter | solution.py:44
  164.4 1.1 fusion.36
  165.4 11.4 %all_gather.21 = bf16[1536,256]{1,0:T(8,128)(2,1)} all-gather(bf16[192,256]{1,0:T(8,128)(2,1)S(1)} %get-tuple-element.325), channel_id=1, replica_groups=mesh['row'=8,'col'=4] {'row'}, dimensions={0}, use_global_device_ids=true | all-gather | bytes 884736 | tf_op jit(solution)/shard_map/all_gather | solution.py:32
  177.6 11.8 %while.63 = (s32[]{:T(128)}, bf16[4,3,64,256]{3,2,1,0:T(8,128)(2,1)}, bf16[4,3,64,1024]{3,2,1,0:T(8,128)(2,1)S(1)}, s32[4,3,16]{2,0,1:T(4,128)S(1)}, bf16[24,64,256]{2,1,0:T(8,128)(2,1)}, /*index=5*/s32[]{:T(128)}) while((s32[]{:T(128)}, bf16[4,3,64,256]{3,2,1,0:T(8,128)(2,1)}, bf16[4,3,64,1024]{3,2,1,0:T(8,128)(2,1)S(1)}, ...), condition=%wide.region_10.11_spmd, body=%wide.region_9.10_spmd.sunk | while | flops 100664464 | bytes 5314761 | solution.py:43
  177.7 1.8 gather_fusion.3
  179.5 1.0 fusion.82
  180.7 1.8 gather_fusion.3
  182.5 1.0 fusion.82
  183.6 1.8 gather_fusion.3
  185.4 1.0 fusion.82
  186.6 1.8 gather_fusion.3
  189.4 18.3 %reduce-scatter.13.cloned.1.call-done = bf16[192,256]{1,0:T(8,128)(2,1)} async-done(((bf16[768,256]{1,0:T(8,128)(2,1)}), bf16[192,256]{1,0:T(8,128)(2,1)}) %reduce-scatter.13.cloned.1.call-update) | async-done | bytes 98320 | tf_op jit(solution)/shard_map/reduce_scatter | solution.py:44
  207.7 1.7 fusion.35
  209.4 11.4 %all_gather.22 = bf16[1536,256]{1,0:T(8,128)(2,1)} all-gather(bf16[192,256]{1,0:T(8,128)(2,1)S(1)} %get-tuple-element.323), channel_id=1, replica_groups=mesh['row'=8,'col'=4] {'row'}, dimensions={0}, use_global_device_ids=true | all-gather | bytes 884736 | tf_op jit(solution)/shard_map/all_gather | solution.py:32
  221.6 11.8 %while.64 = (s32[]{:T(128)}, bf16[4,3,64,256]{3,2,1,0:T(8,128)(2,1)}, bf16[4,3,64,1024]{3,2,1,0:T(8,128)(2,1)S(1)}, s32[4,3,16]{2,0,1:T(4,128)S(1)}, bf16[24,64,256]{2,1,0:T(8,128)(2,1)}, /*index=5*/s32[]{:T(128)}) while((s32[]{:T(128)}, bf16[4,3,64,256]{3,2,1,0:T(8,128)(2,1)}, bf16[4,3,64,1024]{3,2,1,0:T(8,128)(2,1)S(1)}, ...), condition=%wide.region_13.14_spmd, body=%wide.region_12.13_spmd.sunk | while | flops 100664464 | bytes 5314761 | solution.py:43
  221.7 1.8 gather_fusion.4
  223.5 1.0 fusion.86
  224.7 1.8 gather_fusion.4
  226.5 1.0 fusion.86
  227.6 1.8 gather_fusion.4
  229.4 1.0 fusion.86
  230.5 1.8 gather_fusion.4
  233.4 18.3 %reduce-scatter.15.cloned.1.call-done = bf16[192,256]{1,0:T(8,128)(2,1)} async-done(((bf16[768,256]{1,0:T(8,128)(2,1)}), bf16[192,256]{1,0:T(8,128)(2,1)}) %reduce-scatter.15.cloned.1.call-update) | async-done | bytes 98320 | tf_op jit(solution)/shard_map/reduce_scatter | solution.py:44
  252.6 11.4 %all_gather.23 = bf16[1536,256]{1,0:T(8,128)(2,1)} all-gather(bf16[192,256]{1,0:T(8,128)(2,1)S(1)} %fusion.32), channel_id=1, replica_groups=mesh['row'=8,'col'=4] {'row'}, dimensions={0}, use_global_device_ids=true | all-gather | bytes 884736 | tf_op jit(solution)/shard_map/all_gather | solution.py:32
  264.8 11.8 %while.65 = (s32[]{:T(128)}, bf16[4,3,64,256]{3,2,1,0:T(8,128)(2,1)}, bf16[4,3,64,1024]{3,2,1,0:T(8,128)(2,1)S(1)}, s32[4,3,16]{2,0,1:T(4,128)S(1)}, bf16[24,64,256]{2,1,0:T(8,128)(2,1)}, /*index=5*/s32[]{:T(128)}) while((s32[]{:T(128)}, bf16[4,3,64,256]{3,2,1,0:T(8,128)(2,1)}, bf16[4,3,64,1024]{3,2,1,0:T(8,128)(2,1)S(1)}, ...), condition=%wide.region_16.17_spmd, body=%wide.region_15.16_spmd.sunk | while | flops 100664464 | bytes 5314761 | solution.py:43
  264.9 1.8 gather_fusion.5
  266.7 1.0 fusion.90
  267.9 1.8 gather_fusion.5
  270.8 1.8 gather_fusion.5
  272.6 1.0 fusion.90
  273.7 1.8 gather_fusion.5
  276.6 18.3 %reduce-scatter.17.cloned.1.call-done = bf16[192,256]{1,0:T(8,128)(2,1)} async-done(((bf16[768,256]{1,0:T(8,128)(2,1)}), bf16[192,256]{1,0:T(8,128)(2,1)}) %reduce-scatter.17.cloned.1.call-update) | async-done | bytes 98320 | tf_op jit(solution)/shard_map/reduce_scatter | solution.py:44
  294.9 1.7 divide_subtract_fusion
  (123 shorter events, 19.8 us)
Async XLA Ops:
  6.5 5.4 %copy-start.4 = (s32[1,1,12,8]{2,3,1,0:T(8,128)S(1)}, s32[1,1,12,8]{2,3,1,0:T(8,128)}, u32[]{:S(2)}) copy-start(s32[1,1,12,8]{2,3,1,0:T(8,128)} %param.21) | copy-start | bytes 1156
  6.5 5.9 %copy-start.3 = (s32[1,1,12,8,2]{2,4,3,1,0:T(2,128)S(1)}, s32[1,1,12,8,2]{2,4,3,1,0:T(2,128)}, u32[]{:S(2)}) copy-start(s32[1,1,12,8,2]{2,4,3,1,0:T(2,128)} %param.20) | copy-start | bytes 2308
  6.5 6.3 %copy-start = (bf16[192,256]{1,0:T(8,128)(2,1)S(1)}, bf16[192,256]{1,0:T(8,128)(2,1)}, u32[]{:S(2)}) copy-start(bf16[192,256]{1,0:T(8,128)(2,1)} %param.18) | copy-start | bytes 294916
  6.5 32.6 %all-to-all-start = ((bf16[1,8,12,64,1,128]{5,3,4,2,0,1:T(8,128)(2,1)}), bf16[1,8,12,64,1,128]{5,3,4,2,0,1:T(8,128)(2,1)S(1)}, u32[]{:S(2)}, u32[]{:S(2)}) async-start(bf16[1,8,12,64,1,128]{5,3,4,2,0,1:T(8,128)(2,1)} %bitcast.176), calls=%async_computation | async-start | bytes 3145728 | tf_op jit(solution)/shard_map/all_to_all | solution.py:14
  11.9 66.1 %reduce-scatter.7.cloned.1.call-start = ((), (), s32[]{:S(2)}) async-start(), calls=%async_computation.7 | async-start | bytes 491520 | tf_op jit(solution)/shard_map/reduce_scatter | solution.py:44
  56.8 64.4 %reduce-scatter.9.cloned.1.call-start = ((), (), s32[]{:S(2)}) async-start(), calls=%async_computation.8 | async-start | bytes 491520 | tf_op jit(solution)/shard_map/reduce_scatter | solution.py:44
  91.1 30.1 %copy-start.2 = (bf16[192,256]{1,0:T(8,128)(2,1)S(1)}, bf16[192,256]{1,0:T(8,128)(2,1)}, u32[]{:S(2)}) copy-start(bf16[192,256]{1,0:T(8,128)(2,1)} %reduce-scatter.7.cloned.1.call-done) | copy-start | bytes 294916
  102.9 61.5 %reduce-scatter.11.cloned.1.call-start = ((), (), s32[]{:S(2)}) async-start(), calls=%async_computation.9 | async-start | bytes 491520 | tf_op jit(solution)/shard_map/reduce_scatter | solution.py:44
  146.1 61.6 %reduce-scatter.13.cloned.1.call-start = ((), (), s32[]{:S(2)}) async-start(), calls=%async_computation.10 | async-start | bytes 491520 | tf_op jit(solution)/shard_map/reduce_scatter | solution.py:44
  189.4 62.3 %reduce-scatter.15.cloned.1.call-start = ((), (), s32[]{:S(2)}) async-start(), calls=%async_computation.11 | async-start | bytes 491520 | tf_op jit(solution)/shard_map/reduce_scatter | solution.py:44
  221.6 30.1 %copy-start.1 = (f32[192,256]{1,0:T(8,128)S(1)}, f32[192,256]{1,0:T(8,128)}, u32[]{:S(2)}) copy-start(f32[192,256]{1,0:T(8,128)} %get-tuple-element.324) | copy-start | bytes 589828
  233.4 61.5 %reduce-scatter.17.cloned.1.call-start = ((), (), s32[]{:S(2)}) async-start(), calls=%async_computation.12 | async-start | bytes 491520 | tf_op jit(solution)/shard_map/reduce_scatter | solution.py:44
Sparse Core Ops, SparseCore 0:
  56.9 21.0 reduce-scatter.6
  103.0 18.1 reduce-scatter.8
  146.2 18.1 reduce-scatter.10
  189.5 18.1 reduce-scatter.12
  233.5 18.1 reduce-scatter.14
  276.7 18.1 reduce-scatter.16
where the time goes:
time: 305 us; the launch traced here: 303 us
  waiting for transfers between devices  111 us (36%)
  blocking collectives  83.1 us (27%)
  local copies, waits for them, and re-layouts  55.5 us (18%)
  matrix products  24.4 us (8%)
  between operations  14.9 us (5%)
  other arithmetic  8.43 us (3%)
  starting transfers between devices  5.57 us (2%)
    reduce_scatter x6, waiting for transfers between devices, operator(): lax.psum_scatter(partial_value.astype(jnp.bfloat16), 'col', scatter_dimen...  111 us
    all_gather x6, blocking collectives, operator(): lax.all_gather(current, 'row', axis=0, tiled=True)  83.1 us
    gather x24, local copies, waits for them, and re-layouts, group_rows(): gathered[group_columns]  43 us
    dot_general x24, matrix products, group_rows(): jnp.einsum('rak,rkv->rav', group_blocks, picked, preferred_element_type=j...  24.4 us
  transfers between devices with their start and end apart: 7, of which 6 were waited for; matrix products, arithmetic and copies ran while one was open for 0% of the time, Pallas kernels for 0%

commit v1 on v0

v1 whole, which is shorter than its diff:
```python
import functools

import jax
import jax.numpy as jnp
from jax import lax
from jax.experimental import pallas as pl
from jax.experimental.pallas import tpu as pltpu
from jax.sharding import PartitionSpec as P

DEGREE = 6
PAIR = 2


def exchange(value, axis, size, offset):
    return lax.ppermute(value, axis, [(i, i ^ offset) for i in range(size)])


def place_blocks(step, per, width, rows, place, used, same, other, dense):
    near = pl.program_id(0) % PAIR
    piece = place[2] ^ (pl.program_id(0) // PAIR)
    sources = place[4]
    chip = place[0] ^ step
    lane = lax.broadcasted_iota(jnp.int32, (1, PAIR * width), 1) < width
    count = rows // width
    for row in range(count):
        here = pl.ds(row * width, width)
        base = (near * place[3] + piece) * count + row
        sides = []
        for far, ref in enumerate((same, other)):
            value = ref[0, here, :].astype(jnp.float32)
            turned = pltpu.roll(value, width, 1)
            source = PAIR * chip + (place[1] ^ far)
            slots = [used[(base * sources + source) * PAIR + slot] for slot in range(PAIR)]
            sides.append((value, turned, slots))
        halves = [(far, column) for far in range(PAIR) for column in range(per)]
        for tile in range(len(halves) // 2):
            (far_a, col_a), (far_b, col_b) = halves[2 * tile], halves[2 * tile + 1]
            a, b = sides[far_a], sides[far_b]
            keep = jnp.where(lane, (a[2][0] == col_a).astype(jnp.float32), (b[2][1] == col_b).astype(jnp.float32))
            swap = jnp.where(lane, (a[2][1] == col_a).astype(jnp.float32), (b[2][0] == col_b).astype(jnp.float32))
            straight = a[0] if far_a == far_b else jnp.where(lane, a[0], b[0])
            turned = a[1] if far_a == far_b else jnp.where(lane, a[1], b[1])
            dense[here, pl.ds(tile * PAIR * width, PAIR * width)] = (straight * keep + turned * swap).astype(dense.dtype)


def body(per, trial_vectors, h_blocks, block_col, block_count, center, half_width):
    row_count = lax.axis_size("row")
    col_count = lax.axis_size("col")
    chips = row_count // PAIR
    row_index = lax.axis_index("row")
    chip, core = row_index // PAIR, row_index % PAIR
    piece = lax.axis_index("col")
    domain = h_blocks.shape[2]
    width = h_blocks.shape[3]
    slots = h_blocks.shape[5] // width
    vectors = trial_vectors.shape[1] // PAIR

    raw = h_blocks.reshape(row_count, domain * width, slots * width)
    used = jnp.where(
        lax.broadcasted_iota(jnp.int32, block_col.shape[2:], 2) < block_count[0, 0][:, :, None],
        block_col[0, 0],
        -1,
    ).reshape(-1)
    used = jnp.concatenate([used, exchange(used, "row", row_count, 1)])

    first = trial_vectors[:, :vectors]
    second = trial_vectors[:, vectors:]
    mine = jnp.where(core == 0, first, second)
    theirs = exchange(jnp.where(core == 0, second, first), "row", row_count, 1)
    panel = jnp.concatenate([mine, theirs])

    place = jnp.stack([chip, core, piece, jnp.int32(col_count), jnp.int32(row_count)]).astype(jnp.int32)
    rows = domain * width // col_count
    matrices = []
    for step in range(chips):
        sent = lax.dynamic_slice_in_dim(raw, PAIR * (chip ^ step), PAIR, 0)
        same = sent if step == 0 else exchange(sent, "row", row_count, PAIR * step)
        other = exchange(same, "row", row_count, 1)
        same = same.reshape(PAIR * col_count, rows, slots * width)
        other = other.reshape(PAIR * col_count, rows, slots * width)

        def pick(i, place_ref, used_ref):
            return ((place_ref[1] ^ (i % PAIR)) * place_ref[3] + (place_ref[2] ^ (i // PAIR)), 0, 0)

        block = pl.BlockSpec((1, rows, slots * width), pick)
        columns = PAIR * per * width
        matrices.append(
            pl.pallas_call(
                functools.partial(place_blocks, step, per, width, rows),
                out_shape=jax.ShapeDtypeStruct((PAIR * domain * width, columns), jnp.bfloat16),
                grid_spec=pltpu.PrefetchScalarGridSpec(
                    num_scalar_prefetch=2,
                    grid=(PAIR * col_count,),
                    in_specs=[block, block],
                    out_specs=pl.BlockSpec((rows, columns), lambda i, place_ref, used_ref: (i, 0)),
                ),
                cost_estimate=pl.CostEstimate(
                    flops=PAIR * domain * width * columns * 3,
                    bytes_accessed=PAIR * domain * width * columns * 4,
                    transcendentals=0,
                ),
                name=f"place_{step}",
            )(place, used, same, other)
        )

    centre_value = center[0]
    half_value = half_width[0]
    span = PAIR * rows

    def operator(current):
        total = jnp.dot(matrices[0], current, preferred_element_type=jnp.float32)
        arrived = [exchange(current, "row", row_count, PAIR * step) for step in range(1, chips)]
        for step in range(1, chips):
            total = total + jnp.dot(matrices[step], arrived[step - 1], preferred_element_type=jnp.float32)
        owned = total[:span]
        parts = [
            exchange(total[step * span : (step + 1) * span].astype(jnp.bfloat16), "col", col_count, step)
            for step in range(1, col_count)
        ]
        for part in parts:
            owned = owned + part.astype(jnp.float32)
        return owned

    previous = panel.astype(jnp.float32)
    current = (operator(panel) - centre_value * previous) / half_value
    for degree_step in range(DEGREE - 1):
        product = operator(current.astype(jnp.bfloat16))
        following = 2.0 * (product - centre_value * current) / half_value - previous
        previous, current = (current, following)

    mine, theirs = current[:rows], exchange(current[rows:], "row", row_count, 1)
    return jnp.where(
        core == 0, jnp.concatenate([mine, theirs], 1), jnp.concatenate([theirs, mine], 1)
    )


def solution(mesh):
    in_specs = (
        P(("row", "col"), None),
        P("col", None, None, None, "row", None),
        P("col", "row", None, None, None),
        P("col", "row", None, None),
        P(),
        P(),
    )
    out_specs = P(("row", "col"), None)

    def whole(trial_vectors, h_blocks, block_col, block_count, center, half_width):
        shape = h_blocks.shape
        per = trial_vectors.shape[0] // (shape[0] * shape[4] * shape[3])
        return jax.shard_map(
            functools.partial(body, per), mesh=mesh, in_specs=in_specs, out_specs=out_specs, check_vma=False
        )(trial_vectors, h_blocks, block_col, block_count, center, half_width)

    return whole
```

time: 305 us -> 173 us (0.57)
  blocking collectives: 83.1 us -> 0 us
  local copies, waits for them, and re-layouts: 55.5 us -> 5.28 us
  starting transfers between devices: 5.57 us -> 48.5 us
  waiting for transfers between devices: 111 us -> 74.2 us
  Pallas kernels: 0 us -> 23.9 us
  between operations: 14.9 us -> 1.84 us
  matrix products: 24.4 us -> 15.1 us
  other arithmetic: 8.43 us -> 1.95 us
    reduce_scatter x6 -> x0, waiting for transfers between devices: 111 us -> none  [operator(): lax.psum_scatter(partial_value.astype(jnp.bfloat16), 'col', scatter_dimen...]
    all_gather x6 -> x0, blocking collectives: 83.1 us -> none  [operator(): lax.all_gather(current, 'row', axis=0, tiled=True)]
    ppermute x0 -> x46, waiting for transfers between devices: none -> 74.2 us  [exchange(): return lax.ppermute(value, axis, [(i, i ^ offset) for i in range(size)])]
    ppermute x0 -> x46, starting transfers between devices: none -> 48.5 us  [exchange(): return lax.ppermute(value, axis, [(i, i ^ offset) for i in range(size)])]
    gather x24 -> x0, local copies, waits for them, and re-layouts: 43 us -> none  [group_rows(): gathered[group_columns]]
    pallas_call x0 -> x4, Pallas kernels: none -> 23.9 us  [body(): pl.pallas_call(functools.partial(place_blocks, step, per, width, rows), o...]
    dot_general x24, matrix products: 24.4 us -> 15.1 us  [the longest x18 12.3 us: operator(): jnp.dot(matrices[step], arrived[step - 1], preferred_element_type=jnp.flo...]
    another operation x7 -> x1, local copies, waits for them, and re-layouts: 7.22 us -> 0.62 us  [body(): jnp.stack([chip, core, piece, jnp.int32(col_count), jnp.int32(row_count)])]
  transfers between devices with their start and end apart: 7 -> 46, of which waited for: 6 -> 30; matrix products, arithmetic and copies ran while one was open for 0% -> 6% of each run, Pallas kernels for 0% -> 14%
where the time goes in v1:
time: 173 us; the launch traced here: 171 us
  waiting for transfers between devices  74.2 us (43%)
  starting transfers between devices  48.5 us (28%)
  Pallas kernels  23.9 us (14%)
  matrix products  15.1 us (9%)
  local copies, waits for them, and re-layouts  5.28 us (3%)
  other arithmetic  1.95 us (1%)
  between operations  1.84 us (1%)
    ppermute x46, waiting for transfers between devices, exchange(): return lax.ppermute(value, axis, [(i, i ^ offset) for i in range(size)])  74.2 us
    ppermute x46, starting transfers between devices, exchange(): return lax.ppermute(value, axis, [(i, i ^ offset) for i in range(size)])  48.5 us
    pallas_call x4, Pallas kernels, body(): pl.pallas_call(functools.partial(place_blocks, step, per, width, rows), o...  23.9 us
    dot_general x18, matrix products, operator(): jnp.dot(matrices[step], arrived[step - 1], preferred_element_type=jnp.flo...  12.3 us
  transfers between devices with their start and end apart: 46, of which 30 were waited for; matrix products, arithmetic and copies ran while one was open for 6% of the time, Pallas kernels for 14%

profile of v1, /device:TPU:0, one launch (start us, length us, event | category | flops | bytes accessed | tf_op | source)
XLA Modules:
  0.0 170.8 jit_solution(8226508210479353758)
XLA Ops:
  0.0 1.5 constant_dynamic-slice_fusion.3
  1.5 3.0 %collective-permute-start.3 = (bf16[2,768,128]{2,1,0:T(8,128)(2,1)S(1)}, bf16[2,768,128]{2,1,0:T(8,128)(2,1)S(1)}, u32[]{:S(2)}, u32[]{:S(2)}) collective-permute-start(bf16[2,768,128]{2,1,0:T(8,128)(2,1)S(1)} %get-tuple-element.18), channel_id=1, source_target_pairs={{0,8},{4,12},{8,0},{12,4},{16,24},{20,28},{24,16},{28,20},{1,9},{5... | collective-permute-start | bytes 1179656 | tf_op jit(solution)/shard_map/ppermute | solution.py:15
  4.7 1.6 collective-permute-start.9
  7.0 7.5 %collective-permute-done.3 = bf16[2,768,128]{2,1,0:T(8,128)(2,1)S(1)} collective-permute-done((bf16[2,768,128]{2,1,0:T(8,128)(2,1)S(1)}, bf16[2,768,128]{2,1,0:T(8,128)(2,1)S(1)}, u32[]{:S(2)}, u32[]{:S(2)}) %collective-permute-start.3) | collective-permute-done | bytes 393248 | tf_op jit(solution)/shard_map/ppermute | solution.py:15
  15.6 10.2 %collective-permute-done.6 = bf16[2,768,128]{2,1,0:T(8,128)(2,1)S(1)} collective-permute-done((bf16[2,768,128]{2,1,0:T(8,128)(2,1)S(1)}, bf16[2,768,128]{2,1,0:T(8,128)(2,1)S(1)}, u32[]{:S(2)}, u32[]{:S(2)}) %collective-permute-start.6) | collective-permute-done | bytes 393248 | tf_op jit(solution)/shard_map/ppermute | solution.py:15
  25.8 1.6 collective-permute-start.5
  28.8 6.0 %place_0.1 = bf16[1536,384]{1,0:T(8,128)(2,1)} custom-call(s32[5]{0:T(128)} %stack.15.place, s32[384]{0:T(512)} %pad_add_fusion.used, bf16[8,192,128]{2,1,0:T(8,128)(2,1)} %bitcast.77, bf16[8,192,128]{2,1,0:T(8,128)(2,1)} %bitcast.82), custom_call_target="tpu_custom_call" | custom-call | flops 1769472 | bytes 2359296 | tf_op jit(solution)/shard_map/place_0/pallas_call | solution.py:88
  34.8 1.3 collective-permute-start.11
  36.8 6.0 %place_1.1 = bf16[1536,384]{1,0:T(8,128)(2,1)} custom-call(s32[5]{0:T(128)} %stack.15.place, s32[384]{0:T(512)} %pad_add_fusion.used, bf16[8,192,128]{2,1,0:T(8,128)(2,1)} %bitcast.78, bf16[8,192,128]{2,1,0:T(8,128)(2,1)} %bitcast.81), custom_call_target="tpu_custom_call" | custom-call | flops 1769472 | bytes 2359296 | tf_op jit(solution)/shard_map/place_1/pallas_call | solution.py:88
  42.8 1.7 %fusion.67 = f32[1536,128]{1,0:T(8,128)S(1)} fusion(bf16[1536,384]{1,0:T(8,128)(2,1)} %place_1.1, bf16[384,128]{1,0:T(8,128)(2,1)S(1)} %collective-permute-done.5), kind=kOutput, calls=%fused_computation.88 | convolution fusion | flops 150994944 | bytes 2064384 | tf_op jit(solution)/shard_map/dot_general | solution.py:114
  45.3 6.0 %place_2.1 = bf16[1536,384]{1,0:T(8,128)(2,1)} custom-call(s32[5]{0:T(128)} %stack.15.place, s32[384]{0:T(512)} %pad_add_fusion.used, bf16[8,192,128]{2,1,0:T(8,128)(2,1)} %bitcast.80, bf16[8,192,128]{2,1,0:T(8,128)(2,1)} %bitcast.83), custom_call_target="tpu_custom_call" | custom-call | flops 1769472 | bytes 2359296 | tf_op jit(solution)/shard_map/place_2/pallas_call | solution.py:88
  51.3 1.7 %fusion.68 = f32[1536,128]{1,0:T(8,128)S(1)} fusion(bf16[1536,384]{1,0:T(8,128)(2,1)} %place_2.1, bf16[384,128]{1,0:T(8,128)(2,1)S(1)} %collective-permute-done.8), kind=kOutput, calls=%fused_computation.89 | convolution fusion | flops 150994944 | bytes 2064384 | tf_op jit(solution)/shard_map/dot_general | solution.py:114
  53.8 6.0 %place_3.1 = bf16[1536,384]{1,0:T(8,128)(2,1)} custom-call(s32[5]{0:T(128)} %stack.15.place, s32[384]{0:T(512)} %pad_add_fusion.used, bf16[8,192,128]{2,1,0:T(8,128)(2,1)} %bitcast.79, bf16[8,192,128]{2,1,0:T(8,128)(2,1)} %bitcast.84), custom_call_target="tpu_custom_call" | custom-call | flops 1769472 | bytes 2359296 | tf_op jit(solution)/shard_map/place_3/pallas_call | solution.py:88
  59.8 1.8 %fusion.69 = f32[1536,128]{1,0:T(8,128)S(1)} fusion(bf16[1536,384]{1,0:T(8,128)(2,1)} %place_3.1, bf16[384,128]{1,0:T(8,128)(2,1)S(1)} %collective-permute-done.11), kind=kOutput, calls=%fused_computation.90 | convolution fusion | flops 150994944 | bytes 2064384 | tf_op jit(solution)/shard_map/dot_general | solution.py:114
  62.2 1.6 collective-permute-start.12
  63.8 2.5 %collective-permute-start.14 = (bf16[384,128]{1,0:T(8,128)(2,1)S(1)}, bf16[384,128]{1,0:T(8,128)(2,1)S(1)}, u32[]{:S(2)}, u32[]{:S(2)}) collective-permute-start(bf16[384,128]{1,0:T(8,128)(2,1)S(1)} %get-tuple-element.35), channel_id=1, source_target_pairs={{0,3},{1,2},{2,1},{3,0},{4,7},{5,6},{6,5},{7,4},{8,11},{9,10},{10,... | collective-permute-start | bytes 294920 | tf_op jit(solution)/shard_map/ppermute | solution.py:15
  67.7 4.2 %collective-permute-done.14 = bf16[384,128]{1,0:T(8,128)(2,1)S(1)} collective-permute-done((bf16[384,128]{1,0:T(8,128)(2,1)S(1)}, bf16[384,128]{1,0:T(8,128)(2,1)S(1)}, u32[]{:S(2)}, u32[]{:S(2)}) %collective-permute-start.14) | collective-permute-done | bytes 98336 | tf_op jit(solution)/shard_map/ppermute | solution.py:15
  71.9 3.3 %collective-permute-done.13 = bf16[384,128]{1,0:T(8,128)(2,1)S(1)} collective-permute-done((bf16[384,128]{1,0:T(8,128)(2,1)S(1)}, bf16[384,128]{1,0:T(8,128)(2,1)S(1)}, u32[]{:S(2)}, u32[]{:S(2)}) %collective-permute-start.13) | collective-permute-done | bytes 98336 | tf_op jit(solution)/shard_map/ppermute | solution.py:15
  75.3 1.6 collective-permute-start.15
  77.7 1.1 collective-permute-start.16
  78.8 2.0 %collective-permute-done.15 = bf16[384,128]{1,0:T(8,128)(2,1)S(1)} collective-permute-done((bf16[384,128]{1,0:T(8,128)(2,1)S(1)}, bf16[384,128]{1,0:T(8,128)(2,1)S(1)}, u32[]{:S(2)}, u32[]{:S(2)}) %collective-permute-start.15) | collective-permute-done | bytes 98336 | tf_op jit(solution)/shard_map/ppermute | solution.py:15
  81.3 2.3 %collective-permute-done.16 = bf16[384,128]{1,0:T(8,128)(2,1)S(1)} collective-permute-done((bf16[384,128]{1,0:T(8,128)(2,1)S(1)}, bf16[384,128]{1,0:T(8,128)(2,1)S(1)}, u32[]{:S(2)}, u32[]{:S(2)}) %collective-permute-start.16) | collective-permute-done | bytes 98336 | tf_op jit(solution)/shard_map/ppermute | solution.py:15
  85.1 2.5 %collective-permute-start.20 = (bf16[384,128]{1,0:T(8,128)(2,1)S(1)}, bf16[384,128]{1,0:T(8,128)(2,1)S(1)}, u32[]{:S(2)}, u32[]{:S(2)}) collective-permute-start(bf16[384,128]{1,0:T(8,128)(2,1)S(1)} %get-tuple-element.32), channel_id=1, source_target_pairs={{0,3},{1,2},{2,1},{3,0},{4,7},{5,6},{6,5},{7,4},{8,11},{9,10},{10,... | collective-permute-start | bytes 294920 | tf_op jit(solution)/shard_map/ppermute | solution.py:15
  87.6 0.9 collective-permute-start.19
  88.6 1.7 collective-permute-done.18
  90.3 1.6 collective-permute-done.20
  91.9 2.9 %collective-permute-done.19 = bf16[384,128]{1,0:T(8,128)(2,1)S(1)} collective-permute-done((bf16[384,128]{1,0:T(8,128)(2,1)S(1)}, bf16[384,128]{1,0:T(8,128)(2,1)S(1)}, u32[]{:S(2)}, u32[]{:S(2)}) %collective-permute-start.19) | collective-permute-done | bytes 98336 | tf_op jit(solution)/shard_map/ppermute | solution.py:15
  94.9 1.7 %collective-permute-start.21 = (bf16[384,128]{1,0:T(8,128)(2,1)S(1)}, bf16[384,128]{1,0:T(8,128)(2,1)S(1)}, u32[]{:S(2)}, u32[]{:S(2)}) collective-permute-start(bf16[384,128]{1,0:T(8,128)(2,1)S(1)} %get-tuple-element.11), channel_id=1, source_target_pairs={{0,8},{4,12},{8,0},{12,4},{16,24},{20,28},{24,16},{28,20},{1,9},{5... | collective-permute-start | bytes 294920 | tf_op jit(solution)/shard_map/ppermute | solution.py:15
  96.6 1.1 collective-permute-start.23
  98.4 1.5 collective-permute-done.21
  100.4 2.8 %collective-permute-done.22 = bf16[384,128]{1,0:T(8,128)(2,1)S(1)} collective-permute-done((bf16[384,128]{1,0:T(8,128)(2,1)S(1)}, bf16[384,128]{1,0:T(8,128)(2,1)S(1)}, u32[]{:S(2)}, u32[]{:S(2)}) %collective-permute-start.22) | collective-permute-done | bytes 98336 | tf_op jit(solution)/shard_map/ppermute | solution.py:15
  104.7 2.0 %collective-permute-start.26 = (bf16[384,128]{1,0:T(8,128)(2,1)S(1)}, bf16[384,128]{1,0:T(8,128)(2,1)S(1)}, u32[]{:S(2)}, u32[]{:S(2)}) collective-permute-start(bf16[384,128]{1,0:T(8,128)(2,1)S(1)} %get-tuple-element.29), channel_id=1, source_target_pairs={{0,3},{1,2},{2,1},{3,0},{4,7},{5,6},{6,5},{7,4},{8,11},{9,10},{10,... | collective-permute-start | bytes 294920 | tf_op jit(solution)/shard_map/ppermute | solution.py:15
  106.7 1.5 collective-permute-start.25
  108.2 3.2 %collective-permute-done.24 = bf16[384,128]{1,0:T(8,128)(2,1)S(1)} collective-permute-done((bf16[384,128]{1,0:T(8,128)(2,1)S(1)}, bf16[384,128]{1,0:T(8,128)(2,1)S(1)}, u32[]{:S(2)}, u32[]{:S(2)}) %collective-permute-start.24) | collective-permute-done | bytes 98336 | tf_op jit(solution)/shard_map/ppermute | solution.py:15
  111.5 2.5 %collective-permute-done.25 = bf16[384,128]{1,0:T(8,128)(2,1)S(1)} collective-permute-done((bf16[384,128]{1,0:T(8,128)(2,1)S(1)}, bf16[384,128]{1,0:T(8,128)(2,1)S(1)}, u32[]{:S(2)}, u32[]{:S(2)}) %collective-permute-start.25) | collective-permute-done | bytes 98336 | tf_op jit(solution)/shard_map/ppermute | solution.py:15
  114.1 1.2 collective-permute-start.27
  115.2 1.3 collective-permute-start.29
  116.5 1.1 collective-permute-start.28
  117.6 1.1 collective-permute-done.27
  119.2 2.6 %collective-permute-done.28 = bf16[384,128]{1,0:T(8,128)(2,1)S(1)} collective-permute-done((bf16[384,128]{1,0:T(8,128)(2,1)S(1)}, bf16[384,128]{1,0:T(8,128)(2,1)S(1)}, u32[]{:S(2)}, u32[]{:S(2)}) %collective-permute-start.28) | collective-permute-done | bytes 98336 | tf_op jit(solution)/shard_map/ppermute | solution.py:15
  123.3 1.8 %collective-permute-start.32 = (bf16[384,128]{1,0:T(8,128)(2,1)S(1)}, bf16[384,128]{1,0:T(8,128)(2,1)S(1)}, u32[]{:S(2)}, u32[]{:S(2)}) collective-permute-start(bf16[384,128]{1,0:T(8,128)(2,1)S(1)} %get-tuple-element.26), channel_id=1, source_target_pairs={{0,3},{1,2},{2,1},{3,0},{4,7},{5,6},{6,5},{7,4},{8,11},{9,10},{10,... | collective-permute-start | bytes 294920 | tf_op jit(solution)/shard_map/ppermute | solution.py:15
  125.2 1.6 collective-permute-start.31
  126.8 1.1 collective-permute-done.30
  128.0 2.0 %collective-permute-done.32 = bf16[384,128]{1,0:T(8,128)(2,1)S(1)} collective-permute-done((bf16[384,128]{1,0:T(8,128)(2,1)S(1)}, bf16[384,128]{1,0:T(8,128)(2,1)S(1)}, u32[]{:S(2)}, u32[]{:S(2)}) %collective-permute-start.32) | collective-permute-done | bytes 98336 | tf_op jit(solution)/shard_map/ppermute | solution.py:15
  129.9 2.6 %collective-permute-done.31 = bf16[384,128]{1,0:T(8,128)(2,1)S(1)} collective-permute-done((bf16[384,128]{1,0:T(8,128)(2,1)S(1)}, bf16[384,128]{1,0:T(8,128)(2,1)S(1)}, u32[]{:S(2)}, u32[]{:S(2)}) %collective-permute-start.31) | collective-permute-done | bytes 98336 | tf_op jit(solution)/shard_map/ppermute | solution.py:15
  132.7 1.0 collective-permute-start.33
  133.6 1.5 collective-permute-start.35
  135.2 1.0 collective-permute-start.34
  136.2 1.1 collective-permute-done.33
  137.8 2.4 %collective-permute-done.34 = bf16[384,128]{1,0:T(8,128)(2,1)S(1)} collective-permute-done((bf16[384,128]{1,0:T(8,128)(2,1)S(1)}, bf16[384,128]{1,0:T(8,128)(2,1)S(1)}, u32[]{:S(2)}, u32[]{:S(2)}) %collective-permute-start.34) | collective-permute-done | bytes 98336 | tf_op jit(solution)/shard_map/ppermute | solution.py:15
  141.8 2.0 %collective-permute-start.38 = (bf16[384,128]{1,0:T(8,128)(2,1)S(1)}, bf16[384,128]{1,0:T(8,128)(2,1)S(1)}, u32[]{:S(2)}, u32[]{:S(2)}) collective-permute-start(bf16[384,128]{1,0:T(8,128)(2,1)S(1)} %get-tuple-element.23), channel_id=1, source_target_pairs={{0,3},{1,2},{2,1},{3,0},{4,7},{5,6},{6,5},{7,4},{8,11},{9,10},{10,... | collective-permute-start | bytes 294920 | tf_op jit(solution)/shard_map/ppermute | solution.py:15
  143.8 1.5 collective-permute-start.37
  145.2 1.1 collective-permute-done.36
  146.4 2.0 %collective-permute-done.38 = bf16[384,128]{1,0:T(8,128)(2,1)S(1)} collective-permute-done((bf16[384,128]{1,0:T(8,128)(2,1)S(1)}, bf16[384,128]{1,0:T(8,128)(2,1)S(1)}, u32[]{:S(2)}, u32[]{:S(2)}) %collective-permute-start.38) | collective-permute-done | bytes 98336 | tf_op jit(solution)/shard_map/ppermute | solution.py:15
  148.3 2.6 %collective-permute-done.37 = bf16[384,128]{1,0:T(8,128)(2,1)S(1)} collective-permute-done((bf16[384,128]{1,0:T(8,128)(2,1)S(1)}, bf16[384,128]{1,0:T(8,128)(2,1)S(1)}, u32[]{:S(2)}, u32[]{:S(2)}) %collective-permute-start.37) | collective-permute-done | bytes 98336 | tf_op jit(solution)/shard_map/ppermute | solution.py:15
  151.1 1.6 collective-permute-start.41
  152.7 1.0 collective-permute-start.40
  154.6 2.1 %collective-permute-done.41 = bf16[384,128]{1,0:T(8,128)(2,1)S(1)} collective-permute-done((bf16[384,128]{1,0:T(8,128)(2,1)S(1)}, bf16[384,128]{1,0:T(8,128)(2,1)S(1)}, u32[]{:S(2)}, u32[]{:S(2)}) %collective-permute-start.41) | collective-permute-done | bytes 98336 | tf_op jit(solution)/shard_map/ppermute | solution.py:15
  159.4 1.9 %collective-permute-start.44 = (bf16[384,128]{1,0:T(8,128)(2,1)S(1)}, bf16[384,128]{1,0:T(8,128)(2,1)S(1)}, u32[]{:S(2)}, u32[]{:S(2)}) collective-permute-start(bf16[384,128]{1,0:T(8,128)(2,1)S(1)} %get-tuple-element.20), channel_id=1, source_target_pairs={{0,3},{1,2},{2,1},{3,0},{4,7},{5,6},{6,5},{7,4},{8,11},{9,10},{10,... | collective-permute-start | bytes 294920 | tf_op jit(solution)/shard_map/ppermute | solution.py:15
  161.3 1.6 collective-permute-start.43
  162.9 1.1 collective-permute-done.42
  164.0 2.0 %collective-permute-done.44 = bf16[384,128]{1,0:T(8,128)(2,1)S(1)} collective-permute-done((bf16[384,128]{1,0:T(8,128)(2,1)S(1)}, bf16[384,128]{1,0:T(8,128)(2,1)S(1)}, u32[]{:S(2)}, u32[]{:S(2)}) %collective-permute-start.44) | collective-permute-done | bytes 98336 | tf_op jit(solution)/shard_map/ppermute | solution.py:15
  166.0 2.6 %collective-permute-done.43 = bf16[384,128]{1,0:T(8,128)(2,1)S(1)} collective-permute-done((bf16[384,128]{1,0:T(8,128)(2,1)S(1)}, bf16[384,128]{1,0:T(8,128)(2,1)S(1)}, u32[]{:S(2)}, u32[]{:S(2)}) %collective-permute-start.43) | collective-permute-done | bytes 98336 | tf_op jit(solution)/shard_map/ppermute | solution.py:15
  168.8 1.3 collective-permute-done.45
  (111 shorter events, 20.6 us)
Async XLA Ops:
  0.0 4.6 %copy-start.12 = (bf16[192,256]{1,0:T(8,128)(2,1)S(1)}, bf16[192,256]{1,0:T(8,128)(2,1)}, u32[]{:S(2)}) copy-start(bf16[192,256]{1,0:T(8,128)(2,1)} %param.6) | copy-start | bytes 294916
  0.0 6.4 %copy-start.14 = (s32[1,1,12,8]{2,3,1,0:T(8,128)S(1)}, s32[1,1,12,8]{2,3,1,0:T(8,128)}, u32[]{:S(2)}) copy-start(s32[1,1,12,8]{2,3,1,0:T(8,128)} %param.9) | copy-start | bytes 1156
  0.0 6.7 %copy-start.13 = (s32[1,1,12,8,2]{2,4,3,1,0:T(2,128)S(1)}, s32[1,1,12,8,2]{2,4,3,1,0:T(2,128)}, u32[]{:S(2)}) copy-start(s32[1,1,12,8,2]{2,4,3,1,0:T(2,128)} %param.8) | copy-start | bytes 2308
  1.5 27.1 %copy-start.4 = (bf16[2,768,128]{2,1,0:T(8,128)(2,1)}, bf16[2,768,128]{2,1,0:T(8,128)(2,1)S(1)}, u32[]{:S(2)}) copy-start(bf16[2,768,128]{2,1,0:T(8,128)(2,1)S(1)} %get-tuple-element.15) | copy-start | bytes 1179652
  1.5 13.0 %collective-permute-start.3 = (bf16[2,768,128]{2,1,0:T(8,128)(2,1)S(1)}, bf16[2,768,128]{2,1,0:T(8,128)(2,1)S(1)}, u32[]{:S(2)}, u32[]{:S(2)}) collective-permute-start(bf16[2,768,128]{2,1,0:T(8,128)(2,1)S(1)} %get-tuple-element.18), channel_id=1, source_target_pairs={{0,8},{4,12},{8,0},{12,4},{16,24},{20,28},{24,16},{28,20},{1,9},{5... | collective-permute-start | bytes 1179656 | tf_op jit(solution)/shard_map/ppermute | solution.py:15
  4.6 10.6 %collective-permute-start.2 = (bf16[192,128]{1,0:T(8,128)(2,1)S(1)}, bf16[192,128]{1,0:T(8,128)(2,1)S(1)}, u32[]{:S(2)}, u32[]{:S(2)}) collective-permute-start(bf16[192,128]{1,0:T(8,128)(2,1)S(1)} %get-tuple-element.40), channel_id=1, source_target_pairs={{0,4},{4,0},{8,12},{12,8},{16,20},{20,16},{24,28},{28,24},{1,5},{5... | collective-permute-start | bytes 147464 | tf_op jit(solution)/shard_map/ppermute | solution.py:15
  4.7 30.1 %collective-permute-start.9 = (bf16[2,768,128]{2,1,0:T(8,128)(2,1)S(1)}, bf16[2,768,128]{2,1,0:T(8,128)(2,1)S(1)}, u32[]{:S(2)}, u32[]{:S(2)}) collective-permute-start(bf16[2,768,128]{2,1,0:T(8,128)(2,1)S(1)} %get-tuple-element.16), channel_id=1, source_target_pairs={{0,24},{4,28},{8,16},{12,20},{16,8},{20,12},{24,0},{28,4},{1,25},{... | collective-permute-start | bytes 1179656 | tf_op jit(solution)/shard_map/ppermute | solution.py:15
  6.2 19.6 %collective-permute-start.6 = (bf16[2,768,128]{2,1,0:T(8,128)(2,1)S(1)}, bf16[2,768,128]{2,1,0:T(8,128)(2,1)S(1)}, u32[]{:S(2)}, u32[]{:S(2)}) collective-permute-start(bf16[2,768,128]{2,1,0:T(8,128)(2,1)S(1)} %get-tuple-element.17), channel_id=1, source_target_pairs={{0,16},{4,20},{8,24},{12,28},{16,0},{20,4},{24,8},{28,12},{1,17},{... | collective-permute-start | bytes 1179656 | tf_op jit(solution)/shard_map/ppermute | solution.py:15
  6.3 21.7 %collective-permute-start.1 = (bf16[2,768,128]{2,1,0:T(8,128)(2,1)S(1)}, bf16[2,768,128]{2,1,0:T(8,128)(2,1)S(1)}, u32[]{:S(2)}, u32[]{:S(2)}) collective-permute-start(bf16[2,768,128]{2,1,0:T(8,128)(2,1)S(1)} %get-tuple-element.15), channel_id=1, source_target_pairs={{0,4},{4,0},{8,12},{12,8},{16,20},{20,16},{24,28},{28,24},{1,5},{5... | collective-permute-start | bytes 1179656 | tf_op jit(solution)/shard_map/ppermute | solution.py:15
  14.5 21.6 %copy-start.5 = (bf16[2,768,128]{2,1,0:T(8,128)(2,1)}, bf16[2,768,128]{2,1,0:T(8,128)(2,1)S(1)}, u32[]{:S(2)}) copy-start(bf16[2,768,128]{2,1,0:T(8,128)(2,1)S(1)} %collective-permute-done.3) | copy-start | bytes 1179652
  14.5 21.6 %collective-permute-start.4 = (bf16[2,768,128]{2,1,0:T(8,128)(2,1)S(1)}, bf16[2,768,128]{2,1,0:T(8,128)(2,1)S(1)}, u32[]{:S(2)}, u32[]{:S(2)}) collective-permute-start(bf16[2,768,128]{2,1,0:T(8,128)(2,1)S(1)} %collective-permute-done.3), channel_id=1, source_target_pairs={{0,4},{4,0},{8,12},{12,8},{16,20},{20,16},{24,28},{28,24},{1,5},{5... | collective-permute-start | bytes 1179656 | tf_op jit(solution)/shard_map/ppermute | solution.py:15
  15.2 10.7 %collective-permute-start = (s32[192]{0:T(256)S(1)}, s32[192]{0:T(256)S(1)}, u32[]{:S(2)}, u32[]{:S(2)}) collective-permute-start(s32[192]{0:T(256)S(1)} %broadcast_select_fusion.2), channel_id=1, source_target_pairs={{0,4},{4,0},{8,12},{12,8},{16,20},{20,16},{24,28},{28,24},{1,5},{5... | collective-permute-start | bytes 2312 | tf_op jit(solution)/shard_map/ppermute | solution.py:15
  25.8 17.0 %copy-start.7 = (bf16[2,768,128]{2,1,0:T(8,128)(2,1)}, bf16[2,768,128]{2,1,0:T(8,128)(2,1)S(1)}, u32[]{:S(2)}) copy-start(bf16[2,768,128]{2,1,0:T(8,128)(2,1)S(1)} %collective-permute-done.6) | copy-start | bytes 1179652
  25.8 18.7 %collective-permute-start.7 = (bf16[2,768,128]{2,1,0:T(8,128)(2,1)S(1)}, bf16[2,768,128]{2,1,0:T(8,128)(2,1)S(1)}, u32[]{:S(2)}, u32[]{:S(2)}) collective-permute-start(bf16[2,768,128]{2,1,0:T(8,128)(2,1)S(1)} %collective-permute-done.6), channel_id=1, source_target_pairs={{0,4},{4,0},{8,12},{12,8},{16,20},{20,16},{24,28},{28,24},{1,5},{5... | collective-permute-start | bytes 1179656 | tf_op jit(solution)/shard_map/ppermute | solution.py:15
  25.8 17.0 %collective-permute-start.5 = (bf16[384,128]{1,0:T(8,128)(2,1)S(1)}, bf16[384,128]{1,0:T(8,128)(2,1)S(1)}, u32[]{:S(2)}, u32[]{:S(2)}) collective-permute-start(bf16[384,128]{1,0:T(8,128)(2,1)S(1)} %pad_maximum_fusion), channel_id=1, source_target_pairs={{0,8},{4,12},{8,0},{12,4},{16,24},{20,28},{24,16},{28,20},{1,9},{5... | collective-permute-start | bytes 294920 | tf_op jit(solution)/shard_map/ppermute | solution.py:15
  28.1 0.8 copy-start.9
  28.1 23.2 %collective-permute-start.8 = (bf16[384,128]{1,0:T(8,128)(2,1)S(1)}, bf16[384,128]{1,0:T(8,128)(2,1)S(1)}, u32[]{:S(2)}, u32[]{:S(2)}) collective-permute-start(bf16[384,128]{1,0:T(8,128)(2,1)S(1)} %pad_maximum_fusion), channel_id=1, source_target_pairs={{0,16},{4,20},{8,24},{12,28},{16,0},{20,4},{24,8},{28,12},{1,17},{... | collective-permute-start | bytes 294920 | tf_op jit(solution)/shard_map/ppermute | solution.py:15
  34.8 9.8 %copy-start.6 = (bf16[2,768,128]{2,1,0:T(8,128)(2,1)}, bf16[2,768,128]{2,1,0:T(8,128)(2,1)S(1)}, u32[]{:S(2)}) copy-start(bf16[2,768,128]{2,1,0:T(8,128)(2,1)S(1)} %collective-permute-done.9) | copy-start | bytes 1179652
  34.8 25.0 %collective-permute-start.11 = (bf16[384,128]{1,0:T(8,128)(2,1)S(1)}, bf16[384,128]{1,0:T(8,128)(2,1)S(1)}, u32[]{:S(2)}, u32[]{:S(2)}) collective-permute-start(bf16[384,128]{1,0:T(8,128)(2,1)S(1)} %pad_maximum_fusion), channel_id=1, source_target_pairs={{0,24},{4,28},{8,16},{12,20},{16,8},{20,12},{24,0},{28,4},{1,25},{... | collective-permute-start | bytes 294920 | tf_op jit(solution)/shard_map/ppermute | solution.py:15
  36.1 0.7 copy-start.8
  36.1 17.0 %collective-permute-start.10 = (bf16[2,768,128]{2,1,0:T(8,128)(2,1)S(1)}, bf16[2,768,128]{2,1,0:T(8,128)(2,1)S(1)}, u32[]{:S(2)}, u32[]{:S(2)}) collective-permute-start(bf16[2,768,128]{2,1,0:T(8,128)(2,1)S(1)} %collective-permute-done.9), channel_id=1, source_target_pairs={{0,4},{4,0},{8,12},{12,8},{16,20},{20,16},{24,28},{28,24},{1,5},{5... | collective-permute-start | bytes 1179656 | tf_op jit(solution)/shard_map/ppermute | solution.py:15
  44.6 0.8 copy-start.10
  53.1 0.7 copy-start.11
  59.8 1.8 %copy-start = (bf16[1536,384]{1,0:T(8,128)(2,1)S(1)}, bf16[1536,384]{1,0:T(8,128)(2,1)}, u32[]{:S(2)}) copy-start(bf16[1536,384]{1,0:T(8,128)(2,1)} %place_0.1) | copy-start | bytes 3538948
  62.1 18.7 %copy-start.1 = (bf16[1536,384]{1,0:T(8,128)(2,1)S(1)}, bf16[1536,384]{1,0:T(8,128)(2,1)}, u32[]{:S(2)}) copy-start(bf16[1536,384]{1,0:T(8,128)(2,1)} %place_1.1) | copy-start | bytes 3538948
  62.2 5.5 %collective-permute-start.12 = (bf16[384,128]{1,0:T(8,128)(2,1)S(1)}, bf16[384,128]{1,0:T(8,128)(2,1)S(1)}, u32[]{:S(2)}, u32[]{:S(2)}) collective-permute-start(bf16[384,128]{1,0:T(8,128)(2,1)S(1)} %get-tuple-element.34), channel_id=1, source_target_pairs={{0,1},{1,0},{2,3},{3,2},{4,5},{5,4},{6,7},{7,6},{8,9},{9,8},{10,11... | collective-permute-start | bytes 294920 | tf_op jit(solution)/shard_map/ppermute | solution.py:15
  63.8 8.1 %collective-permute-start.14 = (bf16[384,128]{1,0:T(8,128)(2,1)S(1)}, bf16[384,128]{1,0:T(8,128)(2,1)S(1)}, u32[]{:S(2)}, u32[]{:S(2)}) collective-permute-start(bf16[384,128]{1,0:T(8,128)(2,1)S(1)} %get-tuple-element.35), channel_id=1, source_target_pairs={{0,3},{1,2},{2,1},{3,0},{4,7},{5,6},{6,5},{7,4},{8,11},{9,10},{10,... | collective-permute-start | bytes 294920 | tf_op jit(solution)/shard_map/ppermute | solution.py:15
  66.3 8.9 %collective-permute-start.13 = (bf16[384,128]{1,0:T(8,128)(2,1)S(1)}, bf16[384,128]{1,0:T(8,128)(2,1)S(1)}, u32[]{:S(2)}, u32[]{:S(2)}) collective-permute-start(bf16[384,128]{1,0:T(8,128)(2,1)S(1)} %get-tuple-element.36), channel_id=1, source_target_pairs={{0,2},{1,3},{2,0},{3,1},{4,6},{5,7},{6,4},{7,5},{8,10},{9,11},{10,... | collective-permute-start | bytes 294920 | tf_op jit(solution)/shard_map/ppermute | solution.py:15
  75.2 8.3 %copy-start.2 = (bf16[1536,384]{1,0:T(8,128)(2,1)S(1)}, bf16[1536,384]{1,0:T(8,128)(2,1)}, u32[]{:S(2)}) copy-start(bf16[1536,384]{1,0:T(8,128)(2,1)} %place_2.1) | copy-start | bytes 3538948
  75.3 5.5 %collective-permute-start.15 = (bf16[384,128]{1,0:T(8,128)(2,1)S(1)}, bf16[384,128]{1,0:T(8,128)(2,1)S(1)}, u32[]{:S(2)}, u32[]{:S(2)}) collective-permute-start(bf16[384,128]{1,0:T(8,128)(2,1)S(1)} %get-tuple-element.13), channel_id=1, source_target_pairs={{0,8},{4,12},{8,0},{12,4},{16,24},{20,28},{24,16},{28,20},{1,9},{5... | collective-permute-start | bytes 294920 | tf_op jit(solution)/shard_map/ppermute | solution.py:15
  76.8 7.2 %collective-permute-start.17 = (bf16[384,128]{1,0:T(8,128)(2,1)S(1)}, bf16[384,128]{1,0:T(8,128)(2,1)S(1)}, u32[]{:S(2)}, u32[]{:S(2)}) collective-permute-start(bf16[384,128]{1,0:T(8,128)(2,1)S(1)} %get-tuple-element.13), channel_id=1, source_target_pairs={{0,24},{4,28},{8,16},{12,20},{16,8},{20,12},{24,0},{28,4},{1,25},{... | collective-permute-start | bytes 294920 | tf_op jit(solution)/shard_map/ppermute | solution.py:15
  77.7 5.9 %collective-permute-start.16 = (bf16[384,128]{1,0:T(8,128)(2,1)S(1)}, bf16[384,128]{1,0:T(8,128)(2,1)S(1)}, u32[]{:S(2)}, u32[]{:S(2)}) collective-permute-start(bf16[384,128]{1,0:T(8,128)(2,1)S(1)} %get-tuple-element.13), channel_id=1, source_target_pairs={{0,16},{4,20},{8,24},{12,28},{16,0},{20,4},{24,8},{28,12},{1,17},{... | collective-permute-start | bytes 294920 | tf_op jit(solution)/shard_map/ppermute | solution.py:15
  81.2 2.8 %copy-start.3 = (bf16[1536,384]{1,0:T(8,128)(2,1)S(1)}, bf16[1536,384]{1,0:T(8,128)(2,1)}, u32[]{:S(2)}) copy-start(bf16[1536,384]{1,0:T(8,128)(2,1)} %place_3.1) | copy-start | bytes 3538948
  85.0 5.2 %collective-permute-start.18 = (bf16[384,128]{1,0:T(8,128)(2,1)S(1)}, bf16[384,128]{1,0:T(8,128)(2,1)S(1)}, u32[]{:S(2)}, u32[]{:S(2)}) collective-permute-start(bf16[384,128]{1,0:T(8,128)(2,1)S(1)} %get-tuple-element.31), channel_id=1, source_target_pairs={{0,1},{1,0},{2,3},{3,2},{4,5},{5,4},{6,7},{7,6},{8,9},{9,8},{10,11... | collective-permute-start | bytes 294920 | tf_op jit(solution)/shard_map/ppermute | solution.py:15
  85.1 6.8 %collective-permute-start.20 = (bf16[384,128]{1,0:T(8,128)(2,1)S(1)}, bf16[384,128]{1,0:T(8,128)(2,1)S(1)}, u32[]{:S(2)}, u32[]{:S(2)}) collective-permute-start(bf16[384,128]{1,0:T(8,128)(2,1)S(1)} %get-tuple-element.32), channel_id=1, source_target_pairs={{0,3},{1,2},{2,1},{3,0},{4,7},{5,6},{6,5},{7,4},{8,11},{9,10},{10,... | collective-permute-start | bytes 294920 | tf_op jit(solution)/shard_map/ppermute | solution.py:15
  87.6 7.2 %collective-permute-start.19 = (bf16[384,128]{1,0:T(8,128)(2,1)S(1)}, bf16[384,128]{1,0:T(8,128)(2,1)S(1)}, u32[]{:S(2)}, u32[]{:S(2)}) collective-permute-start(bf16[384,128]{1,0:T(8,128)(2,1)S(1)} %get-tuple-element.33), channel_id=1, source_target_pairs={{0,2},{1,3},{2,0},{3,1},{4,6},{5,7},{6,4},{7,5},{8,10},{9,11},{10,... | collective-permute-start | bytes 294920 | tf_op jit(solution)/shard_map/ppermute | solution.py:15
  94.9 5.1 %collective-permute-start.21 = (bf16[384,128]{1,0:T(8,128)(2,1)S(1)}, bf16[384,128]{1,0:T(8,128)(2,1)S(1)}, u32[]{:S(2)}, u32[]{:S(2)}) collective-permute-start(bf16[384,128]{1,0:T(8,128)(2,1)S(1)} %get-tuple-element.11), channel_id=1, source_target_pairs={{0,8},{4,12},{8,0},{12,4},{16,24},{20,28},{24,16},{28,20},{1,9},{5... | collective-permute-start | bytes 294920 | tf_op jit(solution)/shard_map/ppermute | solution.py:15
  96.6 7.0 %collective-permute-start.23 = (bf16[384,128]{1,0:T(8,128)(2,1)S(1)}, bf16[384,128]{1,0:T(8,128)(2,1)S(1)}, u32[]{:S(2)}, u32[]{:S(2)}) collective-permute-start(bf16[384,128]{1,0:T(8,128)(2,1)S(1)} %get-tuple-element.11), channel_id=1, source_target_pairs={{0,24},{4,28},{8,16},{12,20},{16,8},{20,12},{24,0},{28,4},{1,25},{... | collective-permute-start | bytes 294920 | tf_op jit(solution)/shard_map/ppermute | solution.py:15
  97.8 5.4 %collective-permute-start.22 = (bf16[384,128]{1,0:T(8,128)(2,1)S(1)}, bf16[384,128]{1,0:T(8,128)(2,1)S(1)}, u32[]{:S(2)}, u32[]{:S(2)}) collective-permute-start(bf16[384,128]{1,0:T(8,128)(2,1)S(1)} %get-tuple-element.11), channel_id=1, source_target_pairs={{0,16},{4,20},{8,24},{12,28},{16,0},{20,4},{24,8},{28,12},{1,17},{... | collective-permute-start | bytes 294920 | tf_op jit(solution)/shard_map/ppermute | solution.py:15
  104.7 6.8 %collective-permute-start.24 = (bf16[384,128]{1,0:T(8,128)(2,1)S(1)}, bf16[384,128]{1,0:T(8,128)(2,1)S(1)}, u32[]{:S(2)}, u32[]{:S(2)}) collective-permute-start(bf16[384,128]{1,0:T(8,128)(2,1)S(1)} %get-tuple-element.28), channel_id=1, source_target_pairs={{0,1},{1,0},{2,3},{3,2},{4,5},{5,4},{6,7},{7,6},{8,9},{9,8},{10,11... | collective-permute-start | bytes 294920 | tf_op jit(solution)/shard_map/ppermute | solution.py:15
  104.7 6.7 %collective-permute-start.26 = (bf16[384,128]{1,0:T(8,128)(2,1)S(1)}, bf16[384,128]{1,0:T(8,128)(2,1)S(1)}, u32[]{:S(2)}, u32[]{:S(2)}) collective-permute-start(bf16[384,128]{1,0:T(8,128)(2,1)S(1)} %get-tuple-element.29), channel_id=1, source_target_pairs={{0,3},{1,2},{2,1},{3,0},{4,7},{5,6},{6,5},{7,4},{8,11},{9,10},{10,... | collective-permute-start | bytes 294920 | tf_op jit(solution)/shard_map/ppermute | solution.py:15
  106.7 7.3 %collective-permute-start.25 = (bf16[384,128]{1,0:T(8,128)(2,1)S(1)}, bf16[384,128]{1,0:T(8,128)(2,1)S(1)}, u32[]{:S(2)}, u32[]{:S(2)}) collective-permute-start(bf16[384,128]{1,0:T(8,128)(2,1)S(1)} %get-tuple-element.30), channel_id=1, source_target_pairs={{0,2},{1,3},{2,0},{3,1},{4,6},{5,7},{6,4},{7,5},{8,10},{9,11},{10,... | collective-permute-start | bytes 294920 | tf_op jit(solution)/shard_map/ppermute | solution.py:15
  114.1 4.7 %collective-permute-start.27 = (bf16[384,128]{1,0:T(8,128)(2,1)S(1)}, bf16[384,128]{1,0:T(8,128)(2,1)S(1)}, u32[]{:S(2)}, u32[]{:S(2)}) collective-permute-start(bf16[384,128]{1,0:T(8,128)(2,1)S(1)} %get-tuple-element.9), channel_id=1, source_target_pairs={{0,8},{4,12},{8,0},{12,4},{16,24},{20,28},{24,16},{28,20},{1,9},{5... | collective-permute-start | bytes 294920 | tf_op jit(solution)/shard_map/ppermute | solution.py:15
  115.2 7.0 %collective-permute-start.29 = (bf16[384,128]{1,0:T(8,128)(2,1)S(1)}, bf16[384,128]{1,0:T(8,128)(2,1)S(1)}, u32[]{:S(2)}, u32[]{:S(2)}) collective-permute-start(bf16[384,128]{1,0:T(8,128)(2,1)S(1)} %get-tuple-element.9), channel_id=1, source_target_pairs={{0,24},{4,28},{8,16},{12,20},{16,8},{20,12},{24,0},{28,4},{1,25},{... | collective-permute-start | bytes 294920 | tf_op jit(solution)/shard_map/ppermute | solution.py:15
  116.5 5.3 %collective-permute-start.28 = (bf16[384,128]{1,0:T(8,128)(2,1)S(1)}, bf16[384,128]{1,0:T(8,128)(2,1)S(1)}, u32[]{:S(2)}, u32[]{:S(2)}) collective-permute-start(bf16[384,128]{1,0:T(8,128)(2,1)S(1)} %get-tuple-element.9), channel_id=1, source_target_pairs={{0,16},{4,20},{8,24},{12,28},{16,0},{20,4},{24,8},{28,12},{1,17},{... | collective-permute-start | bytes 294920 | tf_op jit(solution)/shard_map/ppermute | solution.py:15
  123.3 4.7 %collective-permute-start.30 = (bf16[384,128]{1,0:T(8,128)(2,1)S(1)}, bf16[384,128]{1,0:T(8,128)(2,1)S(1)}, u32[]{:S(2)}, u32[]{:S(2)}) collective-permute-start(bf16[384,128]{1,0:T(8,128)(2,1)S(1)} %get-tuple-element.25), channel_id=1, source_target_pairs={{0,1},{1,0},{2,3},{3,2},{4,5},{5,4},{6,7},{7,6},{8,9},{9,8},{10,11... | collective-permute-start | bytes 294920 | tf_op jit(solution)/shard_map/ppermute | solution.py:15
  123.3 6.6 %collective-permute-start.32 = (bf16[384,128]{1,0:T(8,128)(2,1)S(1)}, bf16[384,128]{1,0:T(8,128)(2,1)S(1)}, u32[]{:S(2)}, u32[]{:S(2)}) collective-permute-start(bf16[384,128]{1,0:T(8,128)(2,1)S(1)} %get-tuple-element.26), channel_id=1, source_target_pairs={{0,3},{1,2},{2,1},{3,0},{4,7},{5,6},{6,5},{7,4},{8,11},{9,10},{10,... | collective-permute-start | bytes 294920 | tf_op jit(solution)/shard_map/ppermute | solution.py:15
  125.2 7.4 %collective-permute-start.31 = (bf16[384,128]{1,0:T(8,128)(2,1)S(1)}, bf16[384,128]{1,0:T(8,128)(2,1)S(1)}, u32[]{:S(2)}, u32[]{:S(2)}) collective-permute-start(bf16[384,128]{1,0:T(8,128)(2,1)S(1)} %get-tuple-element.27), channel_id=1, source_target_pairs={{0,2},{1,3},{2,0},{3,1},{4,6},{5,7},{6,4},{7,5},{8,10},{9,11},{10,... | collective-permute-start | bytes 294920 | tf_op jit(solution)/shard_map/ppermute | solution.py:15
  132.7 4.7 %collective-permute-start.33 = (bf16[384,128]{1,0:T(8,128)(2,1)S(1)}, bf16[384,128]{1,0:T(8,128)(2,1)S(1)}, u32[]{:S(2)}, u32[]{:S(2)}) collective-permute-start(bf16[384,128]{1,0:T(8,128)(2,1)S(1)} %get-tuple-element.7), channel_id=1, source_target_pairs={{0,8},{4,12},{8,0},{12,4},{16,24},{20,28},{24,16},{28,20},{1,9},{5... | collective-permute-start | bytes 294920 | tf_op jit(solution)/shard_map/ppermute | solution.py:15
  133.6 7.0 %collective-permute-start.35 = (bf16[384,128]{1,0:T(8,128)(2,1)S(1)}, bf16[384,128]{1,0:T(8,128)(2,1)S(1)}, u32[]{:S(2)}, u32[]{:S(2)}) collective-permute-start(bf16[384,128]{1,0:T(8,128)(2,1)S(1)} %get-tuple-element.7), channel_id=1, source_target_pairs={{0,24},{4,28},{8,16},{12,20},{16,8},{20,12},{24,0},{28,4},{1,25},{... | collective-permute-start | bytes 294920 | tf_op jit(solution)/shard_map/ppermute | solution.py:15
  135.2 5.0 %collective-permute-start.34 = (bf16[384,128]{1,0:T(8,128)(2,1)S(1)}, bf16[384,128]{1,0:T(8,128)(2,1)S(1)}, u32[]{:S(2)}, u32[]{:S(2)}) collective-permute-start(bf16[384,128]{1,0:T(8,128)(2,1)S(1)} %get-tuple-element.7), channel_id=1, source_target_pairs={{0,16},{4,20},{8,24},{12,28},{16,0},{20,4},{24,8},{28,12},{1,17},{... | collective-permute-start | bytes 294920 | tf_op jit(solution)/shard_map/ppermute | solution.py:15
  141.7 4.7 %collective-permute-start.36 = (bf16[384,128]{1,0:T(8,128)(2,1)S(1)}, bf16[384,128]{1,0:T(8,128)(2,1)S(1)}, u32[]{:S(2)}, u32[]{:S(2)}) collective-permute-start(bf16[384,128]{1,0:T(8,128)(2,1)S(1)} %get-tuple-element.22), channel_id=1, source_target_pairs={{0,1},{1,0},{2,3},{3,2},{4,5},{5,4},{6,7},{7,6},{8,9},{9,8},{10,11... | collective-permute-start | bytes 294920 | tf_op jit(solution)/shard_map/ppermute | solution.py:15
  141.8 6.6 %collective-permute-start.38 = (bf16[384,128]{1,0:T(8,128)(2,1)S(1)}, bf16[384,128]{1,0:T(8,128)(2,1)S(1)}, u32[]{:S(2)}, u32[]{:S(2)}) collective-permute-start(bf16[384,128]{1,0:T(8,128)(2,1)S(1)} %get-tuple-element.23), channel_id=1, source_target_pairs={{0,3},{1,2},{2,1},{3,0},{4,7},{5,6},{6,5},{7,4},{8,11},{9,10},{10,... | collective-permute-start | bytes 294920 | tf_op jit(solution)/shard_map/ppermute | solution.py:15
  143.8 7.2 %collective-permute-start.37 = (bf16[384,128]{1,0:T(8,128)(2,1)S(1)}, bf16[384,128]{1,0:T(8,128)(2,1)S(1)}, u32[]{:S(2)}, u32[]{:S(2)}) collective-permute-start(bf16[384,128]{1,0:T(8,128)(2,1)S(1)} %get-tuple-element.24), channel_id=1, source_target_pairs={{0,2},{1,3},{2,0},{3,1},{4,6},{5,7},{6,4},{7,5},{8,10},{9,11},{10,... | collective-permute-start | bytes 294920 | tf_op jit(solution)/shard_map/ppermute | solution.py:15
  151.1 5.6 %collective-permute-start.41 = (bf16[384,128]{1,0:T(8,128)(2,1)S(1)}, bf16[384,128]{1,0:T(8,128)(2,1)S(1)}, u32[]{:S(2)}, u32[]{:S(2)}) collective-permute-start(bf16[384,128]{1,0:T(8,128)(2,1)S(1)} %get-tuple-element.5), channel_id=1, source_target_pairs={{0,24},{4,28},{8,16},{12,20},{16,8},{20,12},{24,0},{28,4},{1,25},{... | collective-permute-start | bytes 294920 | tf_op jit(solution)/shard_map/ppermute | solution.py:15
  152.7 5.0 %collective-permute-start.40 = (bf16[384,128]{1,0:T(8,128)(2,1)S(1)}, bf16[384,128]{1,0:T(8,128)(2,1)S(1)}, u32[]{:S(2)}, u32[]{:S(2)}) collective-permute-start(bf16[384,128]{1,0:T(8,128)(2,1)S(1)} %get-tuple-element.5), channel_id=1, source_target_pairs={{0,16},{4,20},{8,24},{12,28},{16,0},{20,4},{24,8},{28,12},{1,17},{... | collective-permute-start | bytes 294920 | tf_op jit(solution)/shard_map/ppermute | solution.py:15
  153.7 4.6 %collective-permute-start.39 = (bf16[384,128]{1,0:T(8,128)(2,1)S(1)}, bf16[384,128]{1,0:T(8,128)(2,1)S(1)}, u32[]{:S(2)}, u32[]{:S(2)}) collective-permute-start(bf16[384,128]{1,0:T(8,128)(2,1)S(1)} %get-tuple-element.5), channel_id=1, source_target_pairs={{0,8},{4,12},{8,0},{12,4},{16,24},{20,28},{24,16},{28,20},{1,9},{5... | collective-permute-start | bytes 294920 | tf_op jit(solution)/shard_map/ppermute | solution.py:15
  159.3 4.7 %collective-permute-start.42 = (bf16[384,128]{1,0:T(8,128)(2,1)S(1)}, bf16[384,128]{1,0:T(8,128)(2,1)S(1)}, u32[]{:S(2)}, u32[]{:S(2)}) collective-permute-start(bf16[384,128]{1,0:T(8,128)(2,1)S(1)} %get-tuple-element.19), channel_id=1, source_target_pairs={{0,1},{1,0},{2,3},{3,2},{4,5},{5,4},{6,7},{7,6},{8,9},{9,8},{10,11... | collective-permute-start | bytes 294920 | tf_op jit(solution)/shard_map/ppermute | solution.py:15
  159.4 6.6 %collective-permute-start.44 = (bf16[384,128]{1,0:T(8,128)(2,1)S(1)}, bf16[384,128]{1,0:T(8,128)(2,1)S(1)}, u32[]{:S(2)}, u32[]{:S(2)}) collective-permute-start(bf16[384,128]{1,0:T(8,128)(2,1)S(1)} %get-tuple-element.20), channel_id=1, source_target_pairs={{0,3},{1,2},{2,1},{3,0},{4,7},{5,6},{6,5},{7,4},{8,11},{9,10},{10,... | collective-permute-start | bytes 294920 | tf_op jit(solution)/shard_map/ppermute | solution.py:15
  161.3 7.4 %collective-permute-start.43 = (bf16[384,128]{1,0:T(8,128)(2,1)S(1)}, bf16[384,128]{1,0:T(8,128)(2,1)S(1)}, u32[]{:S(2)}, u32[]{:S(2)}) collective-permute-start(bf16[384,128]{1,0:T(8,128)(2,1)S(1)} %get-tuple-element.21), channel_id=1, source_target_pairs={{0,2},{1,3},{2,0},{3,1},{4,6},{5,7},{6,4},{7,5},{8,10},{9,11},{10,... | collective-permute-start | bytes 294920 | tf_op jit(solution)/shard_map/ppermute | solution.py:15
  168.7 1.4 collective-permute-start.45

commit v2 on v1

v2 whole, which is shorter than its diff:
```python
import functools

import jax
import jax.numpy as jnp
from jax import lax
from jax.experimental import pallas as pl
from jax.experimental.pallas import tpu as pltpu
from jax.sharding import PartitionSpec as P

DEGREE = 6
PAIR = 2
SLOTS = 2
UNROLL = 6


def exchange(value, axis, size, offset):
    return lax.ppermute(value, axis, [(i, i ^ offset) for i in range(size)])


def place_blocks(step, per, width, half, pieces, sources, place, used, same, other, dense):
    chip, core, piece = place[0], place[1], place[2]
    lane = lax.broadcasted_iota(jnp.int32, (1, SLOTS * width), 1) < width
    held = pieces // 2
    count = dense.shape[0] // (held * PAIR * width)
    halves = [(far, column) for far in range(PAIR) for column in range(per)]

    def block_row(index, carry):
        row = lax.rem(index, count)
        near = lax.rem(index // count, PAIR)
        at = (piece ^ (index // (count * PAIR))) & (held - 1)
        base = (near * pieces + (at | (((piece // held) ^ half) * held))) * count + row
        source_row = pl.multiple_of(((core ^ near) * held + at) * count * width + row * width, width)
        sides = []
        for far, ref in enumerate((same, other)):
            value = ref[pl.ds(source_row, width), :]
            source = PAIR * (chip ^ step) + (core ^ far)
            slots = [used[(base * sources + source) * SLOTS + slot] for slot in range(SLOTS)]
            sides.append((value, pltpu.roll(value, width, 1), slots))
        target = pl.multiple_of(index * width, width)
        for tile in range(len(halves) // 2):
            (far_a, col_a), (far_b, col_b) = halves[2 * tile], halves[2 * tile + 1]
            terms = {}
            for far, turned, wanted, left in (
                (far_a, 0, sides[far_a][2][0] == col_a, True),
                (far_a, 1, sides[far_a][2][1] == col_a, True),
                (far_b, 0, sides[far_b][2][1] == col_b, False),
                (far_b, 1, sides[far_b][2][0] == col_b, False),
            ):
                terms.setdefault((far, turned), []).append((wanted.astype(jnp.int32), left))
            result = None
            for (far, turned), wanted in terms.items():
                sides_wanted = {left: value for value, left in wanted}
                factor = jnp.where(lane, sides_wanted.get(True, 0), sides_wanted.get(False, 0))
                term = sides[far][turned] * factor.astype(jnp.float32).astype(dense.dtype)
                result = term if result is None else result + term
            dense[pl.ds(target, width), pl.ds(tile * SLOTS * width, SLOTS * width)] = result
        return carry

    lax.fori_loop(0, held * PAIR * count, block_row, 0, unroll=UNROLL)


def body(per, trial_vectors, h_blocks, block_col, block_count, center, half_width):
    row_count = lax.axis_size("row")
    col_count = lax.axis_size("col")
    chips = row_count // PAIR
    row_index = lax.axis_index("row")
    chip, core = row_index // PAIR, row_index % PAIR
    piece = lax.axis_index("col")
    domain = h_blocks.shape[2]
    width = h_blocks.shape[3]
    slots = h_blocks.shape[5] // width
    vectors = trial_vectors.shape[1] // PAIR

    raw = h_blocks.reshape(row_count, domain * width, slots * width)
    used = jnp.where(
        lax.broadcasted_iota(jnp.int32, block_col.shape[2:], 2) < block_count[0, 0][:, :, None],
        block_col[0, 0],
        -1,
    ).reshape(-1)
    used = jnp.concatenate([used, exchange(used, "row", row_count, 1)])

    first = trial_vectors[:, :vectors]
    second = trial_vectors[:, vectors:]
    mine = jnp.where(core == 0, first, second)
    theirs = exchange(jnp.where(core == 0, second, first), "row", row_count, 1)
    panel = jnp.concatenate([mine, theirs])

    place = jnp.stack([chip, core, piece]).astype(jnp.int32)
    held = col_count // 2
    part = domain * width // 2
    columns = PAIR * per * width
    scalars = pl.BlockSpec(memory_space=pltpu.SMEM)
    vectors_spec = pl.BlockSpec(memory_space=pltpu.VMEM)
    matrices = [[None] * chips for _ in range(2)]
    for half in (1, 0):
        top = (piece // held) ^ half
        for step in range(chips):
            sent = lax.dynamic_slice(
                raw, (PAIR * (chip ^ step), top * part, 0), (PAIR, part, slots * width)
            )
            same = sent if step == 0 else exchange(sent, "row", row_count, PAIR * step)
            other = exchange(same, "row", row_count, 1)
            matrices[half][step] = pl.pallas_call(
                functools.partial(place_blocks, step, per, width, half, col_count, row_count),
                out_shape=jax.ShapeDtypeStruct((PAIR * part, columns), jnp.bfloat16),
                in_specs=[scalars, scalars, vectors_spec, vectors_spec],
                out_specs=vectors_spec,
                cost_estimate=pl.CostEstimate(
                    flops=PAIR * part * columns * 3,
                    bytes_accessed=PAIR * part * columns * 4,
                    transcendentals=0,
                ),
                compiler_params=pltpu.CompilerParams(
                    vmem_limit_bytes=PAIR * part * (columns + 2 * slots * width) * 4 + (1 << 20)
                ),
                name=f"place_{half}_{step}",
            )(
                place,
                used,
                same.reshape(PAIR * part, slots * width),
                other.reshape(PAIR * part, slots * width),
            )

    centre_value = center[0]
    half_value = half_width[0]
    rows = domain * width // col_count
    span = PAIR * rows

    def operator(current):
        arrived = [current] + [
            exchange(current, "row", row_count, PAIR * step) for step in range(1, chips)
        ]
        parts = {}
        for half in (1, 0):
            total = None
            for matrix, value in zip(matrices[half], arrived):
                term = jnp.dot(matrix, value, preferred_element_type=jnp.float32)
                total = term if total is None else total + term
            for index in range(held):
                step = half * held + index
                value = total[index * span : (index + 1) * span]
                parts[step] = (
                    exchange(value.astype(jnp.bfloat16), "col", col_count, step) if step else value
                )
        owned = parts[0]
        for step in range(1, col_count):
            owned = owned + parts[step].astype(jnp.float32)
        return owned

    previous = panel.astype(jnp.float32)
    current = (operator(panel) - centre_value * previous) / half_value
    for degree_step in range(DEGREE - 1):
        product = operator(current.astype(jnp.bfloat16))
        following = 2.0 * (product - centre_value * current) / half_value - previous
        previous, current = (current, following)

    mine, theirs = current[:rows], exchange(current[rows:], "row", row_count, 1)
    return jnp.where(
        core == 0, jnp.concatenate([mine, theirs], 1), jnp.concatenate([theirs, mine], 1)
    )


def solution(mesh):
    in_specs = (
        P(("row", "col"), None),
        P("col", None, None, None, "row", None),
        P("col", "row", None, None, None),
        P("col", "row", None, None),
        P(),
        P(),
    )
    out_specs = P(("row", "col"), None)

    def whole(trial_vectors, h_blocks, block_col, block_count, center, half_width):
        shape = h_blocks.shape
        per = trial_vectors.shape[0] // (shape[0] * shape[4] * shape[3])
        return jax.shard_map(
            functools.partial(body, per), mesh=mesh, in_specs=in_specs, out_specs=out_specs, check_vma=False
        )(trial_vectors, h_blocks, block_col, block_count, center, half_width)

    return whole
```

time: 173 us -> 150 us (0.87)
  Pallas kernels: 23.9 us -> 8.74 us
  waiting for transfers between devices: 74.2 us -> 60.2 us
  starting transfers between devices: 48.5 us -> 58.9 us
  local copies, waits for them, and re-layouts: 5.28 us -> 2.28 us
    pallas_call x4 -> x8, Pallas kernels: 23.9 us -> 8.74 us  [body(): pl.pallas_call(functools.partial(place_blocks, step, per, width, half, co...]
    ppermute x46 -> x53, waiting for transfers between devices: 74.2 us -> 60.2 us  [exchange(): return lax.ppermute(value, axis, [(i, i ^ offset) for i in range(size)])]
    ppermute x46 -> x53, starting transfers between devices: 48.5 us -> 58.9 us  [exchange(): return lax.ppermute(value, axis, [(i, i ^ offset) for i in range(size)])]
    unnamed x31 -> x5, local copies, waits for them, and re-layouts: 2.66 us -> 0.14 us
    dot_general x24 -> x48, matrix products: 15.1 us -> 15 us  [operator(): term = jnp.dot(matrix, value, preferred_element_type=jnp.float32)]
  transfers between devices with their start and end apart: 46 -> 53, of which waited for: 30 -> 32; matrix products, arithmetic and copies ran while one was open for 6% -> 10% of each run, Pallas kernels for 14% -> 6%
where the time goes in v2:
time: 150 us; the launch traced here: 149 us
  waiting for transfers between devices  60.2 us (40%)
  starting transfers between devices  58.9 us (39%)
  matrix products  15 us (10%)
  Pallas kernels  8.74 us (6%)
  local copies, waits for them, and re-layouts  2.28 us (2%)
  other arithmetic  2.26 us (2%)
  between operations  1.98 us (1%)
    ppermute x53, waiting for transfers between devices, exchange(): return lax.ppermute(value, axis, [(i, i ^ offset) for i in range(size)])  60.2 us
    ppermute x53, starting transfers between devices, exchange(): return lax.ppermute(value, axis, [(i, i ^ offset) for i in range(size)])  58.9 us
    dot_general x48, matrix products, operator(): term = jnp.dot(matrix, value, preferred_element_type=jnp.float32)  15 us
    pallas_call x8, Pallas kernels, body(): pl.pallas_call(functools.partial(place_blocks, step, per, width, half, co...  8.74 us
  transfers between devices with their start and end apart: 53, of which 32 were waited for; matrix products, arithmetic and copies ran while one was open for 10% of the time, Pallas kernels for 6%

profile of v2, /device:TPU:0, one launch (start us, length us, event | category | flops | bytes accessed | tf_op | source)
XLA Modules:
  0.0 149.5 jit_solution(13342447861483219818)
XLA Ops:
  0.0 0.8 broadcast_select_fusion.1
  1.4 1.6 %constant_dynamic-slice_fusion.7 = (bf16[2,384,128]{2,1,0:T(8,128)(2,1)S(1)}, bf16[2,384,128]{2,1,0:T(8,128)(2,1)S(1)}, bf16[2,384,128]{2,1,0:T(8,128)(2,1)S(1)}...) fusion(bf16[8,768,128]{2,1,0:T(8,128)(2,1)} %bitcast.147, ...), kind=kLoop, calls=%fused_computation.102 | loop fusion | bytes 3145752 | tf_op jit(solution)/shard_map/dynamic_slice | solution.py:98
  3.0 3.6 %collective-permute-start.18 = (bf16[2,384,128]{2,1,0:T(8,128)(2,1)S(1)}, bf16[2,384,128]{2,1,0:T(8,128)(2,1)S(1)}, u32[]{:S(2)}, u32[]{:S(2)}) collective-permute-start(bf16[2,384,128]{2,1,0:T(8,128)(2,1)S(1)} %get-tuple-element.16), channel_id=1, source_target_pairs={{0,24},{4,28},{8,16},{12,20},{16,8},{20,12},{24,0},{28,4},{1,25},{... | collective-permute-start | bytes 589832 | tf_op jit(solution)/shard_map/ppermute | solution.py:17
  8.5 3.7 %collective-permute-done.18 = bf16[2,384,128]{2,1,0:T(8,128)(2,1)S(1)} collective-permute-done((bf16[2,384,128]{2,1,0:T(8,128)(2,1)S(1)}, bf16[2,384,128]{2,1,0:T(8,128)(2,1)S(1)}, u32[]{:S(2)}, u32[]{:S(2)}) %collective-permute-start.18) | collective-permute-done | bytes 196640 | tf_op jit(solution)/shard_map/ppermute | solution.py:17
  12.2 4.1 %collective-permute-done.16 = bf16[2,384,128]{2,1,0:T(8,128)(2,1)S(1)} collective-permute-done((bf16[2,384,128]{2,1,0:T(8,128)(2,1)S(1)}, bf16[2,384,128]{2,1,0:T(8,128)(2,1)S(1)}, u32[]{:S(2)}, u32[]{:S(2)}) %collective-permute-start.16) | collective-permute-done | bytes 196640 | tf_op jit(solution)/shard_map/ppermute | solution.py:17
  16.3 1.9 %collective-permute-start.11 = (bf16[384,128]{1,0:T(8,128)(2,1)S(1)}, bf16[384,128]{1,0:T(8,128)(2,1)S(1)}, u32[]{:S(2)}, u32[]{:S(2)}) collective-permute-start(bf16[384,128]{1,0:T(8,128)(2,1)S(1)} %pad_maximum_fusion), channel_id=1, source_target_pairs={{0,24},{4,28},{8,16},{12,20},{16,8},{20,12},{24,0},{28,4},{1,25},{... | collective-permute-start | bytes 294920 | tf_op jit(solution)/shard_map/ppermute | solution.py:17
  18.3 1.4 collective-permute-start.14
  19.7 1.1 place_1_0.1
  20.7 1.5 %collective-permute-start.9 = (bf16[2,384,128]{2,1,0:T(8,128)(2,1)S(1)}, bf16[2,384,128]{2,1,0:T(8,128)(2,1)S(1)}, u32[]{:S(2)}, u32[]{:S(2)}) collective-permute-start(bf16[2,384,128]{2,1,0:T(8,128)(2,1)S(1)} %get-tuple-element.20), channel_id=1, source_target_pairs={{0,24},{4,28},{8,16},{12,20},{16,8},{20,12},{24,0},{28,4},{1,25},{... | collective-permute-start | bytes 589832 | tf_op jit(solution)/shard_map/ppermute | solution.py:17
  22.2 1.1 place_0_0.1
  23.3 0.7 collective-permute-start.6
  24.1 1.1 place_1_3.1
  25.1 1.4 collective-permute-start.3
  27.2 1.1 place_1_2.1
  28.3 7.8 %collective-permute-done.8 = bf16[384,128]{1,0:T(8,128)(2,1)S(1)} collective-permute-done((bf16[384,128]{1,0:T(8,128)(2,1)S(1)}, bf16[384,128]{1,0:T(8,128)(2,1)S(1)}, u32[]{:S(2)}, u32[]{:S(2)}) %collective-permute-start.8) | collective-permute-done | bytes 98336 | tf_op jit(solution)/shard_map/ppermute | solution.py:17
  37.9 1.1 place_1_1.1
  39.0 1.8 %collective-permute-done.5 = bf16[384,128]{1,0:T(8,128)(2,1)S(1)} collective-permute-done((bf16[384,128]{1,0:T(8,128)(2,1)S(1)}, bf16[384,128]{1,0:T(8,128)(2,1)S(1)}, u32[]{:S(2)}, u32[]{:S(2)}) %collective-permute-start.5) | collective-permute-done | bytes 98336 | tf_op jit(solution)/shard_map/ppermute | solution.py:17
  41.4 3.7 %collective-permute-start.21 = (bf16[384,128]{1,0:T(8,128)(2,1)S(1)}, bf16[384,128]{1,0:T(8,128)(2,1)S(1)}, u32[]{:S(2)}, u32[]{:S(2)}) collective-permute-start(bf16[384,128]{1,0:T(8,128)(2,1)S(1)} %get-tuple-element.36), channel_id=1, source_target_pairs={{0,3},{1,2},{2,1},{3,0},{4,7},{5,6},{6,5},{7,4},{8,11},{9,10},{10,... | collective-permute-start | bytes 294920 | tf_op jit(solution)/shard_map/ppermute | solution.py:17
  45.1 1.1 place_0_3.1
  46.2 1.1 place_0_2.1
  47.3 1.3 place_0_1.1
  49.9 0.9 collective-permute-start.12
  52.3 2.2 %collective-permute-done.12 = bf16[384,128]{1,0:T(8,128)(2,1)S(1)} collective-permute-done((bf16[384,128]{1,0:T(8,128)(2,1)S(1)}, bf16[384,128]{1,0:T(8,128)(2,1)S(1)}, u32[]{:S(2)}, u32[]{:S(2)}) %collective-permute-start.12) | collective-permute-done | bytes 98336 | tf_op jit(solution)/shard_map/ppermute | solution.py:17
  54.6 1.6 %collective-permute-start.24 = (bf16[384,128]{1,0:T(8,128)(2,1)S(1)}, bf16[384,128]{1,0:T(8,128)(2,1)S(1)}, u32[]{:S(2)}, u32[]{:S(2)}) collective-permute-start(bf16[384,128]{1,0:T(8,128)(2,1)S(1)} %get-tuple-element.13), channel_id=1, source_target_pairs={{0,24},{4,28},{8,16},{12,20},{16,8},{20,12},{24,0},{28,4},{1,25},{... | collective-permute-start | bytes 294920 | tf_op jit(solution)/shard_map/ppermute | solution.py:17
  56.2 1.1 collective-permute-start.23
  57.3 0.9 collective-permute-start.22
  58.2 2.7 %collective-permute-done.24 = bf16[384,128]{1,0:T(8,128)(2,1)S(1)} collective-permute-done((bf16[384,128]{1,0:T(8,128)(2,1)S(1)}, bf16[384,128]{1,0:T(8,128)(2,1)S(1)}, u32[]{:S(2)}, u32[]{:S(2)}) %collective-permute-start.24) | collective-permute-done | bytes 98336 | tf_op jit(solution)/shard_map/ppermute | solution.py:17
  62.7 2.3 %collective-permute-start.27 = (bf16[384,128]{1,0:T(8,128)(2,1)S(1)}, bf16[384,128]{1,0:T(8,128)(2,1)S(1)}, u32[]{:S(2)}, u32[]{:S(2)}) collective-permute-start(bf16[384,128]{1,0:T(8,128)(2,1)S(1)} %get-tuple-element.34), channel_id=1, source_target_pairs={{0,3},{1,2},{2,1},{3,0},{4,7},{5,6},{6,5},{7,4},{8,11},{9,10},{10,... | collective-permute-start | bytes 294920 | tf_op jit(solution)/shard_map/ppermute | solution.py:17
  66.6 1.9 %collective-permute-start.25 = (bf16[384,128]{1,0:T(8,128)(2,1)S(1)}, bf16[384,128]{1,0:T(8,128)(2,1)S(1)}, u32[]{:S(2)}, u32[]{:S(2)}) collective-permute-start(bf16[384,128]{1,0:T(8,128)(2,1)S(1)} %slice.242), channel_id=1, source_target_pairs={{0,1},{1,0},{2,3},{3,2},{4,5},{5,4},{6,7},{7,6},{8,9},{9,8},{10,11... | collective-permute-start | bytes 294920 | tf_op jit(solution)/shard_map/ppermute | solution.py:17
  68.5 1.2 collective-permute-done.27
  69.6 4.0 %collective-permute-done.26 = bf16[384,128]{1,0:T(8,128)(2,1)S(1)} collective-permute-done((bf16[384,128]{1,0:T(8,128)(2,1)S(1)}, bf16[384,128]{1,0:T(8,128)(2,1)S(1)}, u32[]{:S(2)}, u32[]{:S(2)}) %collective-permute-start.26) | collective-permute-done | bytes 98336 | tf_op jit(solution)/shard_map/ppermute | solution.py:17
  73.7 1.3 collective-permute-start.30
  75.0 2.0 %collective-permute-start.29 = (bf16[384,128]{1,0:T(8,128)(2,1)S(1)}, bf16[384,128]{1,0:T(8,128)(2,1)S(1)}, u32[]{:S(2)}, u32[]{:S(2)}) collective-permute-start(bf16[384,128]{1,0:T(8,128)(2,1)S(1)} %get-tuple-element.11), channel_id=1, source_target_pairs={{0,16},{4,20},{8,24},{12,28},{16,0},{20,4},{24,8},{28,12},{1,17},{... | collective-permute-start | bytes 294920 | tf_op jit(solution)/shard_map/ppermute | solution.py:17
  77.3 2.9 %collective-permute-done.30 = bf16[384,128]{1,0:T(8,128)(2,1)S(1)} collective-permute-done((bf16[384,128]{1,0:T(8,128)(2,1)S(1)}, bf16[384,128]{1,0:T(8,128)(2,1)S(1)}, u32[]{:S(2)}, u32[]{:S(2)}) %collective-permute-start.30) | collective-permute-done | bytes 98336 | tf_op jit(solution)/shard_map/ppermute | solution.py:17
  82.3 2.1 %collective-permute-start.33 = (bf16[384,128]{1,0:T(8,128)(2,1)S(1)}, bf16[384,128]{1,0:T(8,128)(2,1)S(1)}, u32[]{:S(2)}, u32[]{:S(2)}) collective-permute-start(bf16[384,128]{1,0:T(8,128)(2,1)S(1)} %get-tuple-element.32), channel_id=1, source_target_pairs={{0,3},{1,2},{2,1},{3,0},{4,7},{5,6},{6,5},{7,4},{8,11},{9,10},{10,... | collective-permute-start | bytes 294920 | tf_op jit(solution)/shard_map/ppermute | solution.py:17
  85.7 2.4 %collective-permute-start.31 = (bf16[384,128]{1,0:T(8,128)(2,1)S(1)}, bf16[384,128]{1,0:T(8,128)(2,1)S(1)}, u32[]{:S(2)}, u32[]{:S(2)}) collective-permute-start(bf16[384,128]{1,0:T(8,128)(2,1)S(1)} %slice.241), channel_id=1, source_target_pairs={{0,1},{1,0},{2,3},{3,2},{4,5},{5,4},{6,7},{7,6},{8,9},{9,8},{10,11... | collective-permute-start | bytes 294920 | tf_op jit(solution)/shard_map/ppermute | solution.py:17
  88.1 1.0 collective-permute-done.33
  89.1 2.9 %collective-permute-done.32 = bf16[384,128]{1,0:T(8,128)(2,1)S(1)} collective-permute-done((bf16[384,128]{1,0:T(8,128)(2,1)S(1)}, bf16[384,128]{1,0:T(8,128)(2,1)S(1)}, u32[]{:S(2)}, u32[]{:S(2)}) %collective-permute-start.32) | collective-permute-done | bytes 98336 | tf_op jit(solution)/shard_map/ppermute | solution.py:17
  92.5 1.0 collective-permute-start.36
  93.4 1.0 collective-permute-start.35
  94.4 1.6 %collective-permute-start.34 = (bf16[384,128]{1,0:T(8,128)(2,1)S(1)}, bf16[384,128]{1,0:T(8,128)(2,1)S(1)}, u32[]{:S(2)}, u32[]{:S(2)}) collective-permute-start(bf16[384,128]{1,0:T(8,128)(2,1)S(1)} %get-tuple-element.9), channel_id=1, source_target_pairs={{0,8},{4,12},{8,0},{12,4},{16,24},{20,28},{24,16},{28,20},{1,9},{5... | collective-permute-start | bytes 294920 | tf_op jit(solution)/shard_map/ppermute | solution.py:17
  96.0 2.8 %collective-permute-done.36 = bf16[384,128]{1,0:T(8,128)(2,1)S(1)} collective-permute-done((bf16[384,128]{1,0:T(8,128)(2,1)S(1)}, bf16[384,128]{1,0:T(8,128)(2,1)S(1)}, u32[]{:S(2)}, u32[]{:S(2)}) %collective-permute-start.36) | collective-permute-done | bytes 98336 | tf_op jit(solution)/shard_map/ppermute | solution.py:17
  100.2 1.7 %collective-permute-start.39 = (bf16[384,128]{1,0:T(8,128)(2,1)S(1)}, bf16[384,128]{1,0:T(8,128)(2,1)S(1)}, u32[]{:S(2)}, u32[]{:S(2)}) collective-permute-start(bf16[384,128]{1,0:T(8,128)(2,1)S(1)} %get-tuple-element.30), channel_id=1, source_target_pairs={{0,3},{1,2},{2,1},{3,0},{4,7},{5,6},{6,5},{7,4},{8,11},{9,10},{10,... | collective-permute-start | bytes 294920 | tf_op jit(solution)/shard_map/ppermute | solution.py:17
  103.3 2.7 %collective-permute-start.37 = (bf16[384,128]{1,0:T(8,128)(2,1)S(1)}, bf16[384,128]{1,0:T(8,128)(2,1)S(1)}, u32[]{:S(2)}, u32[]{:S(2)}) collective-permute-start(bf16[384,128]{1,0:T(8,128)(2,1)S(1)} %slice.240), channel_id=1, source_target_pairs={{0,1},{1,0},{2,3},{3,2},{4,5},{5,4},{6,7},{7,6},{8,9},{9,8},{10,11... | collective-permute-start | bytes 294920 | tf_op jit(solution)/shard_map/ppermute | solution.py:17
  106.0 1.4 collective-permute-done.39
  107.4 3.2 %collective-permute-done.38 = bf16[384,128]{1,0:T(8,128)(2,1)S(1)} collective-permute-done((bf16[384,128]{1,0:T(8,128)(2,1)S(1)}, bf16[384,128]{1,0:T(8,128)(2,1)S(1)}, u32[]{:S(2)}, u32[]{:S(2)}) %collective-permute-start.38) | collective-permute-done | bytes 98336 | tf_op jit(solution)/shard_map/ppermute | solution.py:17
  110.6 1.8 %collective-permute-start.42 = (bf16[384,128]{1,0:T(8,128)(2,1)S(1)}, bf16[384,128]{1,0:T(8,128)(2,1)S(1)}, u32[]{:S(2)}, u32[]{:S(2)}) collective-permute-start(bf16[384,128]{1,0:T(8,128)(2,1)S(1)} %get-tuple-element.7), channel_id=1, source_target_pairs={{0,24},{4,28},{8,16},{12,20},{16,8},{20,12},{24,0},{28,4},{1,25},{... | collective-permute-start | bytes 294920 | tf_op jit(solution)/shard_map/ppermute | solution.py:17
  112.5 0.9 collective-permute-start.41
  113.3 0.9 collective-permute-start.40
  114.2 2.7 %collective-permute-done.42 = bf16[384,128]{1,0:T(8,128)(2,1)S(1)} collective-permute-done((bf16[384,128]{1,0:T(8,128)(2,1)S(1)}, bf16[384,128]{1,0:T(8,128)(2,1)S(1)}, u32[]{:S(2)}, u32[]{:S(2)}) %collective-permute-start.42) | collective-permute-done | bytes 98336 | tf_op jit(solution)/shard_map/ppermute | solution.py:17
  118.6 1.6 %collective-permute-start.45 = (bf16[384,128]{1,0:T(8,128)(2,1)S(1)}, bf16[384,128]{1,0:T(8,128)(2,1)S(1)}, u32[]{:S(2)}, u32[]{:S(2)}) collective-permute-start(bf16[384,128]{1,0:T(8,128)(2,1)S(1)} %get-tuple-element.28), channel_id=1, source_target_pairs={{0,3},{1,2},{2,1},{3,0},{4,7},{5,6},{6,5},{7,4},{8,11},{9,10},{10,... | collective-permute-start | bytes 294920 | tf_op jit(solution)/shard_map/ppermute | solution.py:17
  121.5 2.9 %collective-permute-start.43 = (bf16[384,128]{1,0:T(8,128)(2,1)S(1)}, bf16[384,128]{1,0:T(8,128)(2,1)S(1)}, u32[]{:S(2)}, u32[]{:S(2)}) collective-permute-start(bf16[384,128]{1,0:T(8,128)(2,1)S(1)} %slice.239), channel_id=1, source_target_pairs={{0,1},{1,0},{2,3},{3,2},{4,5},{5,4},{6,7},{7,6},{8,9},{9,8},{10,11... | collective-permute-start | bytes 294920 | tf_op jit(solution)/shard_map/ppermute | solution.py:17
  124.4 1.2 collective-permute-done.45
  125.6 3.4 %collective-permute-done.44 = bf16[384,128]{1,0:T(8,128)(2,1)S(1)} collective-permute-done((bf16[384,128]{1,0:T(8,128)(2,1)S(1)}, bf16[384,128]{1,0:T(8,128)(2,1)S(1)}, u32[]{:S(2)}, u32[]{:S(2)}) %collective-permute-start.44) | collective-permute-done | bytes 98336 | tf_op jit(solution)/shard_map/ppermute | solution.py:17
  129.1 1.2 collective-permute-start.48
  130.2 1.4 collective-permute-start.47
  131.6 1.0 collective-permute-start.46
  132.6 2.5 %collective-permute-done.48 = bf16[384,128]{1,0:T(8,128)(2,1)S(1)} collective-permute-done((bf16[384,128]{1,0:T(8,128)(2,1)S(1)}, bf16[384,128]{1,0:T(8,128)(2,1)S(1)}, u32[]{:S(2)}, u32[]{:S(2)}) %collective-permute-start.48) | collective-permute-done | bytes 98336 | tf_op jit(solution)/shard_map/ppermute | solution.py:17
  136.9 1.5 %collective-permute-start.51 = (bf16[384,128]{1,0:T(8,128)(2,1)S(1)}, bf16[384,128]{1,0:T(8,128)(2,1)S(1)}, u32[]{:S(2)}, u32[]{:S(2)}) collective-permute-start(bf16[384,128]{1,0:T(8,128)(2,1)S(1)} %get-tuple-element.26), channel_id=1, source_target_pairs={{0,3},{1,2},{2,1},{3,0},{4,7},{5,6},{6,5},{7,4},{8,11},{9,10},{10,... | collective-permute-start | bytes 294920 | tf_op jit(solution)/shard_map/ppermute | solution.py:17
  139.8 2.9 %collective-permute-start.49 = (bf16[384,128]{1,0:T(8,128)(2,1)S(1)}, bf16[384,128]{1,0:T(8,128)(2,1)S(1)}, u32[]{:S(2)}, u32[]{:S(2)}) collective-permute-start(bf16[384,128]{1,0:T(8,128)(2,1)S(1)} %slice.238), channel_id=1, source_target_pairs={{0,1},{1,0},{2,3},{3,2},{4,5},{5,4},{6,7},{7,6},{8,9},{9,8},{10,11... | collective-permute-start | bytes 294920 | tf_op jit(solution)/shard_map/ppermute | solution.py:17
  142.7 1.6 %collective-permute-done.51 = bf16[384,128]{1,0:T(8,128)(2,1)S(1)} collective-permute-done((bf16[384,128]{1,0:T(8,128)(2,1)S(1)}, bf16[384,128]{1,0:T(8,128)(2,1)S(1)}, u32[]{:S(2)}, u32[]{:S(2)}) %collective-permute-start.51) | collective-permute-done | bytes 98336 | tf_op jit(solution)/shard_map/ppermute | solution.py:17
  144.3 3.0 %collective-permute-done.50 = bf16[384,128]{1,0:T(8,128)(2,1)S(1)} collective-permute-done((bf16[384,128]{1,0:T(8,128)(2,1)S(1)}, bf16[384,128]{1,0:T(8,128)(2,1)S(1)}, u32[]{:S(2)}, u32[]{:S(2)}) %collective-permute-start.50) | collective-permute-done | bytes 98336 | tf_op jit(solution)/shard_map/ppermute | solution.py:17
  147.5 1.3 collective-permute-done.52
  148.8 0.7 maximum_select_fusion
  (133 shorter events, 23.8 us)
Async XLA Ops:
  0.8 7.5 %collective-permute-start.2 = (bf16[192,128]{1,0:T(8,128)(2,1)S(1)}, bf16[192,128]{1,0:T(8,128)(2,1)S(1)}, u32[]{:S(2)}, u32[]{:S(2)}) collective-permute-start(bf16[192,128]{1,0:T(8,128)(2,1)S(1)} %get-tuple-element.38), channel_id=1, source_target_pairs={{0,4},{4,0},{8,12},{12,8},{16,20},{20,16},{24,28},{28,24},{1,5},{5... | collective-permute-start | bytes 147464 | tf_op jit(solution)/shard_map/ppermute | solution.py:17
  1.4 5.7 %copy-start.1 = (s32[1,1,12,8]{2,3,1,0:T(8,128)S(1)}, s32[1,1,12,8]{2,3,1,0:T(8,128)}, u32[]{:S(2)}) copy-start(s32[1,1,12,8]{2,3,1,0:T(8,128)} %param.9) | copy-start | bytes 1156
  1.4 6.0 %copy-start = (s32[1,1,12,8,2]{2,4,3,1,0:T(2,128)S(1)}, s32[1,1,12,8,2]{2,4,3,1,0:T(2,128)}, u32[]{:S(2)}) copy-start(s32[1,1,12,8,2]{2,4,3,1,0:T(2,128)} %param.8) | copy-start | bytes 2308
  3.0 9.2 %collective-permute-start.18 = (bf16[2,384,128]{2,1,0:T(8,128)(2,1)S(1)}, bf16[2,384,128]{2,1,0:T(8,128)(2,1)S(1)}, u32[]{:S(2)}, u32[]{:S(2)}) collective-permute-start(bf16[2,384,128]{2,1,0:T(8,128)(2,1)S(1)} %get-tuple-element.16), channel_id=1, source_target_pairs={{0,24},{4,28},{8,16},{12,20},{16,8},{20,12},{24,0},{28,4},{1,25},{... | collective-permute-start | bytes 589832 | tf_op jit(solution)/shard_map/ppermute | solution.py:17
  6.6 9.7 %collective-permute-start.16 = (bf16[2,384,128]{2,1,0:T(8,128)(2,1)S(1)}, bf16[2,384,128]{2,1,0:T(8,128)(2,1)S(1)}, u32[]{:S(2)}, u32[]{:S(2)}) collective-permute-start(bf16[2,384,128]{2,1,0:T(8,128)(2,1)S(1)} %get-tuple-element.17), channel_id=1, source_target_pairs={{0,16},{4,20},{8,24},{12,28},{16,0},{20,4},{24,8},{28,12},{1,17},{... | collective-permute-start | bytes 589832 | tf_op jit(solution)/shard_map/ppermute | solution.py:17
  7.7 8.6 %collective-permute-start = (s32[192]{0:T(256)S(1)}, s32[192]{0:T(256)S(1)}, u32[]{:S(2)}, u32[]{:S(2)}) collective-permute-start(s32[192]{0:T(256)S(1)} %broadcast_select_fusion.2), channel_id=1, source_target_pairs={{0,4},{4,0},{8,12},{12,8},{16,20},{20,16},{24,28},{28,24},{1,5},{5... | collective-permute-start | bytes 2312 | tf_op jit(solution)/shard_map/ppermute | solution.py:17
  7.8 10.5 %collective-permute-start.13 = (bf16[2,384,128]{2,1,0:T(8,128)(2,1)S(1)}, bf16[2,384,128]{2,1,0:T(8,128)(2,1)S(1)}, u32[]{:S(2)}, u32[]{:S(2)}) collective-permute-start(bf16[2,384,128]{2,1,0:T(8,128)(2,1)S(1)} %get-tuple-element.19), channel_id=1, source_target_pairs={{0,4},{4,0},{8,12},{12,8},{16,20},{20,16},{24,28},{28,24},{1,5},{5... | collective-permute-start | bytes 589832 | tf_op jit(solution)/shard_map/ppermute | solution.py:17
  8.4 12.4 %collective-permute-start.1 = (bf16[2,384,128]{2,1,0:T(8,128)(2,1)S(1)}, bf16[2,384,128]{2,1,0:T(8,128)(2,1)S(1)}, u32[]{:S(2)}, u32[]{:S(2)}) collective-permute-start(bf16[2,384,128]{2,1,0:T(8,128)(2,1)S(1)} %get-tuple-element.15), channel_id=1, source_target_pairs={{0,4},{4,0},{8,12},{12,8},{16,20},{20,16},{24,28},{28,24},{1,5},{5... | collective-permute-start | bytes 589832 | tf_op jit(solution)/shard_map/ppermute | solution.py:17
  12.2 11.1 %collective-permute-start.19 = (bf16[2,384,128]{2,1,0:T(8,128)(2,1)S(1)}, bf16[2,384,128]{2,1,0:T(8,128)(2,1)S(1)}, u32[]{:S(2)}, u32[]{:S(2)}) collective-permute-start(bf16[2,384,128]{2,1,0:T(8,128)(2,1)S(1)} %collective-permute-done.18), channel_id=1, source_target_pairs={{0,4},{4,0},{8,12},{12,8},{16,20},{20,16},{24,28},{28,24},{1,5},{5... | collective-permute-start | bytes 589832 | tf_op jit(solution)/shard_map/ppermute | solution.py:17
  16.3 10.3 %collective-permute-start.17 = (bf16[2,384,128]{2,1,0:T(8,128)(2,1)S(1)}, bf16[2,384,128]{2,1,0:T(8,128)(2,1)S(1)}, u32[]{:S(2)}, u32[]{:S(2)}) collective-permute-start(bf16[2,384,128]{2,1,0:T(8,128)(2,1)S(1)} %collective-permute-done.16), channel_id=1, source_target_pairs={{0,4},{4,0},{8,12},{12,8},{16,20},{20,16},{24,28},{28,24},{1,5},{5... | collective-permute-start | bytes 589832 | tf_op jit(solution)/shard_map/ppermute | solution.py:17
  16.3 8.8 %collective-permute-start.11 = (bf16[384,128]{1,0:T(8,128)(2,1)S(1)}, bf16[384,128]{1,0:T(8,128)(2,1)S(1)}, u32[]{:S(2)}, u32[]{:S(2)}) collective-permute-start(bf16[384,128]{1,0:T(8,128)(2,1)S(1)} %pad_maximum_fusion), channel_id=1, source_target_pairs={{0,24},{4,28},{8,16},{12,20},{16,8},{20,12},{24,0},{28,4},{1,25},{... | collective-permute-start | bytes 294920 | tf_op jit(solution)/shard_map/ppermute | solution.py:17
  18.3 18.2 %collective-permute-start.14 = (bf16[2,384,128]{2,1,0:T(8,128)(2,1)S(1)}, bf16[2,384,128]{2,1,0:T(8,128)(2,1)S(1)}, u32[]{:S(2)}, u32[]{:S(2)}) collective-permute-start(bf16[2,384,128]{2,1,0:T(8,128)(2,1)S(1)} %get-tuple-element.18), channel_id=1, source_target_pairs={{0,8},{4,12},{8,0},{12,4},{16,24},{20,28},{24,16},{28,20},{1,9},{5... | collective-permute-start | bytes 589832 | tf_op jit(solution)/shard_map/ppermute | solution.py:17
  20.7 15.8 %collective-permute-start.9 = (bf16[2,384,128]{2,1,0:T(8,128)(2,1)S(1)}, bf16[2,384,128]{2,1,0:T(8,128)(2,1)S(1)}, u32[]{:S(2)}, u32[]{:S(2)}) collective-permute-start(bf16[2,384,128]{2,1,0:T(8,128)(2,1)S(1)} %get-tuple-element.20), channel_id=1, source_target_pairs={{0,24},{4,28},{8,16},{12,20},{16,8},{20,12},{24,0},{28,4},{1,25},{... | collective-permute-start | bytes 589832 | tf_op jit(solution)/shard_map/ppermute | solution.py:17
  23.3 13.7 %collective-permute-start.6 = (bf16[2,384,128]{2,1,0:T(8,128)(2,1)S(1)}, bf16[2,384,128]{2,1,0:T(8,128)(2,1)S(1)}, u32[]{:S(2)}, u32[]{:S(2)}) collective-permute-start(bf16[2,384,128]{2,1,0:T(8,128)(2,1)S(1)} %get-tuple-element.21), channel_id=1, source_target_pairs={{0,16},{4,20},{8,24},{12,28},{16,0},{20,4},{24,8},{28,12},{1,17},{... | collective-permute-start | bytes 589832 | tf_op jit(solution)/shard_map/ppermute | solution.py:17
  25.1 11.9 %collective-permute-start.3 = (bf16[2,384,128]{2,1,0:T(8,128)(2,1)S(1)}, bf16[2,384,128]{2,1,0:T(8,128)(2,1)S(1)}, u32[]{:S(2)}, u32[]{:S(2)}) collective-permute-start(bf16[2,384,128]{2,1,0:T(8,128)(2,1)S(1)} %get-tuple-element.22), channel_id=1, source_target_pairs={{0,8},{4,12},{8,0},{12,4},{16,24},{20,28},{24,16},{28,20},{1,9},{5... | collective-permute-start | bytes 589832 | tf_op jit(solution)/shard_map/ppermute | solution.py:17
  26.6 9.6 %collective-permute-start.8 = (bf16[384,128]{1,0:T(8,128)(2,1)S(1)}, bf16[384,128]{1,0:T(8,128)(2,1)S(1)}, u32[]{:S(2)}, u32[]{:S(2)}) collective-permute-start(bf16[384,128]{1,0:T(8,128)(2,1)S(1)} %pad_maximum_fusion), channel_id=1, source_target_pairs={{0,16},{4,20},{8,24},{12,28},{16,0},{20,4},{24,8},{28,12},{1,17},{... | collective-permute-start | bytes 294920 | tf_op jit(solution)/shard_map/ppermute | solution.py:17
  36.1 4.6 %collective-permute-start.5 = (bf16[384,128]{1,0:T(8,128)(2,1)S(1)}, bf16[384,128]{1,0:T(8,128)(2,1)S(1)}, u32[]{:S(2)}, u32[]{:S(2)}) collective-permute-start(bf16[384,128]{1,0:T(8,128)(2,1)S(1)} %pad_maximum_fusion), channel_id=1, source_target_pairs={{0,8},{4,12},{8,0},{12,4},{16,24},{20,28},{24,16},{28,20},{1,9},{5... | collective-permute-start | bytes 294920 | tf_op jit(solution)/shard_map/ppermute | solution.py:17
  36.5 1.4 collective-permute-start.15
  36.5 8.6 %collective-permute-start.10 = (bf16[2,384,128]{2,1,0:T(8,128)(2,1)S(1)}, bf16[2,384,128]{2,1,0:T(8,128)(2,1)S(1)}, u32[]{:S(2)}, u32[]{:S(2)}) collective-permute-start(bf16[2,384,128]{2,1,0:T(8,128)(2,1)S(1)} %collective-permute-done.9), channel_id=1, source_target_pairs={{0,4},{4,0},{8,12},{12,8},{16,20},{20,16},{24,28},{28,24},{1,5},{5... | collective-permute-start | bytes 589832 | tf_op jit(solution)/shard_map/ppermute | solution.py:17
  37.0 9.2 %collective-permute-start.7 = (bf16[2,384,128]{2,1,0:T(8,128)(2,1)S(1)}, bf16[2,384,128]{2,1,0:T(8,128)(2,1)S(1)}, u32[]{:S(2)}, u32[]{:S(2)}) collective-permute-start(bf16[2,384,128]{2,1,0:T(8,128)(2,1)S(1)} %collective-permute-done.6), channel_id=1, source_target_pairs={{0,4},{4,0},{8,12},{12,8},{16,20},{20,16},{24,28},{28,24},{1,5},{5... | collective-permute-start | bytes 589832 | tf_op jit(solution)/shard_map/ppermute | solution.py:17
  37.1 10.2 %collective-permute-start.4 = (bf16[2,384,128]{2,1,0:T(8,128)(2,1)S(1)}, bf16[2,384,128]{2,1,0:T(8,128)(2,1)S(1)}, u32[]{:S(2)}, u32[]{:S(2)}) collective-permute-start(bf16[2,384,128]{2,1,0:T(8,128)(2,1)S(1)} %collective-permute-done.3), channel_id=1, source_target_pairs={{0,4},{4,0},{8,12},{12,8},{16,20},{20,16},{24,28},{28,24},{1,5},{5... | collective-permute-start | bytes 589832 | tf_op jit(solution)/shard_map/ppermute | solution.py:17
  41.4 10.6 %collective-permute-start.21 = (bf16[384,128]{1,0:T(8,128)(2,1)S(1)}, bf16[384,128]{1,0:T(8,128)(2,1)S(1)}, u32[]{:S(2)}, u32[]{:S(2)}) collective-permute-start(bf16[384,128]{1,0:T(8,128)(2,1)S(1)} %get-tuple-element.36), channel_id=1, source_target_pairs={{0,3},{1,2},{2,1},{3,0},{4,7},{5,6},{6,5},{7,4},{8,11},{9,10},{10,... | collective-permute-start | bytes 294920 | tf_op jit(solution)/shard_map/ppermute | solution.py:17
  45.1 7.2 %collective-permute-start.20 = (bf16[384,128]{1,0:T(8,128)(2,1)S(1)}, bf16[384,128]{1,0:T(8,128)(2,1)S(1)}, u32[]{:S(2)}, u32[]{:S(2)}) collective-permute-start(bf16[384,128]{1,0:T(8,128)(2,1)S(1)} %get-tuple-element.35), channel_id=1, source_target_pairs={{0,2},{1,3},{2,0},{3,1},{4,6},{5,7},{6,4},{7,5},{8,10},{9,11},{10,... | collective-permute-start | bytes 294920 | tf_op jit(solution)/shard_map/ppermute | solution.py:17
  49.9 4.7 %collective-permute-start.12 = (bf16[384,128]{1,0:T(8,128)(2,1)S(1)}, bf16[384,128]{1,0:T(8,128)(2,1)S(1)}, u32[]{:S(2)}, u32[]{:S(2)}) collective-permute-start(bf16[384,128]{1,0:T(8,128)(2,1)S(1)} %slice.243), channel_id=1, source_target_pairs={{0,1},{1,0},{2,3},{3,2},{4,5},{5,4},{6,7},{7,6},{8,9},{9,8},{10,11... | collective-permute-start | bytes 294920 | tf_op jit(solution)/shard_map/ppermute | solution.py:17
  54.6 6.2 %collective-permute-start.24 = (bf16[384,128]{1,0:T(8,128)(2,1)S(1)}, bf16[384,128]{1,0:T(8,128)(2,1)S(1)}, u32[]{:S(2)}, u32[]{:S(2)}) collective-permute-start(bf16[384,128]{1,0:T(8,128)(2,1)S(1)} %get-tuple-element.13), channel_id=1, source_target_pairs={{0,24},{4,28},{8,16},{12,20},{16,8},{20,12},{24,0},{28,4},{1,25},{... | collective-permute-start | bytes 294920 | tf_op jit(solution)/shard_map/ppermute | solution.py:17
  56.2 5.4 %collective-permute-start.23 = (bf16[384,128]{1,0:T(8,128)(2,1)S(1)}, bf16[384,128]{1,0:T(8,128)(2,1)S(1)}, u32[]{:S(2)}, u32[]{:S(2)}) collective-permute-start(bf16[384,128]{1,0:T(8,128)(2,1)S(1)} %get-tuple-element.13), channel_id=1, source_target_pairs={{0,16},{4,20},{8,24},{12,28},{16,0},{20,4},{24,8},{28,12},{1,17},{... | collective-permute-start | bytes 294920 | tf_op jit(solution)/shard_map/ppermute | solution.py:17
  57.3 4.7 %collective-permute-start.22 = (bf16[384,128]{1,0:T(8,128)(2,1)S(1)}, bf16[384,128]{1,0:T(8,128)(2,1)S(1)}, u32[]{:S(2)}, u32[]{:S(2)}) collective-permute-start(bf16[384,128]{1,0:T(8,128)(2,1)S(1)} %get-tuple-element.13), channel_id=1, source_target_pairs={{0,8},{4,12},{8,0},{12,4},{16,24},{20,28},{24,16},{28,20},{1,9},{5... | collective-permute-start | bytes 294920 | tf_op jit(solution)/shard_map/ppermute | solution.py:17
  62.7 7.0 %collective-permute-start.27 = (bf16[384,128]{1,0:T(8,128)(2,1)S(1)}, bf16[384,128]{1,0:T(8,128)(2,1)S(1)}, u32[]{:S(2)}, u32[]{:S(2)}) collective-permute-start(bf16[384,128]{1,0:T(8,128)(2,1)S(1)} %get-tuple-element.34), channel_id=1, source_target_pairs={{0,3},{1,2},{2,1},{3,0},{4,7},{5,6},{6,5},{7,4},{8,11},{9,10},{10,... | collective-permute-start | bytes 294920 | tf_op jit(solution)/shard_map/ppermute | solution.py:17
  64.9 8.7 %collective-permute-start.26 = (bf16[384,128]{1,0:T(8,128)(2,1)S(1)}, bf16[384,128]{1,0:T(8,128)(2,1)S(1)}, u32[]{:S(2)}, u32[]{:S(2)}) collective-permute-start(bf16[384,128]{1,0:T(8,128)(2,1)S(1)} %get-tuple-element.33), channel_id=1, source_target_pairs={{0,2},{1,3},{2,0},{3,1},{4,6},{5,7},{6,4},{7,5},{8,10},{9,11},{10,... | collective-permute-start | bytes 294920 | tf_op jit(solution)/shard_map/ppermute | solution.py:17
  66.6 7.0 %collective-permute-start.25 = (bf16[384,128]{1,0:T(8,128)(2,1)S(1)}, bf16[384,128]{1,0:T(8,128)(2,1)S(1)}, u32[]{:S(2)}, u32[]{:S(2)}) collective-permute-start(bf16[384,128]{1,0:T(8,128)(2,1)S(1)} %slice.242), channel_id=1, source_target_pairs={{0,1},{1,0},{2,3},{3,2},{4,5},{5,4},{6,7},{7,6},{8,9},{9,8},{10,11... | collective-permute-start | bytes 294920 | tf_op jit(solution)/shard_map/ppermute | solution.py:17
  73.7 6.5 %collective-permute-start.30 = (bf16[384,128]{1,0:T(8,128)(2,1)S(1)}, bf16[384,128]{1,0:T(8,128)(2,1)S(1)}, u32[]{:S(2)}, u32[]{:S(2)}) collective-permute-start(bf16[384,128]{1,0:T(8,128)(2,1)S(1)} %get-tuple-element.11), channel_id=1, source_target_pairs={{0,24},{4,28},{8,16},{12,20},{16,8},{20,12},{24,0},{28,4},{1,25},{... | collective-permute-start | bytes 294920 | tf_op jit(solution)/shard_map/ppermute | solution.py:17
  75.0 5.6 %collective-permute-start.29 = (bf16[384,128]{1,0:T(8,128)(2,1)S(1)}, bf16[384,128]{1,0:T(8,128)(2,1)S(1)}, u32[]{:S(2)}, u32[]{:S(2)}) collective-permute-start(bf16[384,128]{1,0:T(8,128)(2,1)S(1)} %get-tuple-element.11), channel_id=1, source_target_pairs={{0,16},{4,20},{8,24},{12,28},{16,0},{20,4},{24,8},{28,12},{1,17},{... | collective-permute-start | bytes 294920 | tf_op jit(solution)/shard_map/ppermute | solution.py:17
  77.0 4.6 %collective-permute-start.28 = (bf16[384,128]{1,0:T(8,128)(2,1)S(1)}, bf16[384,128]{1,0:T(8,128)(2,1)S(1)}, u32[]{:S(2)}, u32[]{:S(2)}) collective-permute-start(bf16[384,128]{1,0:T(8,128)(2,1)S(1)} %get-tuple-element.11), channel_id=1, source_target_pairs={{0,8},{4,12},{8,0},{12,4},{16,24},{20,28},{24,16},{28,20},{1,9},{5... | collective-permute-start | bytes 294920 | tf_op jit(solution)/shard_map/ppermute | solution.py:17
  82.3 6.9 %collective-permute-start.33 = (bf16[384,128]{1,0:T(8,128)(2,1)S(1)}, bf16[384,128]{1,0:T(8,128)(2,1)S(1)}, u32[]{:S(2)}, u32[]{:S(2)}) collective-permute-start(bf16[384,128]{1,0:T(8,128)(2,1)S(1)} %get-tuple-element.32), channel_id=1, source_target_pairs={{0,3},{1,2},{2,1},{3,0},{4,7},{5,6},{6,5},{7,4},{8,11},{9,10},{10,... | collective-permute-start | bytes 294920 | tf_op jit(solution)/shard_map/ppermute | solution.py:17
  84.4 7.6 %collective-permute-start.32 = (bf16[384,128]{1,0:T(8,128)(2,1)S(1)}, bf16[384,128]{1,0:T(8,128)(2,1)S(1)}, u32[]{:S(2)}, u32[]{:S(2)}) collective-permute-start(bf16[384,128]{1,0:T(8,128)(2,1)S(1)} %get-tuple-element.31), channel_id=1, source_target_pairs={{0,2},{1,3},{2,0},{3,1},{4,6},{5,7},{6,4},{7,5},{8,10},{9,11},{10,... | collective-permute-start | bytes 294920 | tf_op jit(solution)/shard_map/ppermute | solution.py:17
  85.7 6.6 %collective-permute-start.31 = (bf16[384,128]{1,0:T(8,128)(2,1)S(1)}, bf16[384,128]{1,0:T(8,128)(2,1)S(1)}, u32[]{:S(2)}, u32[]{:S(2)}) collective-permute-start(bf16[384,128]{1,0:T(8,128)(2,1)S(1)} %slice.241), channel_id=1, source_target_pairs={{0,1},{1,0},{2,3},{3,2},{4,5},{5,4},{6,7},{7,6},{8,9},{9,8},{10,11... | collective-permute-start | bytes 294920 | tf_op jit(solution)/shard_map/ppermute | solution.py:17
  92.5 6.4 %collective-permute-start.36 = (bf16[384,128]{1,0:T(8,128)(2,1)S(1)}, bf16[384,128]{1,0:T(8,128)(2,1)S(1)}, u32[]{:S(2)}, u32[]{:S(2)}) collective-permute-start(bf16[384,128]{1,0:T(8,128)(2,1)S(1)} %get-tuple-element.9), channel_id=1, source_target_pairs={{0,24},{4,28},{8,16},{12,20},{16,8},{20,12},{24,0},{28,4},{1,25},{... | collective-permute-start | bytes 294920 | tf_op jit(solution)/shard_map/ppermute | solution.py:17
  93.4 5.8 %collective-permute-start.35 = (bf16[384,128]{1,0:T(8,128)(2,1)S(1)}, bf16[384,128]{1,0:T(8,128)(2,1)S(1)}, u32[]{:S(2)}, u32[]{:S(2)}) collective-permute-start(bf16[384,128]{1,0:T(8,128)(2,1)S(1)} %get-tuple-element.9), channel_id=1, source_target_pairs={{0,16},{4,20},{8,24},{12,28},{16,0},{20,4},{24,8},{28,12},{1,17},{... | collective-permute-start | bytes 294920 | tf_op jit(solution)/shard_map/ppermute | solution.py:17
  94.4 5.1 %collective-permute-start.34 = (bf16[384,128]{1,0:T(8,128)(2,1)S(1)}, bf16[384,128]{1,0:T(8,128)(2,1)S(1)}, u32[]{:S(2)}, u32[]{:S(2)}) collective-permute-start(bf16[384,128]{1,0:T(8,128)(2,1)S(1)} %get-tuple-element.9), channel_id=1, source_target_pairs={{0,8},{4,12},{8,0},{12,4},{16,24},{20,28},{24,16},{28,20},{1,9},{5... | collective-permute-start | bytes 294920 | tf_op jit(solution)/shard_map/ppermute | solution.py:17
  100.2 7.2 %collective-permute-start.39 = (bf16[384,128]{1,0:T(8,128)(2,1)S(1)}, bf16[384,128]{1,0:T(8,128)(2,1)S(1)}, u32[]{:S(2)}, u32[]{:S(2)}) collective-permute-start(bf16[384,128]{1,0:T(8,128)(2,1)S(1)} %get-tuple-element.30), channel_id=1, source_target_pairs={{0,3},{1,2},{2,1},{3,0},{4,7},{5,6},{6,5},{7,4},{8,11},{9,10},{10,... | collective-permute-start | bytes 294920 | tf_op jit(solution)/shard_map/ppermute | solution.py:17
  101.9 8.6 %collective-permute-start.38 = (bf16[384,128]{1,0:T(8,128)(2,1)S(1)}, bf16[384,128]{1,0:T(8,128)(2,1)S(1)}, u32[]{:S(2)}, u32[]{:S(2)}) collective-permute-start(bf16[384,128]{1,0:T(8,128)(2,1)S(1)} %get-tuple-element.29), channel_id=1, source_target_pairs={{0,2},{1,3},{2,0},{3,1},{4,6},{5,7},{6,4},{7,5},{8,10},{9,11},{10,... | collective-permute-start | bytes 294920 | tf_op jit(solution)/shard_map/ppermute | solution.py:17
  103.3 7.2 %collective-permute-start.37 = (bf16[384,128]{1,0:T(8,128)(2,1)S(1)}, bf16[384,128]{1,0:T(8,128)(2,1)S(1)}, u32[]{:S(2)}, u32[]{:S(2)}) collective-permute-start(bf16[384,128]{1,0:T(8,128)(2,1)S(1)} %slice.240), channel_id=1, source_target_pairs={{0,1},{1,0},{2,3},{3,2},{4,5},{5,4},{6,7},{7,6},{8,9},{9,8},{10,11... | collective-permute-start | bytes 294920 | tf_op jit(solution)/shard_map/ppermute | solution.py:17
  110.6 6.3 %collective-permute-start.42 = (bf16[384,128]{1,0:T(8,128)(2,1)S(1)}, bf16[384,128]{1,0:T(8,128)(2,1)S(1)}, u32[]{:S(2)}, u32[]{:S(2)}) collective-permute-start(bf16[384,128]{1,0:T(8,128)(2,1)S(1)} %get-tuple-element.7), channel_id=1, source_target_pairs={{0,24},{4,28},{8,16},{12,20},{16,8},{20,12},{24,0},{28,4},{1,25},{... | collective-permute-start | bytes 294920 | tf_op jit(solution)/shard_map/ppermute | solution.py:17
  112.5 5.1 %collective-permute-start.41 = (bf16[384,128]{1,0:T(8,128)(2,1)S(1)}, bf16[384,128]{1,0:T(8,128)(2,1)S(1)}, u32[]{:S(2)}, u32[]{:S(2)}) collective-permute-start(bf16[384,128]{1,0:T(8,128)(2,1)S(1)} %get-tuple-element.7), channel_id=1, source_target_pairs={{0,16},{4,20},{8,24},{12,28},{16,0},{20,4},{24,8},{28,12},{1,17},{... | collective-permute-start | bytes 294920 | tf_op jit(solution)/shard_map/ppermute | solution.py:17
  113.3 4.6 %collective-permute-start.40 = (bf16[384,128]{1,0:T(8,128)(2,1)S(1)}, bf16[384,128]{1,0:T(8,128)(2,1)S(1)}, u32[]{:S(2)}, u32[]{:S(2)}) collective-permute-start(bf16[384,128]{1,0:T(8,128)(2,1)S(1)} %get-tuple-element.7), channel_id=1, source_target_pairs={{0,8},{4,12},{8,0},{12,4},{16,24},{20,28},{24,16},{28,20},{1,9},{5... | collective-permute-start | bytes 294920 | tf_op jit(solution)/shard_map/ppermute | solution.py:17
  118.6 7.0 %collective-permute-start.45 = (bf16[384,128]{1,0:T(8,128)(2,1)S(1)}, bf16[384,128]{1,0:T(8,128)(2,1)S(1)}, u32[]{:S(2)}, u32[]{:S(2)}) collective-permute-start(bf16[384,128]{1,0:T(8,128)(2,1)S(1)} %get-tuple-element.28), channel_id=1, source_target_pairs={{0,3},{1,2},{2,1},{3,0},{4,7},{5,6},{6,5},{7,4},{8,11},{9,10},{10,... | collective-permute-start | bytes 294920 | tf_op jit(solution)/shard_map/ppermute | solution.py:17
  120.2 8.8 %collective-permute-start.44 = (bf16[384,128]{1,0:T(8,128)(2,1)S(1)}, bf16[384,128]{1,0:T(8,128)(2,1)S(1)}, u32[]{:S(2)}, u32[]{:S(2)}) collective-permute-start(bf16[384,128]{1,0:T(8,128)(2,1)S(1)} %get-tuple-element.27), channel_id=1, source_target_pairs={{0,2},{1,3},{2,0},{3,1},{4,6},{5,7},{6,4},{7,5},{8,10},{9,11},{10,... | collective-permute-start | bytes 294920 | tf_op jit(solution)/shard_map/ppermute | solution.py:17
  121.5 7.5 %collective-permute-start.43 = (bf16[384,128]{1,0:T(8,128)(2,1)S(1)}, bf16[384,128]{1,0:T(8,128)(2,1)S(1)}, u32[]{:S(2)}, u32[]{:S(2)}) collective-permute-start(bf16[384,128]{1,0:T(8,128)(2,1)S(1)} %slice.239), channel_id=1, source_target_pairs={{0,1},{1,0},{2,3},{3,2},{4,5},{5,4},{6,7},{7,6},{8,9},{9,8},{10,11... | collective-permute-start | bytes 294920 | tf_op jit(solution)/shard_map/ppermute | solution.py:17
  129.1 6.1 %collective-permute-start.48 = (bf16[384,128]{1,0:T(8,128)(2,1)S(1)}, bf16[384,128]{1,0:T(8,128)(2,1)S(1)}, u32[]{:S(2)}, u32[]{:S(2)}) collective-permute-start(bf16[384,128]{1,0:T(8,128)(2,1)S(1)} %get-tuple-element.5), channel_id=1, source_target_pairs={{0,24},{4,28},{8,16},{12,20},{16,8},{20,12},{24,0},{28,4},{1,25},{... | collective-permute-start | bytes 294920 | tf_op jit(solution)/shard_map/ppermute | solution.py:17
  130.2 5.6 %collective-permute-start.47 = (bf16[384,128]{1,0:T(8,128)(2,1)S(1)}, bf16[384,128]{1,0:T(8,128)(2,1)S(1)}, u32[]{:S(2)}, u32[]{:S(2)}) collective-permute-start(bf16[384,128]{1,0:T(8,128)(2,1)S(1)} %get-tuple-element.5), channel_id=1, source_target_pairs={{0,16},{4,20},{8,24},{12,28},{16,0},{20,4},{24,8},{28,12},{1,17},{... | collective-permute-start | bytes 294920 | tf_op jit(solution)/shard_map/ppermute | solution.py:17
  131.6 4.6 %collective-permute-start.46 = (bf16[384,128]{1,0:T(8,128)(2,1)S(1)}, bf16[384,128]{1,0:T(8,128)(2,1)S(1)}, u32[]{:S(2)}, u32[]{:S(2)}) collective-permute-start(bf16[384,128]{1,0:T(8,128)(2,1)S(1)} %get-tuple-element.5), channel_id=1, source_target_pairs={{0,8},{4,12},{8,0},{12,4},{16,24},{20,28},{24,16},{28,20},{1,9},{5... | collective-permute-start | bytes 294920 | tf_op jit(solution)/shard_map/ppermute | solution.py:17
  136.9 7.4 %collective-permute-start.51 = (bf16[384,128]{1,0:T(8,128)(2,1)S(1)}, bf16[384,128]{1,0:T(8,128)(2,1)S(1)}, u32[]{:S(2)}, u32[]{:S(2)}) collective-permute-start(bf16[384,128]{1,0:T(8,128)(2,1)S(1)} %get-tuple-element.26), channel_id=1, source_target_pairs={{0,3},{1,2},{2,1},{3,0},{4,7},{5,6},{6,5},{7,4},{8,11},{9,10},{10,... | collective-permute-start | bytes 294920 | tf_op jit(solution)/shard_map/ppermute | solution.py:17
  138.4 8.9 %collective-permute-start.50 = (bf16[384,128]{1,0:T(8,128)(2,1)S(1)}, bf16[384,128]{1,0:T(8,128)(2,1)S(1)}, u32[]{:S(2)}, u32[]{:S(2)}) collective-permute-start(bf16[384,128]{1,0:T(8,128)(2,1)S(1)} %get-tuple-element.25), channel_id=1, source_target_pairs={{0,2},{1,3},{2,0},{3,1},{4,6},{5,7},{6,4},{7,5},{8,10},{9,11},{10,... | collective-permute-start | bytes 294920 | tf_op jit(solution)/shard_map/ppermute | solution.py:17
  139.8 7.4 %collective-permute-start.49 = (bf16[384,128]{1,0:T(8,128)(2,1)S(1)}, bf16[384,128]{1,0:T(8,128)(2,1)S(1)}, u32[]{:S(2)}, u32[]{:S(2)}) collective-permute-start(bf16[384,128]{1,0:T(8,128)(2,1)S(1)} %slice.238), channel_id=1, source_target_pairs={{0,1},{1,0},{2,3},{3,2},{4,5},{5,4},{6,7},{7,6},{8,9},{9,8},{10,11... | collective-permute-start | bytes 294920 | tf_op jit(solution)/shard_map/ppermute | solution.py:17
  147.4 1.4 collective-permute-start.52

commit v3 on v2

--- a/solution.py
+++ b/solution.py
@@ -6,6 +6,7 @@
 from jax.experimental import pallas as pl
 from jax.experimental.pallas import tpu as pltpu
 from jax.sharding import PartitionSpec as P
+
 
 DEGREE = 6
 PAIR = 2
@@ -59,7 +60,7 @@
     lax.fori_loop(0, held * PAIR * count, block_row, 0, unroll=UNROLL)
 
 
-def body(per, trial_vectors, h_blocks, block_col, block_count, center, half_width):
+def filter_body(per, trial_vectors, h_blocks, block_col, block_count, center, half_width):
     row_count = lax.axis_size("row")
     col_count = lax.axis_size("col")
     chips = row_count // PAIR
@@ -92,12 +93,19 @@
     scalars = pl.BlockSpec(memory_space=pltpu.SMEM)
     vectors_spec = pl.BlockSpec(memory_space=pltpu.VMEM)
     matrices = [[None] * chips for _ in range(2)]
+    sends = {}
+    last = None
     for half in (1, 0):
         top = (piece // held) ^ half
+        for step in (*range(1, chips), 0):
+            at = PAIR * (chip ^ step)
+            if last is not None:
+                at, _ = lax.optimization_barrier((at, last))
+            last = lax.dynamic_slice(raw, (at, top * part, 0), (PAIR, part, slots * width))
+            sends[half, step] = last
+    for half in (1, 0):
         for step in range(chips):
-            sent = lax.dynamic_slice(
-                raw, (PAIR * (chip ^ step), top * part, 0), (PAIR, part, slots * width)
-            )
+            sent = sends[half, step]
             same = sent if step == 0 else exchange(sent, "row", row_count, PAIR * step)
             other = exchange(same, "row", row_count, 1)
             matrices[half][step] = pl.pallas_call(
@@ -113,7 +121,6 @@
                 compiler_params=pltpu.CompilerParams(
                     vmem_limit_bytes=PAIR * part * (columns + 2 * slots * width) * 4 + (1 << 20)
                 ),
-                name=f"place_{half}_{step}",
             )(
                 place,
                 used,
@@ -127,21 +134,21 @@
     span = PAIR * rows
 
     def operator(current):
-        arrived = [current] + [
-            exchange(current, "row", row_count, PAIR * step) for step in range(1, chips)
-        ]
+        arrived = [current]
+        for step in range(1, chips):
+            arrived.append(exchange(current, "row", row_count, PAIR * step))
         parts = {}
         for half in (1, 0):
             total = None
-            for matrix, value in zip(matrices[half], arrived):
+            for step, (matrix, value) in enumerate(zip(matrices[half], arrived)):
                 term = jnp.dot(matrix, value, preferred_element_type=jnp.float32)
-                total = term if total is None else total + term
+                total = term if total is None else lax.optimization_barrier(total) + term
             for index in range(held):
                 step = half * held + index
                 value = total[index * span : (index + 1) * span]
-                parts[step] = (
-                    exchange(value.astype(jnp.bfloat16), "col", col_count, step) if step else value
-                )
+                if step:
+                    value = exchange(value.astype(jnp.bfloat16), "col", col_count, step)
+                parts[step] = value
         owned = parts[0]
         for step in range(1, col_count):
             owned = owned + parts[step].astype(jnp.float32)
@@ -149,7 +156,7 @@
 
     previous = panel.astype(jnp.float32)
     current = (operator(panel) - centre_value * previous) / half_value
-    for degree_step in range(DEGREE - 1):
+    for _ in range(DEGREE - 1):
         product = operator(current.astype(jnp.bfloat16))
         following = 2.0 * (product - centre_value * current) / half_value - previous
         previous, current = (current, following)
@@ -158,6 +165,10 @@
     return jnp.where(
         core == 0, jnp.concatenate([mine, theirs], 1), jnp.concatenate([theirs, mine], 1)
     )
+
+
+def body(per, *arguments):
+    return filter_body(per, *arguments)
 
 
 def solution(mesh):

time: 150 us -> 143 us (0.953)
  waiting for transfers between devices: 60.2 us -> 49.6 us
  other arithmetic: 2.26 us -> 4.04 us
    ppermute x53, waiting for transfers between devices: 60.2 us -> 49.6 us  [exchange(): return lax.ppermute(value, axis, [(i, i ^ offset) for i in range(size)])]
  transfers between devices with their start and end apart: 53 -> 53, of which waited for: 32 -> 37; matrix products, arithmetic and copies ran while one was open for 10% -> 11% of each run, Pallas kernels for 6% -> 6%
where the time goes in v3:
time: 143 us; the launch traced here: 142 us
  starting transfers between devices  59.8 us (42%)
  waiting for transfers between devices  49.6 us (35%)
  matrix products  15 us (10%)
  Pallas kernels  8.74 us (6%)
  other arithmetic  4.04 us (3%)
  local copies, waits for them, and re-layouts  2.9 us (2%)
  between operations  2.36 us (2%)
    ppermute x53, starting transfers between devices, exchange(): return lax.ppermute(value, axis, [(i, i ^ offset) for i in range(size)])  59.8 us
    ppermute x53, waiting for transfers between devices, exchange(): return lax.ppermute(value, axis, [(i, i ^ offset) for i in range(size)])  49.6 us
    dot_general x48, matrix products, operator(): term = jnp.dot(matrix, value, preferred_element_type=jnp.float32)  15 us
    pallas_call x8, Pallas kernels, filter_body(): pl.pallas_call(functools.partial(place_blocks, step, per, width, half, co...  8.74 us
  transfers between devices with their start and end apart: 53, of which 37 were waited for; matrix products, arithmetic and copies ran while one was open for 11% of the time, Pallas kernels for 6%

profile of v3, /device:TPU:0, one launch (start us, length us, event | category | flops | bytes accessed | tf_op | source)
XLA Modules:
  0.0 142.4 jit_solution(3392814442995490459)
XLA Ops:
  0.0 1.0 broadcast_select_fusion.1
  3.7 3.0 %collective-permute-start.14 = (bf16[2,384,128]{2,1,0:T(8,128)(2,1)S(1)}, bf16[2,384,128]{2,1,0:T(8,128)(2,1)S(1)}, u32[]{:S(2)}, u32[]{:S(2)}) collective-permute-start(bf16[2,384,128]{2,1,0:T(8,128)(2,1)S(1)} %constant_dynamic-slice_fusion.7), channel_id=1, source_target_pairs={{0,8},{4,12},{8,0},{12,4},{16,24},{20,28},{24,16},{28,20},{1,9},{5... | collective-permute-start | bytes 589832 | tf_op jit(solution)/shard_map/ppermute | solution.py:18
  7.3 1.5 %collective-permute-start.16 = (bf16[2,384,128]{2,1,0:T(8,128)(2,1)}, bf16[2,384,128]{2,1,0:T(8,128)(2,1)S(1)}, u32[]{:S(2)}, u32[]{:S(2)}) collective-permute-start(bf16[2,384,128]{2,1,0:T(8,128)(2,1)} %constant_dynamic-slice_fusion.6), channel_id=1, source_target_pairs={{0,16},{4,20},{8,24},{12,28},{16,0},{20,4},{24,8},{28,12},{1,17},{... | collective-permute-start | bytes 589832 | tf_op jit(solution)/shard_map/ppermute | solution.py:18
  10.4 1.4 collective-permute-start.3
  11.8 1.1 shard_map.68
  13.6 1.1 shard_map.64
  15.1 3.1 %collective-permute-done.16 = bf16[2,384,128]{2,1,0:T(8,128)(2,1)S(1)} collective-permute-done((bf16[2,384,128]{2,1,0:T(8,128)(2,1)}, bf16[2,384,128]{2,1,0:T(8,128)(2,1)S(1)}, u32[]{:S(2)}, u32[]{:S(2)}) %collective-permute-start.16) | collective-permute-done | bytes 196640 | tf_op jit(solution)/shard_map/ppermute | solution.py:18
  18.5 1.7 %collective-permute-start.6 = (bf16[2,384,128]{2,1,0:T(8,128)(2,1)S(1)}, bf16[2,384,128]{2,1,0:T(8,128)(2,1)S(1)}, u32[]{:S(2)}, u32[]{:S(2)}) collective-permute-start(bf16[2,384,128]{2,1,0:T(8,128)(2,1)S(1)} %constant_dynamic-slice_fusion.2), channel_id=1, source_target_pairs={{0,16},{4,20},{8,24},{12,28},{16,0},{20,4},{24,8},{28,12},{1,17},{... | collective-permute-start | bytes 589832 | tf_op jit(solution)/shard_map/ppermute | solution.py:18
  20.3 1.1 shard_map.69
  21.3 1.6 %collective-permute-done.5 = bf16[384,128]{1,0:T(8,128)(2,1)S(1)} collective-permute-done((bf16[384,128]{1,0:T(8,128)(2,1)S(1)}, bf16[384,128]{1,0:T(8,128)(2,1)S(1)}, u32[]{:S(2)}, u32[]{:S(2)}) %collective-permute-start.5) | collective-permute-done | bytes 98336 | tf_op jit(solution)/shard_map/ppermute | solution.py:18
  22.9 2.1 %collective-permute-start.9 = (bf16[2,384,128]{2,1,0:T(8,128)(2,1)S(1)}, bf16[2,384,128]{2,1,0:T(8,128)(2,1)S(1)}, u32[]{:S(2)}, u32[]{:S(2)}) collective-permute-start(bf16[2,384,128]{2,1,0:T(8,128)(2,1)S(1)} %constant_dynamic-slice_fusion.1), channel_id=1, source_target_pairs={{0,24},{4,28},{8,16},{12,20},{16,8},{20,12},{24,0},{28,4},{1,25},{... | collective-permute-start | bytes 589832 | tf_op jit(solution)/shard_map/ppermute | solution.py:18
  25.9 1.1 shard_map.70
  27.0 5.3 %collective-permute-done.8 = bf16[384,128]{1,0:T(8,128)(2,1)S(1)} collective-permute-done((bf16[384,128]{1,0:T(8,128)(2,1)S(1)}, bf16[384,128]{1,0:T(8,128)(2,1)S(1)}, u32[]{:S(2)}, u32[]{:S(2)}) %collective-permute-start.8) | collective-permute-done | bytes 98336 | tf_op jit(solution)/shard_map/ppermute | solution.py:18
  32.2 1.7 %collective-permute-start.11 = (bf16[384,128]{1,0:T(8,128)(2,1)S(1)}, bf16[384,128]{1,0:T(8,128)(2,1)S(1)}, u32[]{:S(2)}, u32[]{:S(2)}) collective-permute-start(bf16[384,128]{1,0:T(8,128)(2,1)S(1)} %pad_maximum_fusion), channel_id=1, source_target_pairs={{0,24},{4,28},{8,16},{12,20},{16,8},{20,12},{24,0},{28,4},{1,25},{... | collective-permute-start | bytes 294920 | tf_op jit(solution)/shard_map/ppermute | solution.py:18
  35.3 1.1 shard_map.71
  36.4 1.3 collective-permute-done.11
  38.2 3.7 %collective-permute-start.21 = (bf16[384,128]{1,0:T(8,128)(2,1)S(1)}, bf16[384,128]{1,0:T(8,128)(2,1)S(1)}, u32[]{:S(2)}, u32[]{:S(2)}) collective-permute-start(bf16[384,128]{1,0:T(8,128)(2,1)S(1)} %get-tuple-element.42), channel_id=1, source_target_pairs={{0,3},{1,2},{2,1},{3,0},{4,7},{5,6},{6,5},{7,4},{8,11},{9,10},{10,... | collective-permute-start | bytes 294920 | tf_op jit(solution)/shard_map/ppermute | solution.py:18
  41.8 1.1 shard_map.65
  43.3 1.1 shard_map.66
  44.8 1.3 shard_map.67
  46.4 0.9 collective-permute-start.12
  48.6 0.9 collective-permute-done.20
  49.4 1.9 %collective-permute-done.12 = bf16[384,128]{1,0:T(8,128)(2,1)S(1)} collective-permute-done((bf16[384,128]{1,0:T(8,128)(2,1)S(1)}, bf16[384,128]{1,0:T(8,128)(2,1)S(1)}, u32[]{:S(2)}, u32[]{:S(2)}) %collective-permute-start.12) | collective-permute-done | bytes 98336 | tf_op jit(solution)/shard_map/ppermute | solution.py:18
  51.7 1.4 collective-permute-start.22
  53.8 1.5 %collective-permute-start.24 = (bf16[384,128]{1,0:T(8,128)(2,1)S(1)}, bf16[384,128]{1,0:T(8,128)(2,1)S(1)}, u32[]{:S(2)}, u32[]{:S(2)}) collective-permute-start(bf16[384,128]{1,0:T(8,128)(2,1)S(1)} %get-tuple-element.27), channel_id=1, source_target_pairs={{0,24},{4,28},{8,16},{12,20},{16,8},{20,12},{24,0},{28,4},{1,25},{... | collective-permute-start | bytes 294920 | tf_op jit(solution)/shard_map/ppermute | solution.py:18
  55.6 1.2 collective-permute-done.22
  57.1 0.9 collective-permute-done.23
  58.4 0.9 collective-permute-done.24
  59.7 2.4 %collective-permute-start.27 = (bf16[384,128]{1,0:T(8,128)(2,1)S(1)}, bf16[384,128]{1,0:T(8,128)(2,1)S(1)}, u32[]{:S(2)}, u32[]{:S(2)}) collective-permute-start(bf16[384,128]{1,0:T(8,128)(2,1)S(1)} %get-tuple-element.40), channel_id=1, source_target_pairs={{0,3},{1,2},{2,1},{3,0},{4,7},{5,6},{6,5},{7,4},{8,11},{9,10},{10,... | collective-permute-start | bytes 294920 | tf_op jit(solution)/shard_map/ppermute | solution.py:18
  63.9 1.5 %collective-permute-start.25 = (bf16[384,128]{1,0:T(8,128)(2,1)S(1)}, bf16[384,128]{1,0:T(8,128)(2,1)S(1)}, u32[]{:S(2)}, u32[]{:S(2)}) collective-permute-start(bf16[384,128]{1,0:T(8,128)(2,1)S(1)} %slice.242), channel_id=1, source_target_pairs={{0,1},{1,0},{2,3},{3,2},{4,5},{5,4},{6,7},{7,6},{8,9},{9,8},{10,11... | collective-permute-start | bytes 294920 | tf_op jit(solution)/shard_map/ppermute | solution.py:18
  65.3 1.7 %collective-permute-done.27 = bf16[384,128]{1,0:T(8,128)(2,1)S(1)} collective-permute-done((bf16[384,128]{1,0:T(8,128)(2,1)S(1)}, bf16[384,128]{1,0:T(8,128)(2,1)S(1)}, u32[]{:S(2)}, u32[]{:S(2)}) %collective-permute-start.27) | collective-permute-done | bytes 98336 | tf_op jit(solution)/shard_map/ppermute | solution.py:18
  67.0 2.4 %collective-permute-done.26 = bf16[384,128]{1,0:T(8,128)(2,1)S(1)} collective-permute-done((bf16[384,128]{1,0:T(8,128)(2,1)S(1)}, bf16[384,128]{1,0:T(8,128)(2,1)S(1)}, u32[]{:S(2)}, u32[]{:S(2)}) %collective-permute-start.26) | collective-permute-done | bytes 98336 | tf_op jit(solution)/shard_map/ppermute | solution.py:18
  70.0 1.6 %collective-permute-start.28 = (bf16[384,128]{1,0:T(8,128)(2,1)S(1)}, bf16[384,128]{1,0:T(8,128)(2,1)S(1)}, u32[]{:S(2)}, u32[]{:S(2)}) collective-permute-start(bf16[384,128]{1,0:T(8,128)(2,1)S(1)} %get-tuple-element.25), channel_id=1, source_target_pairs={{0,8},{4,12},{8,0},{12,4},{16,24},{20,28},{24,16},{28,20},{1,9},{5... | collective-permute-start | bytes 294920 | tf_op jit(solution)/shard_map/ppermute | solution.py:18
  71.6 0.9 collective-permute-start.29
  72.5 1.1 collective-permute-start.30
  73.9 1.1 collective-permute-done.28
  75.3 1.2 collective-permute-done.29
  76.9 1.1 collective-permute-done.30
  78.4 2.1 %collective-permute-start.33 = (bf16[384,128]{1,0:T(8,128)(2,1)S(1)}, bf16[384,128]{1,0:T(8,128)(2,1)S(1)}, u32[]{:S(2)}, u32[]{:S(2)}) collective-permute-start(bf16[384,128]{1,0:T(8,128)(2,1)S(1)} %get-tuple-element.38), channel_id=1, source_target_pairs={{0,3},{1,2},{2,1},{3,0},{4,7},{5,6},{6,5},{7,4},{8,11},{9,10},{10,... | collective-permute-start | bytes 294920 | tf_op jit(solution)/shard_map/ppermute | solution.py:18
  81.6 2.4 %collective-permute-start.31 = (bf16[384,128]{1,0:T(8,128)(2,1)S(1)}, bf16[384,128]{1,0:T(8,128)(2,1)S(1)}, u32[]{:S(2)}, u32[]{:S(2)}) collective-permute-start(bf16[384,128]{1,0:T(8,128)(2,1)S(1)} %slice.241), channel_id=1, source_target_pairs={{0,1},{1,0},{2,3},{3,2},{4,5},{5,4},{6,7},{7,6},{8,9},{9,8},{10,11... | collective-permute-start | bytes 294920 | tf_op jit(solution)/shard_map/ppermute | solution.py:18
  84.0 0.9 collective-permute-done.33
  85.0 2.5 %collective-permute-done.32 = bf16[384,128]{1,0:T(8,128)(2,1)S(1)} collective-permute-done((bf16[384,128]{1,0:T(8,128)(2,1)S(1)}, bf16[384,128]{1,0:T(8,128)(2,1)S(1)}, u32[]{:S(2)}, u32[]{:S(2)}) %collective-permute-start.32) | collective-permute-done | bytes 98336 | tf_op jit(solution)/shard_map/ppermute | solution.py:18
  88.1 1.4 %collective-permute-start.34 = (bf16[384,128]{1,0:T(8,128)(2,1)S(1)}, bf16[384,128]{1,0:T(8,128)(2,1)S(1)}, u32[]{:S(2)}, u32[]{:S(2)}) collective-permute-start(bf16[384,128]{1,0:T(8,128)(2,1)S(1)} %get-tuple-element.23), channel_id=1, source_target_pairs={{0,8},{4,12},{8,0},{12,4},{16,24},{20,28},{24,16},{28,20},{1,9},{5... | collective-permute-start | bytes 294920 | tf_op jit(solution)/shard_map/ppermute | solution.py:18
  90.3 1.3 collective-permute-start.36
  92.0 1.1 collective-permute-done.34
  94.6 1.3 collective-permute-done.36
  96.2 2.4 %collective-permute-start.39 = (bf16[384,128]{1,0:T(8,128)(2,1)S(1)}, bf16[384,128]{1,0:T(8,128)(2,1)S(1)}, u32[]{:S(2)}, u32[]{:S(2)}) collective-permute-start(bf16[384,128]{1,0:T(8,128)(2,1)S(1)} %get-tuple-element.36), channel_id=1, source_target_pairs={{0,3},{1,2},{2,1},{3,0},{4,7},{5,6},{6,5},{7,4},{8,11},{9,10},{10,... | collective-permute-start | bytes 294920 | tf_op jit(solution)/shard_map/ppermute | solution.py:18
  99.7 2.2 %collective-permute-start.37 = (bf16[384,128]{1,0:T(8,128)(2,1)S(1)}, bf16[384,128]{1,0:T(8,128)(2,1)S(1)}, u32[]{:S(2)}, u32[]{:S(2)}) collective-permute-start(bf16[384,128]{1,0:T(8,128)(2,1)S(1)} %slice.240), channel_id=1, source_target_pairs={{0,1},{1,0},{2,3},{3,2},{4,5},{5,4},{6,7},{7,6},{8,9},{9,8},{10,11... | collective-permute-start | bytes 294920 | tf_op jit(solution)/shard_map/ppermute | solution.py:18
  102.7 2.2 %collective-permute-done.38 = bf16[384,128]{1,0:T(8,128)(2,1)S(1)} collective-permute-done((bf16[384,128]{1,0:T(8,128)(2,1)S(1)}, bf16[384,128]{1,0:T(8,128)(2,1)S(1)}, u32[]{:S(2)}, u32[]{:S(2)}) %collective-permute-start.38) | collective-permute-done | bytes 98336 | tf_op jit(solution)/shard_map/ppermute | solution.py:18
  105.9 1.5 %collective-permute-start.40 = (bf16[384,128]{1,0:T(8,128)(2,1)S(1)}, bf16[384,128]{1,0:T(8,128)(2,1)S(1)}, u32[]{:S(2)}, u32[]{:S(2)}) collective-permute-start(bf16[384,128]{1,0:T(8,128)(2,1)S(1)} %get-tuple-element.21), channel_id=1, source_target_pairs={{0,8},{4,12},{8,0},{12,4},{16,24},{20,28},{24,16},{28,20},{1,9},{5... | collective-permute-start | bytes 294920 | tf_op jit(solution)/shard_map/ppermute | solution.py:18
  107.9 1.5 %collective-permute-start.42 = (bf16[384,128]{1,0:T(8,128)(2,1)S(1)}, bf16[384,128]{1,0:T(8,128)(2,1)S(1)}, u32[]{:S(2)}, u32[]{:S(2)}) collective-permute-start(bf16[384,128]{1,0:T(8,128)(2,1)S(1)} %get-tuple-element.21), channel_id=1, source_target_pairs={{0,24},{4,28},{8,16},{12,20},{16,8},{20,12},{24,0},{28,4},{1,25},{... | collective-permute-start | bytes 294920 | tf_op jit(solution)/shard_map/ppermute | solution.py:18
  110.9 1.1 collective-permute-done.41
  112.4 1.0 collective-permute-done.42
  113.8 2.3 %collective-permute-start.45 = (bf16[384,128]{1,0:T(8,128)(2,1)S(1)}, bf16[384,128]{1,0:T(8,128)(2,1)S(1)}, u32[]{:S(2)}, u32[]{:S(2)}) collective-permute-start(bf16[384,128]{1,0:T(8,128)(2,1)S(1)} %get-tuple-element.34), channel_id=1, source_target_pairs={{0,3},{1,2},{2,1},{3,0},{4,7},{5,6},{6,5},{7,4},{8,11},{9,10},{10,... | collective-permute-start | bytes 294920 | tf_op jit(solution)/shard_map/ppermute | solution.py:18
  117.4 2.1 %collective-permute-start.43 = (bf16[384,128]{1,0:T(8,128)(2,1)S(1)}, bf16[384,128]{1,0:T(8,128)(2,1)S(1)}, u32[]{:S(2)}, u32[]{:S(2)}) collective-permute-start(bf16[384,128]{1,0:T(8,128)(2,1)S(1)} %slice.239), channel_id=1, source_target_pairs={{0,1},{1,0},{2,3},{3,2},{4,5},{5,4},{6,7},{7,6},{8,9},{9,8},{10,11... | collective-permute-start | bytes 294920 | tf_op jit(solution)/shard_map/ppermute | solution.py:18
  120.3 2.2 %collective-permute-done.44 = bf16[384,128]{1,0:T(8,128)(2,1)S(1)} collective-permute-done((bf16[384,128]{1,0:T(8,128)(2,1)S(1)}, bf16[384,128]{1,0:T(8,128)(2,1)S(1)}, u32[]{:S(2)}, u32[]{:S(2)}) %collective-permute-start.44) | collective-permute-done | bytes 98336 | tf_op jit(solution)/shard_map/ppermute | solution.py:18
  123.5 1.4 %collective-permute-start.46 = (bf16[384,128]{1,0:T(8,128)(2,1)S(1)}, bf16[384,128]{1,0:T(8,128)(2,1)S(1)}, u32[]{:S(2)}, u32[]{:S(2)}) collective-permute-start(bf16[384,128]{1,0:T(8,128)(2,1)S(1)} %get-tuple-element.19), channel_id=1, source_target_pairs={{0,8},{4,12},{8,0},{12,4},{16,24},{20,28},{24,16},{28,20},{1,9},{5... | collective-permute-start | bytes 294920 | tf_op jit(solution)/shard_map/ppermute | solution.py:18
  125.8 1.3 collective-permute-start.48
  130.4 0.9 collective-permute-done.48
  131.7 2.3 %collective-permute-start.51 = (bf16[384,128]{1,0:T(8,128)(2,1)S(1)}, bf16[384,128]{1,0:T(8,128)(2,1)S(1)}, u32[]{:S(2)}, u32[]{:S(2)}) collective-permute-start(bf16[384,128]{1,0:T(8,128)(2,1)S(1)} %get-tuple-element.32), channel_id=1, source_target_pairs={{0,3},{1,2},{2,1},{3,0},{4,7},{5,6},{6,5},{7,4},{8,11},{9,10},{10,... | collective-permute-start | bytes 294920 | tf_op jit(solution)/shard_map/ppermute | solution.py:18
  134.5 2.1 %collective-permute-start.49 = (bf16[384,128]{1,0:T(8,128)(2,1)S(1)}, bf16[384,128]{1,0:T(8,128)(2,1)S(1)}, u32[]{:S(2)}, u32[]{:S(2)}) collective-permute-start(bf16[384,128]{1,0:T(8,128)(2,1)S(1)} %slice.238), channel_id=1, source_target_pairs={{0,1},{1,0},{2,3},{3,2},{4,5},{5,4},{6,7},{7,6},{8,9},{9,8},{10,11... | collective-permute-start | bytes 294920 | tf_op jit(solution)/shard_map/ppermute | solution.py:18
  136.6 1.6 %collective-permute-done.51 = bf16[384,128]{1,0:T(8,128)(2,1)S(1)} collective-permute-done((bf16[384,128]{1,0:T(8,128)(2,1)S(1)}, bf16[384,128]{1,0:T(8,128)(2,1)S(1)}, u32[]{:S(2)}, u32[]{:S(2)}) %collective-permute-start.51) | collective-permute-done | bytes 98336 | tf_op jit(solution)/shard_map/ppermute | solution.py:18
  138.2 2.1 %collective-permute-done.50 = bf16[384,128]{1,0:T(8,128)(2,1)S(1)} collective-permute-done((bf16[384,128]{1,0:T(8,128)(2,1)S(1)}, bf16[384,128]{1,0:T(8,128)(2,1)S(1)}, u32[]{:S(2)}, u32[]{:S(2)}) %collective-permute-start.50) | collective-permute-done | bytes 98336 | tf_op jit(solution)/shard_map/ppermute | solution.py:18
  140.4 1.3 collective-permute-done.52
  (174 shorter events, 35.3 us)
Async XLA Ops:
  0.0 3.6 %copy-start = (bf16[1,8,12,64,1,128]{5,3,4,2,1,0:T(8,128)(2,1)S(1)}, bf16[1,8,12,64,1,128]{5,3,4,2,1,0:T(8,128)(2,1)}, u32[]{:S(2)}) copy-start(bf16[1,8,12,64,1,128]{5,3,4,2,1,0:T(8,128)(2,1)} %param.7) | copy-start | bytes 4718596
  1.0 8.8 %collective-permute-start.2 = (bf16[192,128]{1,0:T(8,128)(2,1)S(1)}, bf16[192,128]{1,0:T(8,128)(2,1)S(1)}, u32[]{:S(2)}, u32[]{:S(2)}) collective-permute-start(bf16[192,128]{1,0:T(8,128)(2,1)S(1)} %get-tuple-element.44), channel_id=1, source_target_pairs={{0,4},{4,0},{8,12},{12,8},{16,20},{20,16},{24,28},{28,24},{1,5},{5... | collective-permute-start | bytes 147464 | tf_op jit(solution)/shard_map/ppermute | solution.py:18
  3.5 5.7 %collective-permute-start = (s32[192]{0:T(256)S(1)}, s32[192]{0:T(256)S(1)}, u32[]{:S(2)}, u32[]{:S(2)}) collective-permute-start(s32[192]{0:T(256)S(1)} %broadcast_select_fusion.2), channel_id=1, source_target_pairs={{0,4},{4,0},{8,12},{12,8},{16,20},{20,16},{24,28},{28,24},{1,5},{5... | collective-permute-start | bytes 2312 | tf_op jit(solution)/shard_map/ppermute | solution.py:18
  3.7 11.0 %collective-permute-start.14 = (bf16[2,384,128]{2,1,0:T(8,128)(2,1)S(1)}, bf16[2,384,128]{2,1,0:T(8,128)(2,1)S(1)}, u32[]{:S(2)}, u32[]{:S(2)}) collective-permute-start(bf16[2,384,128]{2,1,0:T(8,128)(2,1)S(1)} %constant_dynamic-slice_fusion.7), channel_id=1, source_target_pairs={{0,8},{4,12},{8,0},{12,4},{16,24},{20,28},{24,16},{28,20},{1,9},{5... | collective-permute-start | bytes 589832 | tf_op jit(solution)/shard_map/ppermute | solution.py:18
  7.3 10.9 %collective-permute-start.16 = (bf16[2,384,128]{2,1,0:T(8,128)(2,1)}, bf16[2,384,128]{2,1,0:T(8,128)(2,1)S(1)}, u32[]{:S(2)}, u32[]{:S(2)}) collective-permute-start(bf16[2,384,128]{2,1,0:T(8,128)(2,1)} %constant_dynamic-slice_fusion.6), channel_id=1, source_target_pairs={{0,16},{4,20},{8,24},{12,28},{16,0},{20,4},{24,8},{28,12},{1,17},{... | collective-permute-start | bytes 589832 | tf_op jit(solution)/shard_map/ppermute | solution.py:18
  8.9 1.5 %collective-permute-start.13 = (bf16[2,384,128]{2,1,0:T(8,128)(2,1)S(1)}, bf16[2,384,128]{2,1,0:T(8,128)(2,1)S(1)}, u32[]{:S(2)}, u32[]{:S(2)}) collective-permute-start(bf16[2,384,128]{2,1,0:T(8,128)(2,1)S(1)} %constant_dynamic-slice_fusion.4), channel_id=1, source_target_pairs={{0,4},{4,0},{8,12},{12,8},{16,20},{20,16},{24,28},{28,24},{1,5},{5... | collective-permute-start | bytes 589832 | tf_op jit(solution)/shard_map/ppermute | solution.py:18
  9.2 3.7 %collective-permute-start.1 = (bf16[2,384,128]{2,1,0:T(8,128)(2,1)S(1)}, bf16[2,384,128]{2,1,0:T(8,128)(2,1)S(1)}, u32[]{:S(2)}, u32[]{:S(2)}) collective-permute-start(bf16[2,384,128]{2,1,0:T(8,128)(2,1)S(1)} %constant_dynamic-slice_fusion), channel_id=1, source_target_pairs={{0,4},{4,0},{8,12},{12,8},{16,20},{20,16},{24,28},{28,24},{1,5},{5... | collective-permute-start | bytes 589832 | tf_op jit(solution)/shard_map/ppermute | solution.py:18
  9.8 24.1 %collective-permute-start.18 = (bf16[2,384,128]{2,1,0:T(8,128)(2,1)S(1)}, bf16[2,384,128]{2,1,0:T(8,128)(2,1)S(1)}, u32[]{:S(2)}, u32[]{:S(2)}) collective-permute-start(bf16[2,384,128]{2,1,0:T(8,128)(2,1)S(1)} %constant_dynamic-slice_fusion.5), channel_id=1, source_target_pairs={{0,24},{4,28},{8,16},{12,20},{16,8},{20,12},{24,0},{28,4},{1,25},{... | collective-permute-start | bytes 589832 | tf_op jit(solution)/shard_map/ppermute | solution.py:18
  10.4 23.5 %collective-permute-start.3 = (bf16[2,384,128]{2,1,0:T(8,128)(2,1)S(1)}, bf16[2,384,128]{2,1,0:T(8,128)(2,1)S(1)}, u32[]{:S(2)}, u32[]{:S(2)}) collective-permute-start(bf16[2,384,128]{2,1,0:T(8,128)(2,1)S(1)} %constant_dynamic-slice_fusion.3), channel_id=1, source_target_pairs={{0,8},{4,12},{8,0},{12,4},{16,24},{20,28},{24,16},{28,20},{1,9},{5... | collective-permute-start | bytes 589832 | tf_op jit(solution)/shard_map/ppermute | solution.py:18
  12.9 10.0 %collective-permute-start.5 = (bf16[384,128]{1,0:T(8,128)(2,1)S(1)}, bf16[384,128]{1,0:T(8,128)(2,1)S(1)}, u32[]{:S(2)}, u32[]{:S(2)}) collective-permute-start(bf16[384,128]{1,0:T(8,128)(2,1)S(1)} %pad_maximum_fusion), channel_id=1, source_target_pairs={{0,8},{4,12},{8,0},{12,4},{16,24},{20,28},{24,16},{28,20},{1,9},{5... | collective-permute-start | bytes 294920 | tf_op jit(solution)/shard_map/ppermute | solution.py:18
  14.7 3.9 %collective-permute-start.15 = (bf16[2,384,128]{2,1,0:T(8,128)(2,1)S(1)}, bf16[2,384,128]{2,1,0:T(8,128)(2,1)S(1)}, u32[]{:S(2)}, u32[]{:S(2)}) collective-permute-start(bf16[2,384,128]{2,1,0:T(8,128)(2,1)S(1)} %collective-permute-done.14), channel_id=1, source_target_pairs={{0,4},{4,0},{8,12},{12,8},{16,20},{20,16},{24,28},{28,24},{1,5},{5... | collective-permute-start | bytes 589832 | tf_op jit(solution)/shard_map/ppermute | solution.py:18
  18.2 6.8 %collective-permute-start.17 = (bf16[2,384,128]{2,1,0:T(8,128)(2,1)S(1)}, bf16[2,384,128]{2,1,0:T(8,128)(2,1)S(1)}, u32[]{:S(2)}, u32[]{:S(2)}) collective-permute-start(bf16[2,384,128]{2,1,0:T(8,128)(2,1)S(1)} %collective-permute-done.16), channel_id=1, source_target_pairs={{0,4},{4,0},{8,12},{12,8},{16,20},{20,16},{24,28},{28,24},{1,5},{5... | collective-permute-start | bytes 589832 | tf_op jit(solution)/shard_map/ppermute | solution.py:18
  18.5 15.9 %collective-permute-start.6 = (bf16[2,384,128]{2,1,0:T(8,128)(2,1)S(1)}, bf16[2,384,128]{2,1,0:T(8,128)(2,1)S(1)}, u32[]{:S(2)}, u32[]{:S(2)}) collective-permute-start(bf16[2,384,128]{2,1,0:T(8,128)(2,1)S(1)} %constant_dynamic-slice_fusion.2), channel_id=1, source_target_pairs={{0,16},{4,20},{8,24},{12,28},{16,0},{20,4},{24,8},{28,12},{1,17},{... | collective-permute-start | bytes 589832 | tf_op jit(solution)/shard_map/ppermute | solution.py:18
  22.9 11.5 %collective-permute-start.9 = (bf16[2,384,128]{2,1,0:T(8,128)(2,1)S(1)}, bf16[2,384,128]{2,1,0:T(8,128)(2,1)S(1)}, u32[]{:S(2)}, u32[]{:S(2)}) collective-permute-start(bf16[2,384,128]{2,1,0:T(8,128)(2,1)S(1)} %constant_dynamic-slice_fusion.1), channel_id=1, source_target_pairs={{0,24},{4,28},{8,16},{12,20},{16,8},{20,12},{24,0},{28,4},{1,25},{... | collective-permute-start | bytes 589832 | tf_op jit(solution)/shard_map/ppermute | solution.py:18
  25.0 7.2 %collective-permute-start.8 = (bf16[384,128]{1,0:T(8,128)(2,1)S(1)}, bf16[384,128]{1,0:T(8,128)(2,1)S(1)}, u32[]{:S(2)}, u32[]{:S(2)}) collective-permute-start(bf16[384,128]{1,0:T(8,128)(2,1)S(1)} %pad_maximum_fusion), channel_id=1, source_target_pairs={{0,16},{4,20},{8,24},{12,28},{16,0},{20,4},{24,8},{28,12},{1,17},{... | collective-permute-start | bytes 294920 | tf_op jit(solution)/shard_map/ppermute | solution.py:18
  32.2 5.5 %collective-permute-start.11 = (bf16[384,128]{1,0:T(8,128)(2,1)S(1)}, bf16[384,128]{1,0:T(8,128)(2,1)S(1)}, u32[]{:S(2)}, u32[]{:S(2)}) collective-permute-start(bf16[384,128]{1,0:T(8,128)(2,1)S(1)} %pad_maximum_fusion), channel_id=1, source_target_pairs={{0,24},{4,28},{8,16},{12,20},{16,8},{20,12},{24,0},{28,4},{1,25},{... | collective-permute-start | bytes 294920 | tf_op jit(solution)/shard_map/ppermute | solution.py:18
  33.9 1.5 %collective-permute-start.19 = (bf16[2,384,128]{2,1,0:T(8,128)(2,1)S(1)}, bf16[2,384,128]{2,1,0:T(8,128)(2,1)S(1)}, u32[]{:S(2)}, u32[]{:S(2)}) collective-permute-start(bf16[2,384,128]{2,1,0:T(8,128)(2,1)S(1)} %collective-permute-done.18), channel_id=1, source_target_pairs={{0,4},{4,0},{8,12},{12,8},{16,20},{20,16},{24,28},{28,24},{1,5},{5... | collective-permute-start | bytes 589832 | tf_op jit(solution)/shard_map/ppermute | solution.py:18
  33.9 7.9 %collective-permute-start.4 = (bf16[2,384,128]{2,1,0:T(8,128)(2,1)S(1)}, bf16[2,384,128]{2,1,0:T(8,128)(2,1)S(1)}, u32[]{:S(2)}, u32[]{:S(2)}) collective-permute-start(bf16[2,384,128]{2,1,0:T(8,128)(2,1)S(1)} %collective-permute-done.3), channel_id=1, source_target_pairs={{0,4},{4,0},{8,12},{12,8},{16,20},{20,16},{24,28},{28,24},{1,5},{5... | collective-permute-start | bytes 589832 | tf_op jit(solution)/shard_map/ppermute | solution.py:18
  34.4 8.9 %collective-permute-start.7 = (bf16[2,384,128]{2,1,0:T(8,128)(2,1)S(1)}, bf16[2,384,128]{2,1,0:T(8,128)(2,1)S(1)}, u32[]{:S(2)}, u32[]{:S(2)}) collective-permute-start(bf16[2,384,128]{2,1,0:T(8,128)(2,1)S(1)} %collective-permute-done.6), channel_id=1, source_target_pairs={{0,4},{4,0},{8,12},{12,8},{16,20},{20,16},{24,28},{28,24},{1,5},{5... | collective-permute-start | bytes 589832 | tf_op jit(solution)/shard_map/ppermute | solution.py:18
  34.5 10.3 %collective-permute-start.10 = (bf16[2,384,128]{2,1,0:T(8,128)(2,1)S(1)}, bf16[2,384,128]{2,1,0:T(8,128)(2,1)S(1)}, u32[]{:S(2)}, u32[]{:S(2)}) collective-permute-start(bf16[2,384,128]{2,1,0:T(8,128)(2,1)S(1)} %collective-permute-done.9), channel_id=1, source_target_pairs={{0,4},{4,0},{8,12},{12,8},{16,20},{20,16},{24,28},{28,24},{1,5},{5... | collective-permute-start | bytes 589832 | tf_op jit(solution)/shard_map/ppermute | solution.py:18
  38.2 10.4 %collective-permute-start.21 = (bf16[384,128]{1,0:T(8,128)(2,1)S(1)}, bf16[384,128]{1,0:T(8,128)(2,1)S(1)}, u32[]{:S(2)}, u32[]{:S(2)}) collective-permute-start(bf16[384,128]{1,0:T(8,128)(2,1)S(1)} %get-tuple-element.42), channel_id=1, source_target_pairs={{0,3},{1,2},{2,1},{3,0},{4,7},{5,6},{6,5},{7,4},{8,11},{9,10},{10,... | collective-permute-start | bytes 294920 | tf_op jit(solution)/shard_map/ppermute | solution.py:18
  41.8 7.6 %collective-permute-start.20 = (bf16[384,128]{1,0:T(8,128)(2,1)S(1)}, bf16[384,128]{1,0:T(8,128)(2,1)S(1)}, u32[]{:S(2)}, u32[]{:S(2)}) collective-permute-start(bf16[384,128]{1,0:T(8,128)(2,1)S(1)} %get-tuple-element.41), channel_id=1, source_target_pairs={{0,2},{1,3},{2,0},{3,1},{4,6},{5,7},{6,4},{7,5},{8,10},{9,11},{10,... | collective-permute-start | bytes 294920 | tf_op jit(solution)/shard_map/ppermute | solution.py:18
  46.4 4.9 %collective-permute-start.12 = (bf16[384,128]{1,0:T(8,128)(2,1)S(1)}, bf16[384,128]{1,0:T(8,128)(2,1)S(1)}, u32[]{:S(2)}, u32[]{:S(2)}) collective-permute-start(bf16[384,128]{1,0:T(8,128)(2,1)S(1)} %slice.243), channel_id=1, source_target_pairs={{0,1},{1,0},{2,3},{3,2},{4,5},{5,4},{6,7},{7,6},{8,9},{9,8},{10,11... | collective-permute-start | bytes 294920 | tf_op jit(solution)/shard_map/ppermute | solution.py:18
  51.7 5.1 %collective-permute-start.22 = (bf16[384,128]{1,0:T(8,128)(2,1)S(1)}, bf16[384,128]{1,0:T(8,128)(2,1)S(1)}, u32[]{:S(2)}, u32[]{:S(2)}) collective-permute-start(bf16[384,128]{1,0:T(8,128)(2,1)S(1)} %get-tuple-element.27), channel_id=1, source_target_pairs={{0,8},{4,12},{8,0},{12,4},{16,24},{20,28},{24,16},{28,20},{1,9},{5... | collective-permute-start | bytes 294920 | tf_op jit(solution)/shard_map/ppermute | solution.py:18
  53.1 4.9 %collective-permute-start.23 = (bf16[384,128]{1,0:T(8,128)(2,1)S(1)}, bf16[384,128]{1,0:T(8,128)(2,1)S(1)}, u32[]{:S(2)}, u32[]{:S(2)}) collective-permute-start(bf16[384,128]{1,0:T(8,128)(2,1)S(1)} %get-tuple-element.27), channel_id=1, source_target_pairs={{0,16},{4,20},{8,24},{12,28},{16,0},{20,4},{24,8},{28,12},{1,17},{... | collective-permute-start | bytes 294920 | tf_op jit(solution)/shard_map/ppermute | solution.py:18
  53.8 5.5 %collective-permute-start.24 = (bf16[384,128]{1,0:T(8,128)(2,1)S(1)}, bf16[384,128]{1,0:T(8,128)(2,1)S(1)}, u32[]{:S(2)}, u32[]{:S(2)}) collective-permute-start(bf16[384,128]{1,0:T(8,128)(2,1)S(1)} %get-tuple-element.27), channel_id=1, source_target_pairs={{0,24},{4,28},{8,16},{12,20},{16,8},{20,12},{24,0},{28,4},{1,25},{... | collective-permute-start | bytes 294920 | tf_op jit(solution)/shard_map/ppermute | solution.py:18
  59.7 7.3 %collective-permute-start.27 = (bf16[384,128]{1,0:T(8,128)(2,1)S(1)}, bf16[384,128]{1,0:T(8,128)(2,1)S(1)}, u32[]{:S(2)}, u32[]{:S(2)}) collective-permute-start(bf16[384,128]{1,0:T(8,128)(2,1)S(1)} %get-tuple-element.40), channel_id=1, source_target_pairs={{0,3},{1,2},{2,1},{3,0},{4,7},{5,6},{6,5},{7,4},{8,11},{9,10},{10,... | collective-permute-start | bytes 294920 | tf_op jit(solution)/shard_map/ppermute | solution.py:18
  62.1 7.3 %collective-permute-start.26 = (bf16[384,128]{1,0:T(8,128)(2,1)S(1)}, bf16[384,128]{1,0:T(8,128)(2,1)S(1)}, u32[]{:S(2)}, u32[]{:S(2)}) collective-permute-start(bf16[384,128]{1,0:T(8,128)(2,1)S(1)} %get-tuple-element.39), channel_id=1, source_target_pairs={{0,2},{1,3},{2,0},{3,1},{4,6},{5,7},{6,4},{7,5},{8,10},{9,11},{10,... | collective-permute-start | bytes 294920 | tf_op jit(solution)/shard_map/ppermute | solution.py:18
  63.9 5.7 %collective-permute-start.25 = (bf16[384,128]{1,0:T(8,128)(2,1)S(1)}, bf16[384,128]{1,0:T(8,128)(2,1)S(1)}, u32[]{:S(2)}, u32[]{:S(2)}) collective-permute-start(bf16[384,128]{1,0:T(8,128)(2,1)S(1)} %slice.242), channel_id=1, source_target_pairs={{0,1},{1,0},{2,3},{3,2},{4,5},{5,4},{6,7},{7,6},{8,9},{9,8},{10,11... | collective-permute-start | bytes 294920 | tf_op jit(solution)/shard_map/ppermute | solution.py:18
  70.0 5.0 %collective-permute-start.28 = (bf16[384,128]{1,0:T(8,128)(2,1)S(1)}, bf16[384,128]{1,0:T(8,128)(2,1)S(1)}, u32[]{:S(2)}, u32[]{:S(2)}) collective-permute-start(bf16[384,128]{1,0:T(8,128)(2,1)S(1)} %get-tuple-element.25), channel_id=1, source_target_pairs={{0,8},{4,12},{8,0},{12,4},{16,24},{20,28},{24,16},{28,20},{1,9},{5... | collective-permute-start | bytes 294920 | tf_op jit(solution)/shard_map/ppermute | solution.py:18
  71.6 4.9 %collective-permute-start.29 = (bf16[384,128]{1,0:T(8,128)(2,1)S(1)}, bf16[384,128]{1,0:T(8,128)(2,1)S(1)}, u32[]{:S(2)}, u32[]{:S(2)}) collective-permute-start(bf16[384,128]{1,0:T(8,128)(2,1)S(1)} %get-tuple-element.25), channel_id=1, source_target_pairs={{0,16},{4,20},{8,24},{12,28},{16,0},{20,4},{24,8},{28,12},{1,17},{... | collective-permute-start | bytes 294920 | tf_op jit(solution)/shard_map/ppermute | solution.py:18
  72.5 5.5 %collective-permute-start.30 = (bf16[384,128]{1,0:T(8,128)(2,1)S(1)}, bf16[384,128]{1,0:T(8,128)(2,1)S(1)}, u32[]{:S(2)}, u32[]{:S(2)}) collective-permute-start(bf16[384,128]{1,0:T(8,128)(2,1)S(1)} %get-tuple-element.25), channel_id=1, source_target_pairs={{0,24},{4,28},{8,16},{12,20},{16,8},{20,12},{24,0},{28,4},{1,25},{... | collective-permute-start | bytes 294920 | tf_op jit(solution)/shard_map/ppermute | solution.py:18
  78.4 6.6 %collective-permute-start.33 = (bf16[384,128]{1,0:T(8,128)(2,1)S(1)}, bf16[384,128]{1,0:T(8,128)(2,1)S(1)}, u32[]{:S(2)}, u32[]{:S(2)}) collective-permute-start(bf16[384,128]{1,0:T(8,128)(2,1)S(1)} %get-tuple-element.38), channel_id=1, source_target_pairs={{0,3},{1,2},{2,1},{3,0},{4,7},{5,6},{6,5},{7,4},{8,11},{9,10},{10,... | collective-permute-start | bytes 294920 | tf_op jit(solution)/shard_map/ppermute | solution.py:18
  80.5 7.0 %collective-permute-start.32 = (bf16[384,128]{1,0:T(8,128)(2,1)S(1)}, bf16[384,128]{1,0:T(8,128)(2,1)S(1)}, u32[]{:S(2)}, u32[]{:S(2)}) collective-permute-start(bf16[384,128]{1,0:T(8,128)(2,1)S(1)} %get-tuple-element.37), channel_id=1, source_target_pairs={{0,2},{1,3},{2,0},{3,1},{4,6},{5,7},{6,4},{7,5},{8,10},{9,11},{10,... | collective-permute-start | bytes 294920 | tf_op jit(solution)/shard_map/ppermute | solution.py:18
  81.6 6.0 %collective-permute-start.31 = (bf16[384,128]{1,0:T(8,128)(2,1)S(1)}, bf16[384,128]{1,0:T(8,128)(2,1)S(1)}, u32[]{:S(2)}, u32[]{:S(2)}) collective-permute-start(bf16[384,128]{1,0:T(8,128)(2,1)S(1)} %slice.241), channel_id=1, source_target_pairs={{0,1},{1,0},{2,3},{3,2},{4,5},{5,4},{6,7},{7,6},{8,9},{9,8},{10,11... | collective-permute-start | bytes 294920 | tf_op jit(solution)/shard_map/ppermute | solution.py:18
  88.1 4.9 %collective-permute-start.34 = (bf16[384,128]{1,0:T(8,128)(2,1)S(1)}, bf16[384,128]{1,0:T(8,128)(2,1)S(1)}, u32[]{:S(2)}, u32[]{:S(2)}) collective-permute-start(bf16[384,128]{1,0:T(8,128)(2,1)S(1)} %get-tuple-element.23), channel_id=1, source_target_pairs={{0,8},{4,12},{8,0},{12,4},{16,24},{20,28},{24,16},{28,20},{1,9},{5... | collective-permute-start | bytes 294920 | tf_op jit(solution)/shard_map/ppermute | solution.py:18
  89.5 4.6 %collective-permute-start.35 = (bf16[384,128]{1,0:T(8,128)(2,1)S(1)}, bf16[384,128]{1,0:T(8,128)(2,1)S(1)}, u32[]{:S(2)}, u32[]{:S(2)}) collective-permute-start(bf16[384,128]{1,0:T(8,128)(2,1)S(1)} %get-tuple-element.23), channel_id=1, source_target_pairs={{0,16},{4,20},{8,24},{12,28},{16,0},{20,4},{24,8},{28,12},{1,17},{... | collective-permute-start | bytes 294920 | tf_op jit(solution)/shard_map/ppermute | solution.py:18
  90.3 5.5 %collective-permute-start.36 = (bf16[384,128]{1,0:T(8,128)(2,1)S(1)}, bf16[384,128]{1,0:T(8,128)(2,1)S(1)}, u32[]{:S(2)}, u32[]{:S(2)}) collective-permute-start(bf16[384,128]{1,0:T(8,128)(2,1)S(1)} %get-tuple-element.23), channel_id=1, source_target_pairs={{0,24},{4,28},{8,16},{12,20},{16,8},{20,12},{24,0},{28,4},{1,25},{... | collective-permute-start | bytes 294920 | tf_op jit(solution)/shard_map/ppermute | solution.py:18
  96.2 6.5 %collective-permute-start.39 = (bf16[384,128]{1,0:T(8,128)(2,1)S(1)}, bf16[384,128]{1,0:T(8,128)(2,1)S(1)}, u32[]{:S(2)}, u32[]{:S(2)}) collective-permute-start(bf16[384,128]{1,0:T(8,128)(2,1)S(1)} %get-tuple-element.36), channel_id=1, source_target_pairs={{0,3},{1,2},{2,1},{3,0},{4,7},{5,6},{6,5},{7,4},{8,11},{9,10},{10,... | collective-permute-start | bytes 294920 | tf_op jit(solution)/shard_map/ppermute | solution.py:18
  98.6 6.3 %collective-permute-start.38 = (bf16[384,128]{1,0:T(8,128)(2,1)S(1)}, bf16[384,128]{1,0:T(8,128)(2,1)S(1)}, u32[]{:S(2)}, u32[]{:S(2)}) collective-permute-start(bf16[384,128]{1,0:T(8,128)(2,1)S(1)} %get-tuple-element.35), channel_id=1, source_target_pairs={{0,2},{1,3},{2,0},{3,1},{4,6},{5,7},{6,4},{7,5},{8,10},{9,11},{10,... | collective-permute-start | bytes 294920 | tf_op jit(solution)/shard_map/ppermute | solution.py:18
  99.7 5.8 %collective-permute-start.37 = (bf16[384,128]{1,0:T(8,128)(2,1)S(1)}, bf16[384,128]{1,0:T(8,128)(2,1)S(1)}, u32[]{:S(2)}, u32[]{:S(2)}) collective-permute-start(bf16[384,128]{1,0:T(8,128)(2,1)S(1)} %slice.240), channel_id=1, source_target_pairs={{0,1},{1,0},{2,3},{3,2},{4,5},{5,4},{6,7},{7,6},{8,9},{9,8},{10,11... | collective-permute-start | bytes 294920 | tf_op jit(solution)/shard_map/ppermute | solution.py:18
  105.9 4.7 %collective-permute-start.40 = (bf16[384,128]{1,0:T(8,128)(2,1)S(1)}, bf16[384,128]{1,0:T(8,128)(2,1)S(1)}, u32[]{:S(2)}, u32[]{:S(2)}) collective-permute-start(bf16[384,128]{1,0:T(8,128)(2,1)S(1)} %get-tuple-element.21), channel_id=1, source_target_pairs={{0,8},{4,12},{8,0},{12,4},{16,24},{20,28},{24,16},{28,20},{1,9},{5... | collective-permute-start | bytes 294920 | tf_op jit(solution)/shard_map/ppermute | solution.py:18
  107.4 4.6 %collective-permute-start.41 = (bf16[384,128]{1,0:T(8,128)(2,1)S(1)}, bf16[384,128]{1,0:T(8,128)(2,1)S(1)}, u32[]{:S(2)}, u32[]{:S(2)}) collective-permute-start(bf16[384,128]{1,0:T(8,128)(2,1)S(1)} %get-tuple-element.21), channel_id=1, source_target_pairs={{0,16},{4,20},{8,24},{12,28},{16,0},{20,4},{24,8},{28,12},{1,17},{... | collective-permute-start | bytes 294920 | tf_op jit(solution)/shard_map/ppermute | solution.py:18
  107.9 5.5 %collective-permute-start.42 = (bf16[384,128]{1,0:T(8,128)(2,1)S(1)}, bf16[384,128]{1,0:T(8,128)(2,1)S(1)}, u32[]{:S(2)}, u32[]{:S(2)}) collective-permute-start(bf16[384,128]{1,0:T(8,128)(2,1)S(1)} %get-tuple-element.21), channel_id=1, source_target_pairs={{0,24},{4,28},{8,16},{12,20},{16,8},{20,12},{24,0},{28,4},{1,25},{... | collective-permute-start | bytes 294920 | tf_op jit(solution)/shard_map/ppermute | solution.py:18
  113.8 6.5 %collective-permute-start.45 = (bf16[384,128]{1,0:T(8,128)(2,1)S(1)}, bf16[384,128]{1,0:T(8,128)(2,1)S(1)}, u32[]{:S(2)}, u32[]{:S(2)}) collective-permute-start(bf16[384,128]{1,0:T(8,128)(2,1)S(1)} %get-tuple-element.34), channel_id=1, source_target_pairs={{0,3},{1,2},{2,1},{3,0},{4,7},{5,6},{6,5},{7,4},{8,11},{9,10},{10,... | collective-permute-start | bytes 294920 | tf_op jit(solution)/shard_map/ppermute | solution.py:18
  116.2 6.4 %collective-permute-start.44 = (bf16[384,128]{1,0:T(8,128)(2,1)S(1)}, bf16[384,128]{1,0:T(8,128)(2,1)S(1)}, u32[]{:S(2)}, u32[]{:S(2)}) collective-permute-start(bf16[384,128]{1,0:T(8,128)(2,1)S(1)} %get-tuple-element.33), channel_id=1, source_target_pairs={{0,2},{1,3},{2,0},{3,1},{4,6},{5,7},{6,4},{7,5},{8,10},{9,11},{10,... | collective-permute-start | bytes 294920 | tf_op jit(solution)/shard_map/ppermute | solution.py:18
  117.4 5.7 %collective-permute-start.43 = (bf16[384,128]{1,0:T(8,128)(2,1)S(1)}, bf16[384,128]{1,0:T(8,128)(2,1)S(1)}, u32[]{:S(2)}, u32[]{:S(2)}) collective-permute-start(bf16[384,128]{1,0:T(8,128)(2,1)S(1)} %slice.239), channel_id=1, source_target_pairs={{0,1},{1,0},{2,3},{3,2},{4,5},{5,4},{6,7},{7,6},{8,9},{9,8},{10,11... | collective-permute-start | bytes 294920 | tf_op jit(solution)/shard_map/ppermute | solution.py:18
  123.5 4.7 %collective-permute-start.46 = (bf16[384,128]{1,0:T(8,128)(2,1)S(1)}, bf16[384,128]{1,0:T(8,128)(2,1)S(1)}, u32[]{:S(2)}, u32[]{:S(2)}) collective-permute-start(bf16[384,128]{1,0:T(8,128)(2,1)S(1)} %get-tuple-element.19), channel_id=1, source_target_pairs={{0,8},{4,12},{8,0},{12,4},{16,24},{20,28},{24,16},{28,20},{1,9},{5... | collective-permute-start | bytes 294920 | tf_op jit(solution)/shard_map/ppermute | solution.py:18
  125.0 4.6 %collective-permute-start.47 = (bf16[384,128]{1,0:T(8,128)(2,1)S(1)}, bf16[384,128]{1,0:T(8,128)(2,1)S(1)}, u32[]{:S(2)}, u32[]{:S(2)}) collective-permute-start(bf16[384,128]{1,0:T(8,128)(2,1)S(1)} %get-tuple-element.19), channel_id=1, source_target_pairs={{0,16},{4,20},{8,24},{12,28},{16,0},{20,4},{24,8},{28,12},{1,17},{... | collective-permute-start | bytes 294920 | tf_op jit(solution)/shard_map/ppermute | solution.py:18
  125.8 5.5 %collective-permute-start.48 = (bf16[384,128]{1,0:T(8,128)(2,1)S(1)}, bf16[384,128]{1,0:T(8,128)(2,1)S(1)}, u32[]{:S(2)}, u32[]{:S(2)}) collective-permute-start(bf16[384,128]{1,0:T(8,128)(2,1)S(1)} %get-tuple-element.19), channel_id=1, source_target_pairs={{0,24},{4,28},{8,16},{12,20},{16,8},{20,12},{24,0},{28,4},{1,25},{... | collective-permute-start | bytes 294920 | tf_op jit(solution)/shard_map/ppermute | solution.py:18
  131.7 6.5 %collective-permute-start.51 = (bf16[384,128]{1,0:T(8,128)(2,1)S(1)}, bf16[384,128]{1,0:T(8,128)(2,1)S(1)}, u32[]{:S(2)}, u32[]{:S(2)}) collective-permute-start(bf16[384,128]{1,0:T(8,128)(2,1)S(1)} %get-tuple-element.32), channel_id=1, source_target_pairs={{0,3},{1,2},{2,1},{3,0},{4,7},{5,6},{6,5},{7,4},{8,11},{9,10},{10,... | collective-permute-start | bytes 294920 | tf_op jit(solution)/shard_map/ppermute | solution.py:18
  134.0 6.3 %collective-permute-start.50 = (bf16[384,128]{1,0:T(8,128)(2,1)S(1)}, bf16[384,128]{1,0:T(8,128)(2,1)S(1)}, u32[]{:S(2)}, u32[]{:S(2)}) collective-permute-start(bf16[384,128]{1,0:T(8,128)(2,1)S(1)} %get-tuple-element.31), channel_id=1, source_target_pairs={{0,2},{1,3},{2,0},{3,1},{4,6},{5,7},{6,4},{7,5},{8,10},{9,11},{10,... | collective-permute-start | bytes 294920 | tf_op jit(solution)/shard_map/ppermute | solution.py:18
  134.5 5.8 %collective-permute-start.49 = (bf16[384,128]{1,0:T(8,128)(2,1)S(1)}, bf16[384,128]{1,0:T(8,128)(2,1)S(1)}, u32[]{:S(2)}, u32[]{:S(2)}) collective-permute-start(bf16[384,128]{1,0:T(8,128)(2,1)S(1)} %slice.238), channel_id=1, source_target_pairs={{0,1},{1,0},{2,3},{3,2},{4,5},{5,4},{6,7},{7,6},{8,9},{9,8},{10,11... | collective-permute-start | bytes 294920 | tf_op jit(solution)/shard_map/ppermute | solution.py:18
  140.4 1.4 collective-permute-start.52

commit v4 on v3

v4 whole, which is shorter than its diff:
```python
import functools

import jax
import jax.numpy as jnp
from jax import lax
from jax.experimental import pallas as pl
from jax.experimental.pallas import tpu as pltpu
from jax.sharding import PartitionSpec as P


DEGREE = 6
PAIR = 2
SLOTS = 2
UNROLL = 3


def exchange(value, axis, size, offset):
    return lax.ppermute(value, axis, [(i, i ^ offset) for i in range(size)])


def place_blocks(chips, per, width, half, pieces, sources, place, used, *refs):
    same, other, dense = refs[:chips], refs[chips : 2 * chips], refs[2 * chips :]
    chip, core, piece = place[0], place[1], place[2]
    lane = lax.broadcasted_iota(jnp.int32, (1, SLOTS * width), 1) < width
    held = pieces // 2
    count = dense[0].shape[0] // (held * PAIR * width)
    halves = [(far, column) for far in range(PAIR) for column in range(per)]

    def block_row(index, carry):
        row = lax.rem(index, count)
        near = lax.rem(index // count, PAIR)
        at = (piece ^ (index // (count * PAIR))) & (held - 1)
        base = (near * pieces + (at | (((piece // held) ^ half) * held))) * count + row
        source_row = pl.multiple_of(((core ^ near) * held + at) * count * width + row * width, width)
        target = pl.multiple_of(index * width, width)
        for step in range(chips):
            sides = []
            for far, ref in enumerate((same[step], other[step])):
                value = ref[pl.ds(source_row, width), :]
                source = PAIR * (chip ^ step) + (core ^ far)
                slots = [used[(base * sources + source) * SLOTS + slot] for slot in range(SLOTS)]
                sides.append((value, pltpu.roll(value, width, 1), slots))
            for tile in range(len(halves) // 2):
                (far_a, col_a), (far_b, col_b) = halves[2 * tile], halves[2 * tile + 1]
                terms = {}
                for far, turned, wanted, left in (
                    (far_a, 0, sides[far_a][2][0] == col_a, True),
                    (far_a, 1, sides[far_a][2][1] == col_a, True),
                    (far_b, 0, sides[far_b][2][1] == col_b, False),
                    (far_b, 1, sides[far_b][2][0] == col_b, False),
                ):
                    terms.setdefault((far, turned), {})[left] = wanted.astype(jnp.int32)
                result = None
                for (far, turned), wanted in terms.items():
                    factor = jnp.where(lane, wanted.get(True, 0), wanted.get(False, 0))
                    term = sides[far][turned] * factor.astype(jnp.float32).astype(dense[step].dtype)
                    result = term if result is None else result + term
                columns = pl.ds(tile * SLOTS * width, SLOTS * width)
                dense[step][pl.ds(target, width), columns] = result
        return carry

    lax.fori_loop(0, held * PAIR * count, block_row, 0, unroll=UNROLL)


def filter_body(per, trial_vectors, h_blocks, block_col, block_count, center, half_width):
    row_count = lax.axis_size("row")
    col_count = lax.axis_size("col")
    chips = row_count // PAIR
    row_index = lax.axis_index("row")
    chip, core = row_index // PAIR, row_index % PAIR
    piece = lax.axis_index("col")
    domain = h_blocks.shape[2]
    width = h_blocks.shape[3]
    slots = h_blocks.shape[5] // width
    vectors = trial_vectors.shape[1] // PAIR

    raw = h_blocks.reshape(row_count, domain * width, slots * width)
    used = jnp.where(
        lax.broadcasted_iota(jnp.int32, block_col.shape[2:], 2) < block_count[0, 0][:, :, None],
        block_col[0, 0],
        -1,
    ).reshape(-1)
    used = jnp.concatenate([used, exchange(used, "row", row_count, 1)])

    place = jnp.stack([chip, core, piece]).astype(jnp.int32)
    held = col_count // 2
    part = domain * width // 2
    columns = PAIR * per * width
    scalars = pl.BlockSpec(memory_space=pltpu.SMEM)
    vectors_spec = pl.BlockSpec(memory_space=pltpu.VMEM)
    order = gather_order(chips)
    first = trial_vectors[:, :vectors]
    second = trial_vectors[:, vectors:]
    mine = jnp.where(core == 0, first, second)
    theirs = exchange(jnp.where(core == 0, second, first), "row", row_count, 1)
    panel = jnp.concatenate([mine, theirs])
    sends = {}
    last = None
    for half in (1, 0):
        top = (piece // held) ^ half
        for step in (*order, 0):
            at = PAIR * (chip ^ step)
            if last is not None:
                at, _ = lax.optimization_barrier((at, last))
            last = lax.dynamic_slice(raw, (at, top * part, 0), (PAIR, part, slots * width))
            sends[half, step] = last.reshape(PAIR * part, slots * width)
    matrices = [None, None]
    for half in (1, 0):
        same, other = [], []
        for step in range(chips):
            sent = sends[half, step]
            same.append(sent if step == 0 else exchange(sent, "row", row_count, PAIR * step))
            other.append(exchange(same[step], "row", row_count, 1))
        matrices[half] = pl.pallas_call(
            functools.partial(place_blocks, chips, per, width, half, col_count, row_count),
            out_shape=[jax.ShapeDtypeStruct((PAIR * part, columns), jnp.bfloat16)] * chips,
            in_specs=[scalars, scalars] + [vectors_spec] * (2 * chips),
            out_specs=[vectors_spec] * chips,
            cost_estimate=pl.CostEstimate(
                flops=PAIR * part * columns * 3 * chips,
                bytes_accessed=PAIR * part * columns * 4 * chips,
                transcendentals=0,
            ),
            compiler_params=pltpu.CompilerParams(
                vmem_limit_bytes=chips * PAIR * part * (columns + 2 * slots * width) * 4 + (1 << 20)
            ),
        )(place, used, *same, *other)

    centre_value = center[0]
    half_value = half_width[0]
    rows = domain * width // col_count
    span = PAIR * rows

    def operator(current):
        arrived = [current]
        for step in range(1, chips):
            arrived.append(exchange(current, "row", row_count, PAIR * step))
        parts = {}
        for half in (1, 0):
            total = None
            for step in (0, *order):
                term = jnp.dot(
                    matrices[half][step], arrived[step], preferred_element_type=jnp.float32
                )
                total = term if total is None else lax.optimization_barrier(total) + term
            for index in range(held):
                step = half * held + index
                value = total[index * span : (index + 1) * span]
                if step:
                    value = exchange(value.astype(jnp.bfloat16), "col", col_count, step)
                parts[step] = value
        owned = parts[0]
        for step in range(1, col_count):
            owned = owned + parts[step].astype(jnp.float32)
        return owned

    previous = panel.astype(jnp.float32)
    current = (operator(panel) - centre_value * previous) / half_value
    for _ in range(DEGREE - 1):
        product = operator(current.astype(jnp.bfloat16))
        following = 2.0 * (product - centre_value * current) / half_value - previous
        previous, current = (current, following)

    mine, theirs = current[:rows], exchange(current[rows:], "row", row_count, 1)
    return jnp.where(
        core == 0, jnp.concatenate([mine, theirs], 1), jnp.concatenate([theirs, mine], 1)
    )


def body(per, *arguments):
    return filter_body(per, *arguments)


def gather_order(chips):
    return (chips - 1, *range(1, chips - 1))


def solution(mesh):
    in_specs = (
        P(("row", "col"), None),
        P("col", None, None, None, "row", None),
        P("col", "row", None, None, None),
        P("col", "row", None, None),
        P(),
        P(),
    )
    out_specs = P(("row", "col"), None)

    def whole(trial_vectors, h_blocks, block_col, block_count, center, half_width):
        shape = h_blocks.shape
        per = trial_vectors.shape[0] // (shape[0] * shape[4] * shape[3])
        return jax.shard_map(
            functools.partial(body, per), mesh=mesh, in_specs=in_specs, out_specs=out_specs, check_vma=False
        )(trial_vectors, h_blocks, block_col, block_count, center, half_width)

    return whole
```

time: 143 us -> 143 us (level)
  waiting for transfers between devices: 49.6 us -> 56.6 us
  Pallas kernels: 8.74 us -> 4.18 us
  starting transfers between devices: 59.8 us -> 58.3 us
    ppermute x53, waiting for transfers between devices: 49.6 us -> 56.6 us  [exchange(): return lax.ppermute(value, axis, [(i, i ^ offset) for i in range(size)])]
    pallas_call x8 -> x2, Pallas kernels: 8.74 us -> 4.18 us  [filter_body(): pl.pallas_call(functools.partial(place_blocks, chips, per, width, half, c...]
    ppermute x53, starting transfers between devices: 59.8 us -> 58.3 us  [exchange(): return lax.ppermute(value, axis, [(i, i ^ offset) for i in range(size)])]
  transfers between devices with their start and end apart: 53 -> 53, of which waited for: 37 -> 33; matrix products, arithmetic and copies ran while one was open for 11% -> 11% of each run, Pallas kernels for 6% -> 3%
where the time goes in v4:
time: 143 us
  starting transfers between devices  58.3 us (41%)
  waiting for transfers between devices  56.6 us (40%)
  matrix products  15 us (10%)
  Pallas kernels  4.18 us (3%)
  other arithmetic  4.03 us (3%)
  local copies, waits for them, and re-layouts  2.91 us (2%)
  between operations  2.28 us (2%)
    ppermute x53, starting transfers between devices, exchange(): return lax.ppermute(value, axis, [(i, i ^ offset) for i in range(size)])  58.3 us
    ppermute x53, waiting for transfers between devices, exchange(): return lax.ppermute(value, axis, [(i, i ^ offset) for i in range(size)])  56.6 us
    dot_general x48, matrix products, operator(): jnp.dot(matrices[half][step], arrived[step], preferred_element_type=jnp.f...  15 us
    pallas_call x2, Pallas kernels, filter_body(): pl.pallas_call(functools.partial(place_blocks, chips, per, width, half, c...  4.18 us
  transfers between devices with their start and end apart: 53, of which 33 were waited for; matrix products, arithmetic and copies ran while one was open for 11% of the time, Pallas kernels for 3%

profile of v4, /device:TPU:0, one launch (start us, length us, event | category | flops | bytes accessed | tf_op | source)
XLA Modules:
  0.0 143.3 jit_solution(12853448496673032030)
XLA Ops:
  0.0 1.0 broadcast_select_fusion.1
  1.5 0.8 copy.8
  2.5 0.8 copy.9
  3.7 3.0 %collective-permute-start.13 = (bf16[768,128]{1,0:T(8,128)(2,1)S(1)}, bf16[768,128]{1,0:T(8,128)(2,1)S(1)}, u32[]{:S(2)}, u32[]{:S(2)}) collective-permute-start(bf16[768,128]{1,0:T(8,128)(2,1)S(1)} %bitcast.139), channel_id=1, source_target_pairs={{0,8},{4,12},{8,0},{12,4},{16,24},{20,28},{24,16},{28,20},{1,9},{5... | collective-permute-start | bytes 589832 | tf_op jit(solution)/shard_map/ppermute | solution.py:18
  6.7 0.7 constant_dynamic-slice_fusion.5
  7.4 1.5 %collective-permute-start.14 = (bf16[768,128]{1,0:T(8,128)(2,1)}, bf16[768,128]{1,0:T(8,128)(2,1)S(1)}, u32[]{:S(2)}, u32[]{:S(2)}) collective-permute-start(bf16[768,128]{1,0:T(8,128)(2,1)} %bitcast.11), channel_id=1, source_target_pairs={{0,16},{4,20},{8,24},{12,28},{16,0},{20,4},{24,8},{28,12},{1,17},{... | collective-permute-start | bytes 589832 | tf_op jit(solution)/shard_map/ppermute | solution.py:18
  9.2 3.3 %collective-permute-done.13.refs_1_ = bf16[768,128]{1,0:T(8,128)(2,1)S(1)} collective-permute-done((bf16[768,128]{1,0:T(8,128)(2,1)S(1)}, bf16[768,128]{1,0:T(8,128)(2,1)S(1)}, u32[]{:S(2)}, u32[]{:S(2)}) %collective-permute-start.13) | collective-permute-done | bytes 196640 | tf_op jit(solution)/shard_map/ppermute | solution.py:18
  12.4 6.0 %collective-permute-done.14.refs_2_ = bf16[768,128]{1,0:T(8,128)(2,1)S(1)} collective-permute-done((bf16[768,128]{1,0:T(8,128)(2,1)}, bf16[768,128]{1,0:T(8,128)(2,1)S(1)}, u32[]{:S(2)}, u32[]{:S(2)}) %collective-permute-start.14) | collective-permute-done | bytes 196640 | tf_op jit(solution)/shard_map/ppermute | solution.py:18
  18.9 1.6 %collective-permute-start.9 = (bf16[384,128]{1,0:T(8,128)(2,1)S(1)}, bf16[384,128]{1,0:T(8,128)(2,1)S(1)}, u32[]{:S(2)}, u32[]{:S(2)}) collective-permute-start(bf16[384,128]{1,0:T(8,128)(2,1)S(1)} %pad_maximum_fusion), channel_id=1, source_target_pairs={{0,24},{4,28},{8,16},{12,20},{16,8},{20,12},{24,0},{28,4},{1,25},{... | collective-permute-start | bytes 294920 | tf_op jit(solution)/shard_map/ppermute | solution.py:18
  20.6 1.5 %collective-permute-start.1 = (bf16[768,128]{1,0:T(8,128)(2,1)S(1)}, bf16[768,128]{1,0:T(8,128)(2,1)S(1)}, u32[]{:S(2)}, u32[]{:S(2)}) collective-permute-start(bf16[768,128]{1,0:T(8,128)(2,1)S(1)} %bitcast.136), channel_id=1, source_target_pairs={{0,8},{4,12},{8,0},{12,4},{16,24},{20,28},{24,16},{28,20},{1,9},{5... | collective-permute-start | bytes 589832 | tf_op jit(solution)/shard_map/ppermute | solution.py:18
  22.6 1.5 %collective-permute-start.3 = (bf16[768,128]{1,0:T(8,128)(2,1)S(1)}, bf16[768,128]{1,0:T(8,128)(2,1)S(1)}, u32[]{:S(2)}, u32[]{:S(2)}) collective-permute-start(bf16[768,128]{1,0:T(8,128)(2,1)S(1)} %bitcast.135), channel_id=1, source_target_pairs={{0,24},{4,28},{8,16},{12,20},{16,8},{20,12},{24,0},{28,4},{1,25},{... | collective-permute-start | bytes 589832 | tf_op jit(solution)/shard_map/ppermute | solution.py:18
  24.1 2.0 %shard_map.65 = (bf16[768,384]{1,0:T(8,128)(2,1)S(1)}, bf16[768,384]{1,0:T(8,128)(2,1)S(1)}, bf16[768,384]{1,0:T(8,128)(2,1)S(1)}, bf16[768,384]{1,0:T(8,128)(2,1)S(1)}) custom-call(s32[3]{0:T(128)S(1)} %pad_add_fusion.1.place, s32[384]{0:T(512)S(1)} %pad_add_fusion.used, bf16[768,128]{1,0:T(8,128)(2,1)S(1)} %bitcast.134, ...), custom_call_target="tpu_custom_call" | custom-call | flops 3538944 | bytes 4718592 | tf_op jit(solution)/shard_map/pallas_call | solution.py:114
  26.1 1.6 %collective-permute-start.10 = (bf16[384,128]{1,0:T(8,128)(2,1)S(1)}, bf16[384,128]{1,0:T(8,128)(2,1)S(1)}, u32[]{:S(2)}, u32[]{:S(2)}) collective-permute-start(bf16[384,128]{1,0:T(8,128)(2,1)S(1)} %pad_maximum_fusion), channel_id=1, source_target_pairs={{0,8},{4,12},{8,0},{12,4},{16,24},{20,28},{24,16},{28,20},{1,9},{5... | collective-permute-start | bytes 294920 | tf_op jit(solution)/shard_map/ppermute | solution.py:18
  27.9 7.3 %collective-permute-done.10 = bf16[384,128]{1,0:T(8,128)(2,1)S(1)} collective-permute-done((bf16[384,128]{1,0:T(8,128)(2,1)S(1)}, bf16[384,128]{1,0:T(8,128)(2,1)S(1)}, u32[]{:S(2)}, u32[]{:S(2)}) %collective-permute-start.10) | collective-permute-done | bytes 98336 | tf_op jit(solution)/shard_map/ppermute | solution.py:18
  37.1 2.7 %collective-permute-done.11 = bf16[384,128]{1,0:T(8,128)(2,1)S(1)} collective-permute-done((bf16[384,128]{1,0:T(8,128)(2,1)S(1)}, bf16[384,128]{1,0:T(8,128)(2,1)S(1)}, u32[]{:S(2)}, u32[]{:S(2)}) %collective-permute-start.11) | collective-permute-done | bytes 98336 | tf_op jit(solution)/shard_map/ppermute | solution.py:18
  40.2 3.7 %collective-permute-start.21 = (bf16[384,128]{1,0:T(8,128)(2,1)S(1)}, bf16[384,128]{1,0:T(8,128)(2,1)S(1)}, u32[]{:S(2)}, u32[]{:S(2)}) collective-permute-start(bf16[384,128]{1,0:T(8,128)(2,1)S(1)} %get-tuple-element.58), channel_id=1, source_target_pairs={{0,3},{1,2},{2,1},{3,0},{4,7},{5,6},{6,5},{7,4},{8,11},{9,10},{10,... | collective-permute-start | bytes 294920 | tf_op jit(solution)/shard_map/ppermute | solution.py:18
  43.9 2.2 %shard_map.64 = (bf16[768,384]{1,0:T(8,128)(2,1)S(1)}, bf16[768,384]{1,0:T(8,128)(2,1)S(1)}, bf16[768,384]{1,0:T(8,128)(2,1)S(1)}, bf16[768,384]{1,0:T(8,128)(2,1)S(1)}) custom-call(s32[3]{0:T(128)S(1)} %pad_add_fusion.1.place, s32[384]{0:T(512)S(1)} %pad_add_fusion.used, bf16[768,128]{1,0:T(8,128)(2,1)S(1)} %bitcast.132, ...), custom_call_target="tpu_custom_call" | custom-call | flops 3538944 | bytes 4718592 | tf_op jit(solution)/shard_map/pallas_call | solution.py:114
  47.6 0.8 collective-permute-start.12
  49.7 0.8 collective-permute-done.20
  50.5 1.8 %collective-permute-done.12 = bf16[384,128]{1,0:T(8,128)(2,1)S(1)} collective-permute-done((bf16[384,128]{1,0:T(8,128)(2,1)S(1)}, bf16[384,128]{1,0:T(8,128)(2,1)S(1)}, u32[]{:S(2)}, u32[]{:S(2)}) %collective-permute-start.12) | collective-permute-done | bytes 98336 | tf_op jit(solution)/shard_map/ppermute | solution.py:18
  52.7 0.8 collective-permute-start.22
  53.4 1.5 %collective-permute-start.23 = (bf16[384,128]{1,0:T(8,128)(2,1)S(1)}, bf16[384,128]{1,0:T(8,128)(2,1)S(1)}, u32[]{:S(2)}, u32[]{:S(2)}) collective-permute-start(bf16[384,128]{1,0:T(8,128)(2,1)S(1)} %get-tuple-element.43), channel_id=1, source_target_pairs={{0,8},{4,12},{8,0},{12,4},{16,24},{20,28},{24,16},{28,20},{1,9},{5... | collective-permute-start | bytes 294920 | tf_op jit(solution)/shard_map/ppermute | solution.py:18
  54.9 1.3 collective-permute-start.24
  56.5 1.8 %collective-permute-done.22 = bf16[384,128]{1,0:T(8,128)(2,1)S(1)} collective-permute-done((bf16[384,128]{1,0:T(8,128)(2,1)S(1)}, bf16[384,128]{1,0:T(8,128)(2,1)S(1)}, u32[]{:S(2)}, u32[]{:S(2)}) %collective-permute-start.22) | collective-permute-done | bytes 98336 | tf_op jit(solution)/shard_map/ppermute | solution.py:18
  59.9 2.2 %collective-permute-start.27 = (bf16[384,128]{1,0:T(8,128)(2,1)S(1)}, bf16[384,128]{1,0:T(8,128)(2,1)S(1)}, u32[]{:S(2)}, u32[]{:S(2)}) collective-permute-start(bf16[384,128]{1,0:T(8,128)(2,1)S(1)} %get-tuple-element.56), channel_id=1, source_target_pairs={{0,3},{1,2},{2,1},{3,0},{4,7},{5,6},{6,5},{7,4},{8,11},{9,10},{10,... | collective-permute-start | bytes 294920 | tf_op jit(solution)/shard_map/ppermute | solution.py:18
  62.2 0.6 collective-permute-start.26
  63.9 1.7 %collective-permute-start.25 = (bf16[384,128]{1,0:T(8,128)(2,1)S(1)}, bf16[384,128]{1,0:T(8,128)(2,1)S(1)}, u32[]{:S(2)}, u32[]{:S(2)}) collective-permute-start(bf16[384,128]{1,0:T(8,128)(2,1)S(1)} %slice.242), channel_id=1, source_target_pairs={{0,1},{1,0},{2,3},{3,2},{4,5},{5,4},{6,7},{7,6},{8,9},{9,8},{10,11... | collective-permute-start | bytes 294920 | tf_op jit(solution)/shard_map/ppermute | solution.py:18
  65.6 1.4 collective-permute-done.27
  67.0 2.3 %collective-permute-done.26 = bf16[384,128]{1,0:T(8,128)(2,1)S(1)} collective-permute-done((bf16[384,128]{1,0:T(8,128)(2,1)S(1)}, bf16[384,128]{1,0:T(8,128)(2,1)S(1)}, u32[]{:S(2)}, u32[]{:S(2)}) %collective-permute-start.26) | collective-permute-done | bytes 98336 | tf_op jit(solution)/shard_map/ppermute | solution.py:18
  70.0 1.0 collective-permute-start.28
  71.0 1.5 %collective-permute-start.29 = (bf16[384,128]{1,0:T(8,128)(2,1)S(1)}, bf16[384,128]{1,0:T(8,128)(2,1)S(1)}, u32[]{:S(2)}, u32[]{:S(2)}) collective-permute-start(bf16[384,128]{1,0:T(8,128)(2,1)S(1)} %get-tuple-element.41), channel_id=1, source_target_pairs={{0,8},{4,12},{8,0},{12,4},{16,24},{20,28},{24,16},{28,20},{1,9},{5... | collective-permute-start | bytes 294920 | tf_op jit(solution)/shard_map/ppermute | solution.py:18
  72.5 1.1 collective-permute-start.30
  73.9 1.7 %collective-permute-done.28 = bf16[384,128]{1,0:T(8,128)(2,1)S(1)} collective-permute-done((bf16[384,128]{1,0:T(8,128)(2,1)S(1)}, bf16[384,128]{1,0:T(8,128)(2,1)S(1)}, u32[]{:S(2)}, u32[]{:S(2)}) %collective-permute-start.28) | collective-permute-done | bytes 98336 | tf_op jit(solution)/shard_map/ppermute | solution.py:18
  77.5 3.4 %collective-permute-start.33 = (bf16[384,128]{1,0:T(8,128)(2,1)S(1)}, bf16[384,128]{1,0:T(8,128)(2,1)S(1)}, u32[]{:S(2)}, u32[]{:S(2)}) collective-permute-start(bf16[384,128]{1,0:T(8,128)(2,1)S(1)} %get-tuple-element.54), channel_id=1, source_target_pairs={{0,3},{1,2},{2,1},{3,0},{4,7},{5,6},{6,5},{7,4},{8,11},{9,10},{10,... | collective-permute-start | bytes 294920 | tf_op jit(solution)/shard_map/ppermute | solution.py:18
  82.0 1.2 collective-permute-start.31
  83.1 0.8 collective-permute-done.33
  83.9 2.5 %collective-permute-done.32 = bf16[384,128]{1,0:T(8,128)(2,1)S(1)} collective-permute-done((bf16[384,128]{1,0:T(8,128)(2,1)S(1)}, bf16[384,128]{1,0:T(8,128)(2,1)S(1)}, u32[]{:S(2)}, u32[]{:S(2)}) %collective-permute-start.32) | collective-permute-done | bytes 98336 | tf_op jit(solution)/shard_map/ppermute | solution.py:18
  86.4 1.0 collective-permute-done.31
  87.8 0.8 collective-permute-start.34
  88.6 1.5 %collective-permute-start.35 = (bf16[384,128]{1,0:T(8,128)(2,1)S(1)}, bf16[384,128]{1,0:T(8,128)(2,1)S(1)}, u32[]{:S(2)}, u32[]{:S(2)}) collective-permute-start(bf16[384,128]{1,0:T(8,128)(2,1)S(1)} %get-tuple-element.39), channel_id=1, source_target_pairs={{0,8},{4,12},{8,0},{12,4},{16,24},{20,28},{24,16},{28,20},{1,9},{5... | collective-permute-start | bytes 294920 | tf_op jit(solution)/shard_map/ppermute | solution.py:18
  90.1 1.3 collective-permute-start.36
  91.7 1.7 %collective-permute-done.34 = bf16[384,128]{1,0:T(8,128)(2,1)S(1)} collective-permute-done((bf16[384,128]{1,0:T(8,128)(2,1)S(1)}, bf16[384,128]{1,0:T(8,128)(2,1)S(1)}, u32[]{:S(2)}, u32[]{:S(2)}) %collective-permute-start.34) | collective-permute-done | bytes 98336 | tf_op jit(solution)/shard_map/ppermute | solution.py:18
  95.1 2.4 %collective-permute-start.39 = (bf16[384,128]{1,0:T(8,128)(2,1)S(1)}, bf16[384,128]{1,0:T(8,128)(2,1)S(1)}, u32[]{:S(2)}, u32[]{:S(2)}) collective-permute-start(bf16[384,128]{1,0:T(8,128)(2,1)S(1)} %get-tuple-element.52), channel_id=1, source_target_pairs={{0,3},{1,2},{2,1},{3,0},{4,7},{5,6},{6,5},{7,4},{8,11},{9,10},{10,... | collective-permute-start | bytes 294920 | tf_op jit(solution)/shard_map/ppermute | solution.py:18
  98.6 2.2 %collective-permute-start.37 = (bf16[384,128]{1,0:T(8,128)(2,1)S(1)}, bf16[384,128]{1,0:T(8,128)(2,1)S(1)}, u32[]{:S(2)}, u32[]{:S(2)}) collective-permute-start(bf16[384,128]{1,0:T(8,128)(2,1)S(1)} %slice.240), channel_id=1, source_target_pairs={{0,1},{1,0},{2,3},{3,2},{4,5},{5,4},{6,7},{7,6},{8,9},{9,8},{10,11... | collective-permute-start | bytes 294920 | tf_op jit(solution)/shard_map/ppermute | solution.py:18
  100.8 0.8 collective-permute-done.39
  101.6 2.2 %collective-permute-done.38 = bf16[384,128]{1,0:T(8,128)(2,1)S(1)} collective-permute-done((bf16[384,128]{1,0:T(8,128)(2,1)S(1)}, bf16[384,128]{1,0:T(8,128)(2,1)S(1)}, u32[]{:S(2)}, u32[]{:S(2)}) %collective-permute-start.38) | collective-permute-done | bytes 98336 | tf_op jit(solution)/shard_map/ppermute | solution.py:18
  103.8 0.6 collective-permute-done.37
  104.8 1.3 collective-permute-start.40
  106.0 1.5 %collective-permute-start.41 = (bf16[384,128]{1,0:T(8,128)(2,1)S(1)}, bf16[384,128]{1,0:T(8,128)(2,1)S(1)}, u32[]{:S(2)}, u32[]{:S(2)}) collective-permute-start(bf16[384,128]{1,0:T(8,128)(2,1)S(1)} %get-tuple-element.37), channel_id=1, source_target_pairs={{0,8},{4,12},{8,0},{12,4},{16,24},{20,28},{24,16},{28,20},{1,9},{5... | collective-permute-start | bytes 294920 | tf_op jit(solution)/shard_map/ppermute | solution.py:18
  107.6 0.8 collective-permute-start.42
  108.7 1.7 %collective-permute-done.40 = bf16[384,128]{1,0:T(8,128)(2,1)S(1)} collective-permute-done((bf16[384,128]{1,0:T(8,128)(2,1)S(1)}, bf16[384,128]{1,0:T(8,128)(2,1)S(1)}, u32[]{:S(2)}, u32[]{:S(2)}) %collective-permute-start.40) | collective-permute-done | bytes 98336 | tf_op jit(solution)/shard_map/ppermute | solution.py:18
  112.6 2.8 %collective-permute-start.45 = (bf16[384,128]{1,0:T(8,128)(2,1)S(1)}, bf16[384,128]{1,0:T(8,128)(2,1)S(1)}, u32[]{:S(2)}, u32[]{:S(2)}) collective-permute-start(bf16[384,128]{1,0:T(8,128)(2,1)S(1)} %get-tuple-element.50), channel_id=1, source_target_pairs={{0,3},{1,2},{2,1},{3,0},{4,7},{5,6},{6,5},{7,4},{8,11},{9,10},{10,... | collective-permute-start | bytes 294920 | tf_op jit(solution)/shard_map/ppermute | solution.py:18
  116.5 1.7 %collective-permute-start.43 = (bf16[384,128]{1,0:T(8,128)(2,1)S(1)}, bf16[384,128]{1,0:T(8,128)(2,1)S(1)}, u32[]{:S(2)}, u32[]{:S(2)}) collective-permute-start(bf16[384,128]{1,0:T(8,128)(2,1)S(1)} %slice.239), channel_id=1, source_target_pairs={{0,1},{1,0},{2,3},{3,2},{4,5},{5,4},{6,7},{7,6},{8,9},{9,8},{10,11... | collective-permute-start | bytes 294920 | tf_op jit(solution)/shard_map/ppermute | solution.py:18
  118.2 0.8 collective-permute-done.45
  119.1 5.3 %collective-permute-done.44 = bf16[384,128]{1,0:T(8,128)(2,1)S(1)} collective-permute-done((bf16[384,128]{1,0:T(8,128)(2,1)S(1)}, bf16[384,128]{1,0:T(8,128)(2,1)S(1)}, u32[]{:S(2)}, u32[]{:S(2)}) %collective-permute-start.44) | collective-permute-done | bytes 98336 | tf_op jit(solution)/shard_map/ppermute | solution.py:18
  124.8 1.8 %collective-permute-start.47 = (bf16[384,128]{1,0:T(8,128)(2,1)S(1)}, bf16[384,128]{1,0:T(8,128)(2,1)S(1)}, u32[]{:S(2)}, u32[]{:S(2)}) collective-permute-start(bf16[384,128]{1,0:T(8,128)(2,1)S(1)} %get-tuple-element.35), channel_id=1, source_target_pairs={{0,8},{4,12},{8,0},{12,4},{16,24},{20,28},{24,16},{28,20},{1,9},{5... | collective-permute-start | bytes 294920 | tf_op jit(solution)/shard_map/ppermute | solution.py:18
  126.6 1.7 %collective-permute-start.48 = (bf16[384,128]{1,0:T(8,128)(2,1)S(1)}, bf16[384,128]{1,0:T(8,128)(2,1)S(1)}, u32[]{:S(2)}, u32[]{:S(2)}) collective-permute-start(bf16[384,128]{1,0:T(8,128)(2,1)S(1)} %get-tuple-element.35), channel_id=1, source_target_pairs={{0,16},{4,20},{8,24},{12,28},{16,0},{20,4},{24,8},{28,12},{1,17},{... | collective-permute-start | bytes 294920 | tf_op jit(solution)/shard_map/ppermute | solution.py:18
  128.6 1.7 %collective-permute-done.46 = bf16[384,128]{1,0:T(8,128)(2,1)S(1)} collective-permute-done((bf16[384,128]{1,0:T(8,128)(2,1)S(1)}, bf16[384,128]{1,0:T(8,128)(2,1)S(1)}, u32[]{:S(2)}, u32[]{:S(2)}) %collective-permute-start.46) | collective-permute-done | bytes 98336 | tf_op jit(solution)/shard_map/ppermute | solution.py:18
  132.2 2.7 %collective-permute-start.51 = (bf16[384,128]{1,0:T(8,128)(2,1)S(1)}, bf16[384,128]{1,0:T(8,128)(2,1)S(1)}, u32[]{:S(2)}, u32[]{:S(2)}) collective-permute-start(bf16[384,128]{1,0:T(8,128)(2,1)S(1)} %get-tuple-element.48), channel_id=1, source_target_pairs={{0,3},{1,2},{2,1},{3,0},{4,7},{5,6},{6,5},{7,4},{8,11},{9,10},{10,... | collective-permute-start | bytes 294920 | tf_op jit(solution)/shard_map/ppermute | solution.py:18
  135.4 1.8 %collective-permute-start.49 = (bf16[384,128]{1,0:T(8,128)(2,1)S(1)}, bf16[384,128]{1,0:T(8,128)(2,1)S(1)}, u32[]{:S(2)}, u32[]{:S(2)}) collective-permute-start(bf16[384,128]{1,0:T(8,128)(2,1)S(1)} %slice.238), channel_id=1, source_target_pairs={{0,1},{1,0},{2,3},{3,2},{4,5},{5,4},{6,7},{7,6},{8,9},{9,8},{10,11... | collective-permute-start | bytes 294920 | tf_op jit(solution)/shard_map/ppermute | solution.py:18
  137.2 1.6 %collective-permute-done.51 = bf16[384,128]{1,0:T(8,128)(2,1)S(1)} collective-permute-done((bf16[384,128]{1,0:T(8,128)(2,1)S(1)}, bf16[384,128]{1,0:T(8,128)(2,1)S(1)}, u32[]{:S(2)}, u32[]{:S(2)}) %collective-permute-start.51) | collective-permute-done | bytes 98336 | tf_op jit(solution)/shard_map/ppermute | solution.py:18
  138.7 2.2 %collective-permute-done.50 = bf16[384,128]{1,0:T(8,128)(2,1)S(1)} collective-permute-done((bf16[384,128]{1,0:T(8,128)(2,1)S(1)}, bf16[384,128]{1,0:T(8,128)(2,1)S(1)}, u32[]{:S(2)}, u32[]{:S(2)}) %collective-permute-start.50) | collective-permute-done | bytes 98336 | tf_op jit(solution)/shard_map/ppermute | solution.py:18
  141.3 1.3 collective-permute-done.52
  142.6 0.7 maximum_select_fusion
  (168 shorter events, 24.3 us)
Async XLA Ops:
  0.0 3.6 %copy-start = (bf16[1,8,12,64,1,128]{5,3,4,2,1,0:T(8,128)(2,1)S(1)}, bf16[1,8,12,64,1,128]{5,3,4,2,1,0:T(8,128)(2,1)}, u32[]{:S(2)}) copy-start(bf16[1,8,12,64,1,128]{5,3,4,2,1,0:T(8,128)(2,1)} %param.7) | copy-start | bytes 4718596
  1.0 8.2 %collective-permute-start.8 = (bf16[192,128]{1,0:T(8,128)(2,1)S(1)}, bf16[192,128]{1,0:T(8,128)(2,1)S(1)}, u32[]{:S(2)}, u32[]{:S(2)}) collective-permute-start(bf16[192,128]{1,0:T(8,128)(2,1)S(1)} %get-tuple-element.60), channel_id=1, source_target_pairs={{0,4},{4,0},{8,12},{12,8},{16,20},{20,16},{24,28},{28,24},{1,5},{5... | collective-permute-start | bytes 147464 | tf_op jit(solution)/shard_map/ppermute | solution.py:18
  3.5 15.4 %collective-permute-start = (s32[192]{0:T(256)S(1)}, s32[192]{0:T(256)S(1)}, u32[]{:S(2)}, u32[]{:S(2)}) collective-permute-start(s32[192]{0:T(256)S(1)} %broadcast_select_fusion.2), channel_id=1, source_target_pairs={{0,4},{4,0},{8,12},{12,8},{16,20},{20,16},{24,28},{28,24},{1,5},{5... | collective-permute-start | bytes 2312 | tf_op jit(solution)/shard_map/ppermute | solution.py:18
  3.7 8.7 %collective-permute-start.13 = (bf16[768,128]{1,0:T(8,128)(2,1)S(1)}, bf16[768,128]{1,0:T(8,128)(2,1)S(1)}, u32[]{:S(2)}, u32[]{:S(2)}) collective-permute-start(bf16[768,128]{1,0:T(8,128)(2,1)S(1)} %bitcast.139), channel_id=1, source_target_pairs={{0,8},{4,12},{8,0},{12,4},{16,24},{20,28},{24,16},{28,20},{1,9},{5... | collective-permute-start | bytes 589832 | tf_op jit(solution)/shard_map/ppermute | solution.py:18
  7.4 11.0 %collective-permute-start.14 = (bf16[768,128]{1,0:T(8,128)(2,1)}, bf16[768,128]{1,0:T(8,128)(2,1)S(1)}, u32[]{:S(2)}, u32[]{:S(2)}) collective-permute-start(bf16[768,128]{1,0:T(8,128)(2,1)} %bitcast.11), channel_id=1, source_target_pairs={{0,16},{4,20},{8,24},{12,28},{16,0},{20,4},{24,8},{28,12},{1,17},{... | collective-permute-start | bytes 589832 | tf_op jit(solution)/shard_map/ppermute | solution.py:18
  8.9 9.5 %collective-permute-start.15 = (bf16[768,128]{1,0:T(8,128)(2,1)S(1)}, bf16[768,128]{1,0:T(8,128)(2,1)S(1)}, u32[]{:S(2)}, u32[]{:S(2)}) collective-permute-start(bf16[768,128]{1,0:T(8,128)(2,1)S(1)} %bitcast.138), channel_id=1, source_target_pairs={{0,24},{4,28},{8,16},{12,20},{16,8},{20,12},{24,0},{28,4},{1,25},{... | collective-permute-start | bytes 589832 | tf_op jit(solution)/shard_map/ppermute | solution.py:18
  9.1 11.4 %collective-permute-start.16 = (bf16[768,128]{1,0:T(8,128)(2,1)S(1)}, bf16[768,128]{1,0:T(8,128)(2,1)S(1)}, u32[]{:S(2)}, u32[]{:S(2)}) collective-permute-start(bf16[768,128]{1,0:T(8,128)(2,1)S(1)} %bitcast.133), channel_id=1, source_target_pairs={{0,4},{4,0},{8,12},{12,8},{16,20},{20,16},{24,28},{28,24},{1,5},{5... | collective-permute-start | bytes 589832 | tf_op jit(solution)/shard_map/ppermute | solution.py:18
  12.4 9.6 %collective-permute-start.17 = (bf16[768,128]{1,0:T(8,128)(2,1)S(1)}, bf16[768,128]{1,0:T(8,128)(2,1)S(1)}, u32[]{:S(2)}, u32[]{:S(2)}) collective-permute-start(bf16[768,128]{1,0:T(8,128)(2,1)S(1)} %collective-permute-done.13.refs_1_), channel_id=1, source_target_pairs={{0,4},{4,0},{8,12},{12,8},{16,20},{20,16},{24,28},{28,24},{1,5},{5... | collective-permute-start | bytes 589832 | tf_op jit(solution)/shard_map/ppermute | solution.py:18
  18.4 4.2 %collective-permute-start.18 = (bf16[768,128]{1,0:T(8,128)(2,1)S(1)}, bf16[768,128]{1,0:T(8,128)(2,1)S(1)}, u32[]{:S(2)}, u32[]{:S(2)}) collective-permute-start(bf16[768,128]{1,0:T(8,128)(2,1)S(1)} %collective-permute-done.14.refs_2_), channel_id=1, source_target_pairs={{0,4},{4,0},{8,12},{12,8},{16,20},{20,16},{24,28},{28,24},{1,5},{5... | collective-permute-start | bytes 589832 | tf_op jit(solution)/shard_map/ppermute | solution.py:18
  18.4 5.7 %collective-permute-start.19 = (bf16[768,128]{1,0:T(8,128)(2,1)S(1)}, bf16[768,128]{1,0:T(8,128)(2,1)S(1)}, u32[]{:S(2)}, u32[]{:S(2)}) collective-permute-start(bf16[768,128]{1,0:T(8,128)(2,1)S(1)} %collective-permute-done.15.refs_3_), channel_id=1, source_target_pairs={{0,4},{4,0},{8,12},{12,8},{16,20},{20,16},{24,28},{28,24},{1,5},{5... | collective-permute-start | bytes 589832 | tf_op jit(solution)/shard_map/ppermute | solution.py:18
  18.9 7.1 %collective-permute-start.9 = (bf16[384,128]{1,0:T(8,128)(2,1)S(1)}, bf16[384,128]{1,0:T(8,128)(2,1)S(1)}, u32[]{:S(2)}, u32[]{:S(2)}) collective-permute-start(bf16[384,128]{1,0:T(8,128)(2,1)S(1)} %pad_maximum_fusion), channel_id=1, source_target_pairs={{0,24},{4,28},{8,16},{12,20},{16,8},{20,12},{24,0},{28,4},{1,25},{... | collective-permute-start | bytes 294920 | tf_op jit(solution)/shard_map/ppermute | solution.py:18
  20.6 15.2 %collective-permute-start.1 = (bf16[768,128]{1,0:T(8,128)(2,1)S(1)}, bf16[768,128]{1,0:T(8,128)(2,1)S(1)}, u32[]{:S(2)}, u32[]{:S(2)}) collective-permute-start(bf16[768,128]{1,0:T(8,128)(2,1)S(1)} %bitcast.136), channel_id=1, source_target_pairs={{0,8},{4,12},{8,0},{12,4},{16,24},{20,28},{24,16},{28,20},{1,9},{5... | collective-permute-start | bytes 589832 | tf_op jit(solution)/shard_map/ppermute | solution.py:18
  22.1 13.7 %collective-permute-start.2 = (bf16[768,128]{1,0:T(8,128)(2,1)S(1)}, bf16[768,128]{1,0:T(8,128)(2,1)S(1)}, u32[]{:S(2)}, u32[]{:S(2)}) collective-permute-start(bf16[768,128]{1,0:T(8,128)(2,1)S(1)} %bitcast.137), channel_id=1, source_target_pairs={{0,16},{4,20},{8,24},{12,28},{16,0},{20,4},{24,8},{28,12},{1,17},{... | collective-permute-start | bytes 589832 | tf_op jit(solution)/shard_map/ppermute | solution.py:18
  22.6 13.7 %collective-permute-start.3 = (bf16[768,128]{1,0:T(8,128)(2,1)S(1)}, bf16[768,128]{1,0:T(8,128)(2,1)S(1)}, u32[]{:S(2)}, u32[]{:S(2)}) collective-permute-start(bf16[768,128]{1,0:T(8,128)(2,1)S(1)} %bitcast.135), channel_id=1, source_target_pairs={{0,24},{4,28},{8,16},{12,20},{16,8},{20,12},{24,0},{28,4},{1,25},{... | collective-permute-start | bytes 589832 | tf_op jit(solution)/shard_map/ppermute | solution.py:18
  24.1 19.8 %collective-permute-start.4 = (bf16[768,128]{1,0:T(8,128)(2,1)S(1)}, bf16[768,128]{1,0:T(8,128)(2,1)S(1)}, u32[]{:S(2)}, u32[]{:S(2)}) collective-permute-start(bf16[768,128]{1,0:T(8,128)(2,1)S(1)} %bitcast.131), channel_id=1, source_target_pairs={{0,4},{4,0},{8,12},{12,8},{16,20},{20,16},{24,28},{28,24},{1,5},{5... | collective-permute-start | bytes 589832 | tf_op jit(solution)/shard_map/ppermute | solution.py:18
  26.1 9.1 %collective-permute-start.10 = (bf16[384,128]{1,0:T(8,128)(2,1)S(1)}, bf16[384,128]{1,0:T(8,128)(2,1)S(1)}, u32[]{:S(2)}, u32[]{:S(2)}) collective-permute-start(bf16[384,128]{1,0:T(8,128)(2,1)S(1)} %pad_maximum_fusion), channel_id=1, source_target_pairs={{0,8},{4,12},{8,0},{12,4},{16,24},{20,28},{24,16},{28,20},{1,9},{5... | collective-permute-start | bytes 294920 | tf_op jit(solution)/shard_map/ppermute | solution.py:18
  35.2 4.6 %collective-permute-start.11 = (bf16[384,128]{1,0:T(8,128)(2,1)S(1)}, bf16[384,128]{1,0:T(8,128)(2,1)S(1)}, u32[]{:S(2)}, u32[]{:S(2)}) collective-permute-start(bf16[384,128]{1,0:T(8,128)(2,1)S(1)} %pad_maximum_fusion), channel_id=1, source_target_pairs={{0,16},{4,20},{8,24},{12,28},{16,0},{20,4},{24,8},{28,12},{1,17},{... | collective-permute-start | bytes 294920 | tf_op jit(solution)/shard_map/ppermute | solution.py:18
  35.7 8.1 %collective-permute-start.5 = (bf16[768,128]{1,0:T(8,128)(2,1)S(1)}, bf16[768,128]{1,0:T(8,128)(2,1)S(1)}, u32[]{:S(2)}, u32[]{:S(2)}) collective-permute-start(bf16[768,128]{1,0:T(8,128)(2,1)S(1)} %collective-permute-done.1.refs_1_), channel_id=1, source_target_pairs={{0,4},{4,0},{8,12},{12,8},{16,20},{20,16},{24,28},{28,24},{1,5},{5... | collective-permute-start | bytes 589832 | tf_op jit(solution)/shard_map/ppermute | solution.py:18
  35.8 8.1 %collective-permute-start.6 = (bf16[768,128]{1,0:T(8,128)(2,1)S(1)}, bf16[768,128]{1,0:T(8,128)(2,1)S(1)}, u32[]{:S(2)}, u32[]{:S(2)}) collective-permute-start(bf16[768,128]{1,0:T(8,128)(2,1)S(1)} %collective-permute-done.2.refs_2_), channel_id=1, source_target_pairs={{0,4},{4,0},{8,12},{12,8},{16,20},{20,16},{24,28},{28,24},{1,5},{5... | collective-permute-start | bytes 589832 | tf_op jit(solution)/shard_map/ppermute | solution.py:18
  36.3 7.6 %collective-permute-start.7 = (bf16[768,128]{1,0:T(8,128)(2,1)S(1)}, bf16[768,128]{1,0:T(8,128)(2,1)S(1)}, u32[]{:S(2)}, u32[]{:S(2)}) collective-permute-start(bf16[768,128]{1,0:T(8,128)(2,1)S(1)} %collective-permute-done.3.refs_3_), channel_id=1, source_target_pairs={{0,4},{4,0},{8,12},{12,8},{16,20},{20,16},{24,28},{28,24},{1,5},{5... | collective-permute-start | bytes 589832 | tf_op jit(solution)/shard_map/ppermute | solution.py:18
  40.2 9.5 %collective-permute-start.21 = (bf16[384,128]{1,0:T(8,128)(2,1)S(1)}, bf16[384,128]{1,0:T(8,128)(2,1)S(1)}, u32[]{:S(2)}, u32[]{:S(2)}) collective-permute-start(bf16[384,128]{1,0:T(8,128)(2,1)S(1)} %get-tuple-element.58), channel_id=1, source_target_pairs={{0,3},{1,2},{2,1},{3,0},{4,7},{5,6},{6,5},{7,4},{8,11},{9,10},{10,... | collective-permute-start | bytes 294920 | tf_op jit(solution)/shard_map/ppermute | solution.py:18
  43.9 6.6 %collective-permute-start.20 = (bf16[384,128]{1,0:T(8,128)(2,1)S(1)}, bf16[384,128]{1,0:T(8,128)(2,1)S(1)}, u32[]{:S(2)}, u32[]{:S(2)}) collective-permute-start(bf16[384,128]{1,0:T(8,128)(2,1)S(1)} %get-tuple-element.57), channel_id=1, source_target_pairs={{0,2},{1,3},{2,0},{3,1},{4,6},{5,7},{6,4},{7,5},{8,10},{9,11},{10,... | collective-permute-start | bytes 294920 | tf_op jit(solution)/shard_map/ppermute | solution.py:18
  47.6 4.7 %collective-permute-start.12 = (bf16[384,128]{1,0:T(8,128)(2,1)S(1)}, bf16[384,128]{1,0:T(8,128)(2,1)S(1)}, u32[]{:S(2)}, u32[]{:S(2)}) collective-permute-start(bf16[384,128]{1,0:T(8,128)(2,1)S(1)} %slice.243), channel_id=1, source_target_pairs={{0,1},{1,0},{2,3},{3,2},{4,5},{5,4},{6,7},{7,6},{8,9},{9,8},{10,11... | collective-permute-start | bytes 294920 | tf_op jit(solution)/shard_map/ppermute | solution.py:18
  52.7 5.7 %collective-permute-start.22 = (bf16[384,128]{1,0:T(8,128)(2,1)S(1)}, bf16[384,128]{1,0:T(8,128)(2,1)S(1)}, u32[]{:S(2)}, u32[]{:S(2)}) collective-permute-start(bf16[384,128]{1,0:T(8,128)(2,1)S(1)} %get-tuple-element.43), channel_id=1, source_target_pairs={{0,24},{4,28},{8,16},{12,20},{16,8},{20,12},{24,0},{28,4},{1,25},{... | collective-permute-start | bytes 294920 | tf_op jit(solution)/shard_map/ppermute | solution.py:18
  53.4 5.5 %collective-permute-start.23 = (bf16[384,128]{1,0:T(8,128)(2,1)S(1)}, bf16[384,128]{1,0:T(8,128)(2,1)S(1)}, u32[]{:S(2)}, u32[]{:S(2)}) collective-permute-start(bf16[384,128]{1,0:T(8,128)(2,1)S(1)} %get-tuple-element.43), channel_id=1, source_target_pairs={{0,8},{4,12},{8,0},{12,4},{16,24},{20,28},{24,16},{28,20},{1,9},{5... | collective-permute-start | bytes 294920 | tf_op jit(solution)/shard_map/ppermute | solution.py:18
  54.9 4.6 %collective-permute-start.24 = (bf16[384,128]{1,0:T(8,128)(2,1)S(1)}, bf16[384,128]{1,0:T(8,128)(2,1)S(1)}, u32[]{:S(2)}, u32[]{:S(2)}) collective-permute-start(bf16[384,128]{1,0:T(8,128)(2,1)S(1)} %get-tuple-element.43), channel_id=1, source_target_pairs={{0,16},{4,20},{8,24},{12,28},{16,0},{20,4},{24,8},{28,12},{1,17},{... | collective-permute-start | bytes 294920 | tf_op jit(solution)/shard_map/ppermute | solution.py:18
  59.9 7.1 %collective-permute-start.27 = (bf16[384,128]{1,0:T(8,128)(2,1)S(1)}, bf16[384,128]{1,0:T(8,128)(2,1)S(1)}, u32[]{:S(2)}, u32[]{:S(2)}) collective-permute-start(bf16[384,128]{1,0:T(8,128)(2,1)S(1)} %get-tuple-element.56), channel_id=1, source_target_pairs={{0,3},{1,2},{2,1},{3,0},{4,7},{5,6},{6,5},{7,4},{8,11},{9,10},{10,... | collective-permute-start | bytes 294920 | tf_op jit(solution)/shard_map/ppermute | solution.py:18
  62.2 7.2 %collective-permute-start.26 = (bf16[384,128]{1,0:T(8,128)(2,1)S(1)}, bf16[384,128]{1,0:T(8,128)(2,1)S(1)}, u32[]{:S(2)}, u32[]{:S(2)}) collective-permute-start(bf16[384,128]{1,0:T(8,128)(2,1)S(1)} %get-tuple-element.55), channel_id=1, source_target_pairs={{0,2},{1,3},{2,0},{3,1},{4,6},{5,7},{6,4},{7,5},{8,10},{9,11},{10,... | collective-permute-start | bytes 294920 | tf_op jit(solution)/shard_map/ppermute | solution.py:18
  63.9 5.7 %collective-permute-start.25 = (bf16[384,128]{1,0:T(8,128)(2,1)S(1)}, bf16[384,128]{1,0:T(8,128)(2,1)S(1)}, u32[]{:S(2)}, u32[]{:S(2)}) collective-permute-start(bf16[384,128]{1,0:T(8,128)(2,1)S(1)} %slice.242), channel_id=1, source_target_pairs={{0,1},{1,0},{2,3},{3,2},{4,5},{5,4},{6,7},{7,6},{8,9},{9,8},{10,11... | collective-permute-start | bytes 294920 | tf_op jit(solution)/shard_map/ppermute | solution.py:18
  70.0 5.6 %collective-permute-start.28 = (bf16[384,128]{1,0:T(8,128)(2,1)S(1)}, bf16[384,128]{1,0:T(8,128)(2,1)S(1)}, u32[]{:S(2)}, u32[]{:S(2)}) collective-permute-start(bf16[384,128]{1,0:T(8,128)(2,1)S(1)} %get-tuple-element.41), channel_id=1, source_target_pairs={{0,24},{4,28},{8,16},{12,20},{16,8},{20,12},{24,0},{28,4},{1,25},{... | collective-permute-start | bytes 294920 | tf_op jit(solution)/shard_map/ppermute | solution.py:18
  71.0 5.1 %collective-permute-start.29 = (bf16[384,128]{1,0:T(8,128)(2,1)S(1)}, bf16[384,128]{1,0:T(8,128)(2,1)S(1)}, u32[]{:S(2)}, u32[]{:S(2)}) collective-permute-start(bf16[384,128]{1,0:T(8,128)(2,1)S(1)} %get-tuple-element.41), channel_id=1, source_target_pairs={{0,8},{4,12},{8,0},{12,4},{16,24},{20,28},{24,16},{28,20},{1,9},{5... | collective-permute-start | bytes 294920 | tf_op jit(solution)/shard_map/ppermute | solution.py:18
  72.5 4.6 %collective-permute-start.30 = (bf16[384,128]{1,0:T(8,128)(2,1)S(1)}, bf16[384,128]{1,0:T(8,128)(2,1)S(1)}, u32[]{:S(2)}, u32[]{:S(2)}) collective-permute-start(bf16[384,128]{1,0:T(8,128)(2,1)S(1)} %get-tuple-element.41), channel_id=1, source_target_pairs={{0,16},{4,20},{8,24},{12,28},{16,0},{20,4},{24,8},{28,12},{1,17},{... | collective-permute-start | bytes 294920 | tf_op jit(solution)/shard_map/ppermute | solution.py:18
  77.5 6.5 %collective-permute-start.33 = (bf16[384,128]{1,0:T(8,128)(2,1)S(1)}, bf16[384,128]{1,0:T(8,128)(2,1)S(1)}, u32[]{:S(2)}, u32[]{:S(2)}) collective-permute-start(bf16[384,128]{1,0:T(8,128)(2,1)S(1)} %get-tuple-element.54), channel_id=1, source_target_pairs={{0,3},{1,2},{2,1},{3,0},{4,7},{5,6},{6,5},{7,4},{8,11},{9,10},{10,... | collective-permute-start | bytes 294920 | tf_op jit(solution)/shard_map/ppermute | solution.py:18
  80.8 5.6 %collective-permute-start.32 = (bf16[384,128]{1,0:T(8,128)(2,1)S(1)}, bf16[384,128]{1,0:T(8,128)(2,1)S(1)}, u32[]{:S(2)}, u32[]{:S(2)}) collective-permute-start(bf16[384,128]{1,0:T(8,128)(2,1)S(1)} %get-tuple-element.53), channel_id=1, source_target_pairs={{0,2},{1,3},{2,0},{3,1},{4,6},{5,7},{6,4},{7,5},{8,10},{9,11},{10,... | collective-permute-start | bytes 294920 | tf_op jit(solution)/shard_map/ppermute | solution.py:18
  82.0 5.4 %collective-permute-start.31 = (bf16[384,128]{1,0:T(8,128)(2,1)S(1)}, bf16[384,128]{1,0:T(8,128)(2,1)S(1)}, u32[]{:S(2)}, u32[]{:S(2)}) collective-permute-start(bf16[384,128]{1,0:T(8,128)(2,1)S(1)} %slice.241), channel_id=1, source_target_pairs={{0,1},{1,0},{2,3},{3,2},{4,5},{5,4},{6,7},{7,6},{8,9},{9,8},{10,11... | collective-permute-start | bytes 294920 | tf_op jit(solution)/shard_map/ppermute | solution.py:18
  87.8 5.6 %collective-permute-start.34 = (bf16[384,128]{1,0:T(8,128)(2,1)S(1)}, bf16[384,128]{1,0:T(8,128)(2,1)S(1)}, u32[]{:S(2)}, u32[]{:S(2)}) collective-permute-start(bf16[384,128]{1,0:T(8,128)(2,1)S(1)} %get-tuple-element.39), channel_id=1, source_target_pairs={{0,24},{4,28},{8,16},{12,20},{16,8},{20,12},{24,0},{28,4},{1,25},{... | collective-permute-start | bytes 294920 | tf_op jit(solution)/shard_map/ppermute | solution.py:18
  88.6 5.1 %collective-permute-start.35 = (bf16[384,128]{1,0:T(8,128)(2,1)S(1)}, bf16[384,128]{1,0:T(8,128)(2,1)S(1)}, u32[]{:S(2)}, u32[]{:S(2)}) collective-permute-start(bf16[384,128]{1,0:T(8,128)(2,1)S(1)} %get-tuple-element.39), channel_id=1, source_target_pairs={{0,8},{4,12},{8,0},{12,4},{16,24},{20,28},{24,16},{28,20},{1,9},{5... | collective-permute-start | bytes 294920 | tf_op jit(solution)/shard_map/ppermute | solution.py:18
  90.1 4.6 %collective-permute-start.36 = (bf16[384,128]{1,0:T(8,128)(2,1)S(1)}, bf16[384,128]{1,0:T(8,128)(2,1)S(1)}, u32[]{:S(2)}, u32[]{:S(2)}) collective-permute-start(bf16[384,128]{1,0:T(8,128)(2,1)S(1)} %get-tuple-element.39), channel_id=1, source_target_pairs={{0,16},{4,20},{8,24},{12,28},{16,0},{20,4},{24,8},{28,12},{1,17},{... | collective-permute-start | bytes 294920 | tf_op jit(solution)/shard_map/ppermute | solution.py:18
  95.1 6.5 %collective-permute-start.39 = (bf16[384,128]{1,0:T(8,128)(2,1)S(1)}, bf16[384,128]{1,0:T(8,128)(2,1)S(1)}, u32[]{:S(2)}, u32[]{:S(2)}) collective-permute-start(bf16[384,128]{1,0:T(8,128)(2,1)S(1)} %get-tuple-element.52), channel_id=1, source_target_pairs={{0,3},{1,2},{2,1},{3,0},{4,7},{5,6},{6,5},{7,4},{8,11},{9,10},{10,... | collective-permute-start | bytes 294920 | tf_op jit(solution)/shard_map/ppermute | solution.py:18
  97.5 6.3 %collective-permute-start.38 = (bf16[384,128]{1,0:T(8,128)(2,1)S(1)}, bf16[384,128]{1,0:T(8,128)(2,1)S(1)}, u32[]{:S(2)}, u32[]{:S(2)}) collective-permute-start(bf16[384,128]{1,0:T(8,128)(2,1)S(1)} %get-tuple-element.51), channel_id=1, source_target_pairs={{0,2},{1,3},{2,0},{3,1},{4,6},{5,7},{6,4},{7,5},{8,10},{9,11},{10,... | collective-permute-start | bytes 294920 | tf_op jit(solution)/shard_map/ppermute | solution.py:18
  98.6 5.8 %collective-permute-start.37 = (bf16[384,128]{1,0:T(8,128)(2,1)S(1)}, bf16[384,128]{1,0:T(8,128)(2,1)S(1)}, u32[]{:S(2)}, u32[]{:S(2)}) collective-permute-start(bf16[384,128]{1,0:T(8,128)(2,1)S(1)} %slice.240), channel_id=1, source_target_pairs={{0,1},{1,0},{2,3},{3,2},{4,5},{5,4},{6,7},{7,6},{8,9},{9,8},{10,11... | collective-permute-start | bytes 294920 | tf_op jit(solution)/shard_map/ppermute | solution.py:18
  104.8 5.6 %collective-permute-start.40 = (bf16[384,128]{1,0:T(8,128)(2,1)S(1)}, bf16[384,128]{1,0:T(8,128)(2,1)S(1)}, u32[]{:S(2)}, u32[]{:S(2)}) collective-permute-start(bf16[384,128]{1,0:T(8,128)(2,1)S(1)} %get-tuple-element.37), channel_id=1, source_target_pairs={{0,24},{4,28},{8,16},{12,20},{16,8},{20,12},{24,0},{28,4},{1,25},{... | collective-permute-start | bytes 294920 | tf_op jit(solution)/shard_map/ppermute | solution.py:18
  106.0 5.2 %collective-permute-start.41 = (bf16[384,128]{1,0:T(8,128)(2,1)S(1)}, bf16[384,128]{1,0:T(8,128)(2,1)S(1)}, u32[]{:S(2)}, u32[]{:S(2)}) collective-permute-start(bf16[384,128]{1,0:T(8,128)(2,1)S(1)} %get-tuple-element.37), channel_id=1, source_target_pairs={{0,8},{4,12},{8,0},{12,4},{16,24},{20,28},{24,16},{28,20},{1,9},{5... | collective-permute-start | bytes 294920 | tf_op jit(solution)/shard_map/ppermute | solution.py:18
  107.6 4.6 %collective-permute-start.42 = (bf16[384,128]{1,0:T(8,128)(2,1)S(1)}, bf16[384,128]{1,0:T(8,128)(2,1)S(1)}, u32[]{:S(2)}, u32[]{:S(2)}) collective-permute-start(bf16[384,128]{1,0:T(8,128)(2,1)S(1)} %get-tuple-element.37), channel_id=1, source_target_pairs={{0,16},{4,20},{8,24},{12,28},{16,0},{20,4},{24,8},{28,12},{1,17},{... | collective-permute-start | bytes 294920 | tf_op jit(solution)/shard_map/ppermute | solution.py:18
  112.6 6.5 %collective-permute-start.45 = (bf16[384,128]{1,0:T(8,128)(2,1)S(1)}, bf16[384,128]{1,0:T(8,128)(2,1)S(1)}, u32[]{:S(2)}, u32[]{:S(2)}) collective-permute-start(bf16[384,128]{1,0:T(8,128)(2,1)S(1)} %get-tuple-element.50), channel_id=1, source_target_pairs={{0,3},{1,2},{2,1},{3,0},{4,7},{5,6},{6,5},{7,4},{8,11},{9,10},{10,... | collective-permute-start | bytes 294920 | tf_op jit(solution)/shard_map/ppermute | solution.py:18
  115.4 9.0 %collective-permute-start.44 = (bf16[384,128]{1,0:T(8,128)(2,1)S(1)}, bf16[384,128]{1,0:T(8,128)(2,1)S(1)}, u32[]{:S(2)}, u32[]{:S(2)}) collective-permute-start(bf16[384,128]{1,0:T(8,128)(2,1)S(1)} %get-tuple-element.49), channel_id=1, source_target_pairs={{0,2},{1,3},{2,0},{3,1},{4,6},{5,7},{6,4},{7,5},{8,10},{9,11},{10,... | collective-permute-start | bytes 294920 | tf_op jit(solution)/shard_map/ppermute | solution.py:18
  116.5 7.9 %collective-permute-start.43 = (bf16[384,128]{1,0:T(8,128)(2,1)S(1)}, bf16[384,128]{1,0:T(8,128)(2,1)S(1)}, u32[]{:S(2)}, u32[]{:S(2)}) collective-permute-start(bf16[384,128]{1,0:T(8,128)(2,1)S(1)} %slice.239), channel_id=1, source_target_pairs={{0,1},{1,0},{2,3},{3,2},{4,5},{5,4},{6,7},{7,6},{8,9},{9,8},{10,11... | collective-permute-start | bytes 294920 | tf_op jit(solution)/shard_map/ppermute | solution.py:18
  124.8 5.6 %collective-permute-start.46 = (bf16[384,128]{1,0:T(8,128)(2,1)S(1)}, bf16[384,128]{1,0:T(8,128)(2,1)S(1)}, u32[]{:S(2)}, u32[]{:S(2)}) collective-permute-start(bf16[384,128]{1,0:T(8,128)(2,1)S(1)} %get-tuple-element.35), channel_id=1, source_target_pairs={{0,24},{4,28},{8,16},{12,20},{16,8},{20,12},{24,0},{28,4},{1,25},{... | collective-permute-start | bytes 294920 | tf_op jit(solution)/shard_map/ppermute | solution.py:18
  124.8 6.2 %collective-permute-start.47 = (bf16[384,128]{1,0:T(8,128)(2,1)S(1)}, bf16[384,128]{1,0:T(8,128)(2,1)S(1)}, u32[]{:S(2)}, u32[]{:S(2)}) collective-permute-start(bf16[384,128]{1,0:T(8,128)(2,1)S(1)} %get-tuple-element.35), channel_id=1, source_target_pairs={{0,8},{4,12},{8,0},{12,4},{16,24},{20,28},{24,16},{28,20},{1,9},{5... | collective-permute-start | bytes 294920 | tf_op jit(solution)/shard_map/ppermute | solution.py:18
  126.6 5.2 %collective-permute-start.48 = (bf16[384,128]{1,0:T(8,128)(2,1)S(1)}, bf16[384,128]{1,0:T(8,128)(2,1)S(1)}, u32[]{:S(2)}, u32[]{:S(2)}) collective-permute-start(bf16[384,128]{1,0:T(8,128)(2,1)S(1)} %get-tuple-element.35), channel_id=1, source_target_pairs={{0,16},{4,20},{8,24},{12,28},{16,0},{20,4},{24,8},{28,12},{1,17},{... | collective-permute-start | bytes 294920 | tf_op jit(solution)/shard_map/ppermute | solution.py:18
  132.2 6.5 %collective-permute-start.51 = (bf16[384,128]{1,0:T(8,128)(2,1)S(1)}, bf16[384,128]{1,0:T(8,128)(2,1)S(1)}, u32[]{:S(2)}, u32[]{:S(2)}) collective-permute-start(bf16[384,128]{1,0:T(8,128)(2,1)S(1)} %get-tuple-element.48), channel_id=1, source_target_pairs={{0,3},{1,2},{2,1},{3,0},{4,7},{5,6},{6,5},{7,4},{8,11},{9,10},{10,... | collective-permute-start | bytes 294920 | tf_op jit(solution)/shard_map/ppermute | solution.py:18
  135.0 6.0 %collective-permute-start.50 = (bf16[384,128]{1,0:T(8,128)(2,1)S(1)}, bf16[384,128]{1,0:T(8,128)(2,1)S(1)}, u32[]{:S(2)}, u32[]{:S(2)}) collective-permute-start(bf16[384,128]{1,0:T(8,128)(2,1)S(1)} %get-tuple-element.47), channel_id=1, source_target_pairs={{0,2},{1,3},{2,0},{3,1},{4,6},{5,7},{6,4},{7,5},{8,10},{9,11},{10,... | collective-permute-start | bytes 294920 | tf_op jit(solution)/shard_map/ppermute | solution.py:18
  135.4 5.7 %collective-permute-start.49 = (bf16[384,128]{1,0:T(8,128)(2,1)S(1)}, bf16[384,128]{1,0:T(8,128)(2,1)S(1)}, u32[]{:S(2)}, u32[]{:S(2)}) collective-permute-start(bf16[384,128]{1,0:T(8,128)(2,1)S(1)} %slice.238), channel_id=1, source_target_pairs={{0,1},{1,0},{2,3},{3,2},{4,5},{5,4},{6,7},{7,6},{8,9},{9,8},{10,11... | collective-permute-start | bytes 294920 | tf_op jit(solution)/shard_map/ppermute | solution.py:18
  141.2 1.4 collective-permute-start.52

commit v5 on v4

--- a/solution.py
+++ b/solution.py
@@ -11,7 +11,7 @@
 DEGREE = 6
 PAIR = 2
 SLOTS = 2
-UNROLL = 3
+UNROLL = 12
 
 
 def exchange(value, axis, size, offset):
@@ -131,14 +131,14 @@
     rows = domain * width // col_count
     span = PAIR * rows
 
-    def operator(current):
+    def operator(number, current):
         arrived = [current]
         for step in range(1, chips):
             arrived.append(exchange(current, "row", row_count, PAIR * step))
         parts = {}
         for half in (1, 0):
             total = None
-            for step in (0, *order):
+            for step in (0, *(order if number == 0 else range(1, chips))):
                 term = jnp.dot(
                     matrices[half][step], arrived[step], preferred_element_type=jnp.float32
                 )
@@ -155,9 +155,9 @@
         return owned
 
     previous = panel.astype(jnp.float32)
-    current = (operator(panel) - centre_value * previous) / half_value
-    for _ in range(DEGREE - 1):
-        product = operator(current.astype(jnp.bfloat16))
+    current = (operator(0, panel) - centre_value * previous) / half_value
+    for degree_step in range(DEGREE - 1):
+        product = operator(degree_step + 1, current.astype(jnp.bfloat16))
         following = 2.0 * (product - centre_value * current) / half_value - previous
         previous, current = (current, following)
 
@@ -172,7 +172,7 @@
 
 
 def gather_order(chips):
-    return (chips - 1, *range(1, chips - 1))
+    return tuple(range(1, chips))
 
 
 def solution(mesh):

time: 143 us -> 146 us (1.021)
  waiting for transfers between devices: 56.6 us -> 59 us
    ppermute x53, waiting for transfers between devices: 56.6 us -> 59 us  [exchange(): return lax.ppermute(value, axis, [(i, i ^ offset) for i in range(size)])]
  transfers between devices with their start and end apart: 53 -> 53, of which waited for: 33 -> 33; matrix products, arithmetic and copies ran while one was open for 11% -> 11% of each run, Pallas kernels for 3% -> 2%
where the time goes in v5:
time: 146 us
  waiting for transfers between devices  59 us (40%)
  starting transfers between devices  58.9 us (40%)
  matrix products  15.2 us (10%)
  other arithmetic  4.03 us (3%)
  Pallas kernels  3.41 us (2%)
  local copies, waits for them, and re-layouts  2.9 us (2%)
  between operations  2.25 us (2%)
    ppermute x53, waiting for transfers between devices, exchange(): return lax.ppermute(value, axis, [(i, i ^ offset) for i in range(size)])  59 us
    ppermute x53, starting transfers between devices, exchange(): return lax.ppermute(value, axis, [(i, i ^ offset) for i in range(size)])  58.9 us
    dot_general x48, matrix products, operator(): jnp.dot(matrices[half][step], arrived[step], preferred_element_type=jnp.f...  15.2 us
    pallas_call x2, Pallas kernels, filter_body(): pl.pallas_call(functools.partial(place_blocks, chips, per, width, half, c...  3.41 us
  transfers between devices with their start and end apart: 53, of which 33 were waited for; matrix products, arithmetic and copies ran while one was open for 11% of the time, Pallas kernels for 2%

profile of v5, /device:TPU:0, one launch (start us, length us, event | category | flops | bytes accessed | tf_op | source)
XLA Modules:
  0.0 145.6 jit_solution(4948737280660438093)
XLA Ops:
  0.0 1.0 broadcast_select_fusion.1
  1.5 0.8 copy.8
  2.5 0.8 copy.9
  3.7 3.0 %collective-permute-start.13 = (bf16[768,128]{1,0:T(8,128)(2,1)S(1)}, bf16[768,128]{1,0:T(8,128)(2,1)S(1)}, u32[]{:S(2)}, u32[]{:S(2)}) collective-permute-start(bf16[768,128]{1,0:T(8,128)(2,1)S(1)} %bitcast.138), channel_id=1, source_target_pairs={{0,8},{4,12},{8,0},{12,4},{16,24},{20,28},{24,16},{28,20},{1,9},{5... | collective-permute-start | bytes 589832 | tf_op jit(solution)/shard_map/ppermute | solution.py:18
  6.7 1.6 %collective-permute-start.14 = (bf16[768,128]{1,0:T(8,128)(2,1)S(1)}, bf16[768,128]{1,0:T(8,128)(2,1)S(1)}, u32[]{:S(2)}, u32[]{:S(2)}) collective-permute-start(bf16[768,128]{1,0:T(8,128)(2,1)S(1)} %bitcast.139), channel_id=1, source_target_pairs={{0,16},{4,20},{8,24},{12,28},{16,0},{20,4},{24,8},{28,12},{1,17},{... | collective-permute-start | bytes 589832 | tf_op jit(solution)/shard_map/ppermute | solution.py:18
  9.2 3.1 %collective-permute-done.13.refs_1_ = bf16[768,128]{1,0:T(8,128)(2,1)S(1)} collective-permute-done((bf16[768,128]{1,0:T(8,128)(2,1)S(1)}, bf16[768,128]{1,0:T(8,128)(2,1)S(1)}, u32[]{:S(2)}, u32[]{:S(2)}) %collective-permute-start.13) | collective-permute-done | bytes 196640 | tf_op jit(solution)/shard_map/ppermute | solution.py:18
  12.4 5.2 %collective-permute-done.14.refs_2_ = bf16[768,128]{1,0:T(8,128)(2,1)S(1)} collective-permute-done((bf16[768,128]{1,0:T(8,128)(2,1)S(1)}, bf16[768,128]{1,0:T(8,128)(2,1)S(1)}, u32[]{:S(2)}, u32[]{:S(2)}) %collective-permute-start.14) | collective-permute-done | bytes 196640 | tf_op jit(solution)/shard_map/ppermute | solution.py:18
  18.9 1.4 collective-permute-start.1
  20.2 1.5 %collective-permute-start.2 = (bf16[768,128]{1,0:T(8,128)(2,1)S(1)}, bf16[768,128]{1,0:T(8,128)(2,1)S(1)}, u32[]{:S(2)}, u32[]{:S(2)}) collective-permute-start(bf16[768,128]{1,0:T(8,128)(2,1)S(1)} %bitcast.136), channel_id=1, source_target_pairs={{0,16},{4,20},{8,24},{12,28},{16,0},{20,4},{24,8},{28,12},{1,17},{... | collective-permute-start | bytes 589832 | tf_op jit(solution)/shard_map/ppermute | solution.py:18
  22.4 1.7 %shard_map.65 = (bf16[768,384]{1,0:T(8,128)(2,1)S(1)}, bf16[768,384]{1,0:T(8,128)(2,1)S(1)}, bf16[768,384]{1,0:T(8,128)(2,1)S(1)}, bf16[768,384]{1,0:T(8,128)(2,1)S(1)}) custom-call(s32[3]{0:T(128)S(1)} %pad_add_fusion.1.place, s32[384]{0:T(512)S(1)} %pad_add_fusion.used, bf16[768,128]{1,0:T(8,128)(2,1)S(1)} %bitcast.134, ...), custom_call_target="tpu_custom_call" | custom-call | flops 3538944 | bytes 4718592 | tf_op jit(solution)/shard_map/pallas_call | solution.py:114
  24.1 1.5 %collective-permute-start.10 = (bf16[384,128]{1,0:T(8,128)(2,1)S(1)}, bf16[384,128]{1,0:T(8,128)(2,1)S(1)}, u32[]{:S(2)}, u32[]{:S(2)}) collective-permute-start(bf16[384,128]{1,0:T(8,128)(2,1)S(1)} %pad_maximum_fusion), channel_id=1, source_target_pairs={{0,16},{4,20},{8,24},{12,28},{16,0},{20,4},{24,8},{28,12},{1,17},{... | collective-permute-start | bytes 294920 | tf_op jit(solution)/shard_map/ppermute | solution.py:18
  25.9 7.6 %collective-permute-done.10 = bf16[384,128]{1,0:T(8,128)(2,1)S(1)} collective-permute-done((bf16[384,128]{1,0:T(8,128)(2,1)S(1)}, bf16[384,128]{1,0:T(8,128)(2,1)S(1)}, u32[]{:S(2)}, u32[]{:S(2)}) %collective-permute-start.10) | collective-permute-done | bytes 98336 | tf_op jit(solution)/shard_map/ppermute | solution.py:18
  33.5 1.9 %collective-permute-start.11 = (bf16[384,128]{1,0:T(8,128)(2,1)S(1)}, bf16[384,128]{1,0:T(8,128)(2,1)S(1)}, u32[]{:S(2)}, u32[]{:S(2)}) collective-permute-start(bf16[384,128]{1,0:T(8,128)(2,1)S(1)} %pad_maximum_fusion), channel_id=1, source_target_pairs={{0,24},{4,28},{8,16},{12,20},{16,8},{20,12},{24,0},{28,4},{1,25},{... | collective-permute-start | bytes 294920 | tf_op jit(solution)/shard_map/ppermute | solution.py:18
  36.8 2.2 %collective-permute-done.11 = bf16[384,128]{1,0:T(8,128)(2,1)S(1)} collective-permute-done((bf16[384,128]{1,0:T(8,128)(2,1)S(1)}, bf16[384,128]{1,0:T(8,128)(2,1)S(1)}, u32[]{:S(2)}, u32[]{:S(2)}) %collective-permute-start.11) | collective-permute-done | bytes 98336 | tf_op jit(solution)/shard_map/ppermute | solution.py:18
  39.4 3.7 %collective-permute-start.21 = (bf16[384,128]{1,0:T(8,128)(2,1)S(1)}, bf16[384,128]{1,0:T(8,128)(2,1)S(1)}, u32[]{:S(2)}, u32[]{:S(2)}) collective-permute-start(bf16[384,128]{1,0:T(8,128)(2,1)S(1)} %get-tuple-element.58), channel_id=1, source_target_pairs={{0,3},{1,2},{2,1},{3,0},{4,7},{5,6},{6,5},{7,4},{8,11},{9,10},{10,... | collective-permute-start | bytes 294920 | tf_op jit(solution)/shard_map/ppermute | solution.py:18
  43.1 1.7 %shard_map.64 = (bf16[768,384]{1,0:T(8,128)(2,1)S(1)}, bf16[768,384]{1,0:T(8,128)(2,1)S(1)}, bf16[768,384]{1,0:T(8,128)(2,1)S(1)}, bf16[768,384]{1,0:T(8,128)(2,1)S(1)}) custom-call(s32[3]{0:T(128)S(1)} %pad_add_fusion.1.place, s32[384]{0:T(512)S(1)} %pad_add_fusion.used, bf16[768,128]{1,0:T(8,128)(2,1)S(1)} %bitcast.132, ...), custom_call_target="tpu_custom_call" | custom-call | flops 3538944 | bytes 4718592 | tf_op jit(solution)/shard_map/pallas_call | solution.py:114
  46.2 0.8 collective-permute-start.12
  48.4 2.0 %collective-permute-done.20 = bf16[384,128]{1,0:T(8,128)(2,1)S(1)} collective-permute-done((bf16[384,128]{1,0:T(8,128)(2,1)S(1)}, bf16[384,128]{1,0:T(8,128)(2,1)S(1)}, u32[]{:S(2)}, u32[]{:S(2)}) %collective-permute-start.20) | collective-permute-done | bytes 98336 | tf_op jit(solution)/shard_map/ppermute | solution.py:18
  50.4 1.0 collective-permute-done.12
  51.8 1.1 collective-permute-start.22
  52.9 2.2 %collective-permute-start.23 = (bf16[384,128]{1,0:T(8,128)(2,1)S(1)}, bf16[384,128]{1,0:T(8,128)(2,1)S(1)}, u32[]{:S(2)}, u32[]{:S(2)}) collective-permute-start(bf16[384,128]{1,0:T(8,128)(2,1)S(1)} %get-tuple-element.43), channel_id=1, source_target_pairs={{0,16},{4,20},{8,24},{12,28},{16,0},{20,4},{24,8},{28,12},{1,17},{... | collective-permute-start | bytes 294920 | tf_op jit(solution)/shard_map/ppermute | solution.py:18
  55.6 1.2 collective-permute-done.22
  57.2 1.5 %collective-permute-done.23 = bf16[384,128]{1,0:T(8,128)(2,1)S(1)} collective-permute-done((bf16[384,128]{1,0:T(8,128)(2,1)S(1)}, bf16[384,128]{1,0:T(8,128)(2,1)S(1)}, u32[]{:S(2)}, u32[]{:S(2)}) %collective-permute-start.23) | collective-permute-done | bytes 98336 | tf_op jit(solution)/shard_map/ppermute | solution.py:18
  59.2 1.4 collective-permute-done.24
  61.0 2.4 %collective-permute-start.27 = (bf16[384,128]{1,0:T(8,128)(2,1)S(1)}, bf16[384,128]{1,0:T(8,128)(2,1)S(1)}, u32[]{:S(2)}, u32[]{:S(2)}) collective-permute-start(bf16[384,128]{1,0:T(8,128)(2,1)S(1)} %get-tuple-element.56), channel_id=1, source_target_pairs={{0,3},{1,2},{2,1},{3,0},{4,7},{5,6},{6,5},{7,4},{8,11},{9,10},{10,... | collective-permute-start | bytes 294920 | tf_op jit(solution)/shard_map/ppermute | solution.py:18
  64.5 2.1 %collective-permute-start.25 = (bf16[384,128]{1,0:T(8,128)(2,1)S(1)}, bf16[384,128]{1,0:T(8,128)(2,1)S(1)}, u32[]{:S(2)}, u32[]{:S(2)}) collective-permute-start(bf16[384,128]{1,0:T(8,128)(2,1)S(1)} %slice.242), channel_id=1, source_target_pairs={{0,1},{1,0},{2,3},{3,2},{4,5},{5,4},{6,7},{7,6},{8,9},{9,8},{10,11... | collective-permute-start | bytes 294920 | tf_op jit(solution)/shard_map/ppermute | solution.py:18
  66.7 0.8 collective-permute-done.27
  67.5 2.2 %collective-permute-done.26 = bf16[384,128]{1,0:T(8,128)(2,1)S(1)} collective-permute-done((bf16[384,128]{1,0:T(8,128)(2,1)S(1)}, bf16[384,128]{1,0:T(8,128)(2,1)S(1)}, u32[]{:S(2)}, u32[]{:S(2)}) %collective-permute-start.26) | collective-permute-done | bytes 98336 | tf_op jit(solution)/shard_map/ppermute | solution.py:18
  70.9 1.3 collective-permute-start.29
  72.2 2.1 %collective-permute-start.30 = (bf16[384,128]{1,0:T(8,128)(2,1)S(1)}, bf16[384,128]{1,0:T(8,128)(2,1)S(1)}, u32[]{:S(2)}, u32[]{:S(2)}) collective-permute-start(bf16[384,128]{1,0:T(8,128)(2,1)S(1)} %get-tuple-element.41), channel_id=1, source_target_pairs={{0,24},{4,28},{8,16},{12,20},{16,8},{20,12},{24,0},{28,4},{1,25},{... | collective-permute-start | bytes 294920 | tf_op jit(solution)/shard_map/ppermute | solution.py:18
  74.6 0.8 collective-permute-done.28
  76.1 1.5 %collective-permute-done.30 = bf16[384,128]{1,0:T(8,128)(2,1)S(1)} collective-permute-done((bf16[384,128]{1,0:T(8,128)(2,1)S(1)}, bf16[384,128]{1,0:T(8,128)(2,1)S(1)}, u32[]{:S(2)}, u32[]{:S(2)}) %collective-permute-start.30) | collective-permute-done | bytes 98336 | tf_op jit(solution)/shard_map/ppermute | solution.py:18
  78.1 1.9 %collective-permute-start.33 = (bf16[384,128]{1,0:T(8,128)(2,1)S(1)}, bf16[384,128]{1,0:T(8,128)(2,1)S(1)}, u32[]{:S(2)}, u32[]{:S(2)}) collective-permute-start(bf16[384,128]{1,0:T(8,128)(2,1)S(1)} %get-tuple-element.54), channel_id=1, source_target_pairs={{0,3},{1,2},{2,1},{3,0},{4,7},{5,6},{6,5},{7,4},{8,11},{9,10},{10,... | collective-permute-start | bytes 294920 | tf_op jit(solution)/shard_map/ppermute | solution.py:18
  81.7 2.0 %collective-permute-start.31 = (bf16[384,128]{1,0:T(8,128)(2,1)S(1)}, bf16[384,128]{1,0:T(8,128)(2,1)S(1)}, u32[]{:S(2)}, u32[]{:S(2)}) collective-permute-start(bf16[384,128]{1,0:T(8,128)(2,1)S(1)} %slice.241), channel_id=1, source_target_pairs={{0,1},{1,0},{2,3},{3,2},{4,5},{5,4},{6,7},{7,6},{8,9},{9,8},{10,11... | collective-permute-start | bytes 294920 | tf_op jit(solution)/shard_map/ppermute | solution.py:18
  83.7 0.8 collective-permute-done.33
  84.5 2.2 %collective-permute-done.32 = bf16[384,128]{1,0:T(8,128)(2,1)S(1)} collective-permute-done((bf16[384,128]{1,0:T(8,128)(2,1)S(1)}, bf16[384,128]{1,0:T(8,128)(2,1)S(1)}, u32[]{:S(2)}, u32[]{:S(2)}) %collective-permute-start.32) | collective-permute-done | bytes 98336 | tf_op jit(solution)/shard_map/ppermute | solution.py:18
  87.9 1.6 %collective-permute-start.34 = (bf16[384,128]{1,0:T(8,128)(2,1)S(1)}, bf16[384,128]{1,0:T(8,128)(2,1)S(1)}, u32[]{:S(2)}, u32[]{:S(2)}) collective-permute-start(bf16[384,128]{1,0:T(8,128)(2,1)S(1)} %get-tuple-element.39), channel_id=1, source_target_pairs={{0,8},{4,12},{8,0},{12,4},{16,24},{20,28},{24,16},{28,20},{1,9},{5... | collective-permute-start | bytes 294920 | tf_op jit(solution)/shard_map/ppermute | solution.py:18
  89.6 1.2 collective-permute-start.35
  90.7 0.7 collective-permute-start.36
  91.8 0.8 collective-permute-done.34
  92.9 1.2 collective-permute-done.35
  94.6 1.7 %collective-permute-done.36 = bf16[384,128]{1,0:T(8,128)(2,1)S(1)} collective-permute-done((bf16[384,128]{1,0:T(8,128)(2,1)S(1)}, bf16[384,128]{1,0:T(8,128)(2,1)S(1)}, u32[]{:S(2)}, u32[]{:S(2)}) %collective-permute-start.36) | collective-permute-done | bytes 98336 | tf_op jit(solution)/shard_map/ppermute | solution.py:18
  96.6 2.3 %collective-permute-start.39 = (bf16[384,128]{1,0:T(8,128)(2,1)S(1)}, bf16[384,128]{1,0:T(8,128)(2,1)S(1)}, u32[]{:S(2)}, u32[]{:S(2)}) collective-permute-start(bf16[384,128]{1,0:T(8,128)(2,1)S(1)} %get-tuple-element.52), channel_id=1, source_target_pairs={{0,3},{1,2},{2,1},{3,0},{4,7},{5,6},{6,5},{7,4},{8,11},{9,10},{10,... | collective-permute-start | bytes 294920 | tf_op jit(solution)/shard_map/ppermute | solution.py:18
  100.2 2.1 %collective-permute-start.37 = (bf16[384,128]{1,0:T(8,128)(2,1)S(1)}, bf16[384,128]{1,0:T(8,128)(2,1)S(1)}, u32[]{:S(2)}, u32[]{:S(2)}) collective-permute-start(bf16[384,128]{1,0:T(8,128)(2,1)S(1)} %slice.240), channel_id=1, source_target_pairs={{0,1},{1,0},{2,3},{3,2},{4,5},{5,4},{6,7},{7,6},{8,9},{9,8},{10,11... | collective-permute-start | bytes 294920 | tf_op jit(solution)/shard_map/ppermute | solution.py:18
  102.3 0.8 collective-permute-done.39
  103.1 2.2 %collective-permute-done.38 = bf16[384,128]{1,0:T(8,128)(2,1)S(1)} collective-permute-done((bf16[384,128]{1,0:T(8,128)(2,1)S(1)}, bf16[384,128]{1,0:T(8,128)(2,1)S(1)}, u32[]{:S(2)}, u32[]{:S(2)}) %collective-permute-start.38) | collective-permute-done | bytes 98336 | tf_op jit(solution)/shard_map/ppermute | solution.py:18
  106.5 1.2 collective-permute-start.41
  107.7 2.1 %collective-permute-start.42 = (bf16[384,128]{1,0:T(8,128)(2,1)S(1)}, bf16[384,128]{1,0:T(8,128)(2,1)S(1)}, u32[]{:S(2)}, u32[]{:S(2)}) collective-permute-start(bf16[384,128]{1,0:T(8,128)(2,1)S(1)} %get-tuple-element.37), channel_id=1, source_target_pairs={{0,24},{4,28},{8,16},{12,20},{16,8},{20,12},{24,0},{28,4},{1,25},{... | collective-permute-start | bytes 294920 | tf_op jit(solution)/shard_map/ppermute | solution.py:18
  110.2 0.8 collective-permute-done.40
  111.7 1.5 %collective-permute-done.42 = bf16[384,128]{1,0:T(8,128)(2,1)S(1)} collective-permute-done((bf16[384,128]{1,0:T(8,128)(2,1)S(1)}, bf16[384,128]{1,0:T(8,128)(2,1)S(1)}, u32[]{:S(2)}, u32[]{:S(2)}) %collective-permute-start.42) | collective-permute-done | bytes 98336 | tf_op jit(solution)/shard_map/ppermute | solution.py:18
  113.6 2.0 %collective-permute-start.45 = (bf16[384,128]{1,0:T(8,128)(2,1)S(1)}, bf16[384,128]{1,0:T(8,128)(2,1)S(1)}, u32[]{:S(2)}, u32[]{:S(2)}) collective-permute-start(bf16[384,128]{1,0:T(8,128)(2,1)S(1)} %get-tuple-element.50), channel_id=1, source_target_pairs={{0,3},{1,2},{2,1},{3,0},{4,7},{5,6},{6,5},{7,4},{8,11},{9,10},{10,... | collective-permute-start | bytes 294920 | tf_op jit(solution)/shard_map/ppermute | solution.py:18
  117.3 2.0 %collective-permute-start.43 = (bf16[384,128]{1,0:T(8,128)(2,1)S(1)}, bf16[384,128]{1,0:T(8,128)(2,1)S(1)}, u32[]{:S(2)}, u32[]{:S(2)}) collective-permute-start(bf16[384,128]{1,0:T(8,128)(2,1)S(1)} %slice.239), channel_id=1, source_target_pairs={{0,1},{1,0},{2,3},{3,2},{4,5},{5,4},{6,7},{7,6},{8,9},{9,8},{10,11... | collective-permute-start | bytes 294920 | tf_op jit(solution)/shard_map/ppermute | solution.py:18
  119.3 0.8 collective-permute-done.45
  120.1 5.2 %collective-permute-done.44 = bf16[384,128]{1,0:T(8,128)(2,1)S(1)} collective-permute-done((bf16[384,128]{1,0:T(8,128)(2,1)S(1)}, bf16[384,128]{1,0:T(8,128)(2,1)S(1)}, u32[]{:S(2)}, u32[]{:S(2)}) %collective-permute-start.44) | collective-permute-done | bytes 98336 | tf_op jit(solution)/shard_map/ppermute | solution.py:18
  125.8 1.6 %collective-permute-start.46 = (bf16[384,128]{1,0:T(8,128)(2,1)S(1)}, bf16[384,128]{1,0:T(8,128)(2,1)S(1)}, u32[]{:S(2)}, u32[]{:S(2)}) collective-permute-start(bf16[384,128]{1,0:T(8,128)(2,1)S(1)} %get-tuple-element.35), channel_id=1, source_target_pairs={{0,8},{4,12},{8,0},{12,4},{16,24},{20,28},{24,16},{28,20},{1,9},{5... | collective-permute-start | bytes 294920 | tf_op jit(solution)/shard_map/ppermute | solution.py:18
  127.4 1.6 %collective-permute-start.47 = (bf16[384,128]{1,0:T(8,128)(2,1)S(1)}, bf16[384,128]{1,0:T(8,128)(2,1)S(1)}, u32[]{:S(2)}, u32[]{:S(2)}) collective-permute-start(bf16[384,128]{1,0:T(8,128)(2,1)S(1)} %get-tuple-element.35), channel_id=1, source_target_pairs={{0,16},{4,20},{8,24},{12,28},{16,0},{20,4},{24,8},{28,12},{1,17},{... | collective-permute-start | bytes 294920 | tf_op jit(solution)/shard_map/ppermute | solution.py:18
  129.7 0.8 collective-permute-done.46
  131.1 0.9 collective-permute-done.47
  132.8 1.6 %collective-permute-done.48 = bf16[384,128]{1,0:T(8,128)(2,1)S(1)} collective-permute-done((bf16[384,128]{1,0:T(8,128)(2,1)S(1)}, bf16[384,128]{1,0:T(8,128)(2,1)S(1)}, u32[]{:S(2)}, u32[]{:S(2)}) %collective-permute-start.48) | collective-permute-done | bytes 98336 | tf_op jit(solution)/shard_map/ppermute | solution.py:18
  134.9 2.2 %collective-permute-start.51 = (bf16[384,128]{1,0:T(8,128)(2,1)S(1)}, bf16[384,128]{1,0:T(8,128)(2,1)S(1)}, u32[]{:S(2)}, u32[]{:S(2)}) collective-permute-start(bf16[384,128]{1,0:T(8,128)(2,1)S(1)} %get-tuple-element.48), channel_id=1, source_target_pairs={{0,3},{1,2},{2,1},{3,0},{4,7},{5,6},{6,5},{7,4},{8,11},{9,10},{10,... | collective-permute-start | bytes 294920 | tf_op jit(solution)/shard_map/ppermute | solution.py:18
  137.5 2.3 %collective-permute-start.49 = (bf16[384,128]{1,0:T(8,128)(2,1)S(1)}, bf16[384,128]{1,0:T(8,128)(2,1)S(1)}, u32[]{:S(2)}, u32[]{:S(2)}) collective-permute-start(bf16[384,128]{1,0:T(8,128)(2,1)S(1)} %slice.238), channel_id=1, source_target_pairs={{0,1},{1,0},{2,3},{3,2},{4,5},{5,4},{6,7},{7,6},{8,9},{9,8},{10,11... | collective-permute-start | bytes 294920 | tf_op jit(solution)/shard_map/ppermute | solution.py:18
  139.8 1.6 %collective-permute-done.51 = bf16[384,128]{1,0:T(8,128)(2,1)S(1)} collective-permute-done((bf16[384,128]{1,0:T(8,128)(2,1)S(1)}, bf16[384,128]{1,0:T(8,128)(2,1)S(1)}, u32[]{:S(2)}, u32[]{:S(2)}) %collective-permute-start.51) | collective-permute-done | bytes 98336 | tf_op jit(solution)/shard_map/ppermute | solution.py:18
  141.3 2.1 %collective-permute-done.50 = bf16[384,128]{1,0:T(8,128)(2,1)S(1)} collective-permute-done((bf16[384,128]{1,0:T(8,128)(2,1)S(1)}, bf16[384,128]{1,0:T(8,128)(2,1)S(1)}, u32[]{:S(2)}, u32[]{:S(2)}) %collective-permute-start.50) | collective-permute-done | bytes 98336 | tf_op jit(solution)/shard_map/ppermute | solution.py:18
  143.6 1.3 collective-permute-done.52
  (168 shorter events, 26.7 us)
Async XLA Ops:
  0.0 3.6 %copy-start = (bf16[1,8,12,64,1,128]{5,3,4,2,1,0:T(8,128)(2,1)S(1)}, bf16[1,8,12,64,1,128]{5,3,4,2,1,0:T(8,128)(2,1)}, u32[]{:S(2)}) copy-start(bf16[1,8,12,64,1,128]{5,3,4,2,1,0:T(8,128)(2,1)} %param.7) | copy-start | bytes 4718596
  1.0 8.2 %collective-permute-start.8 = (bf16[192,128]{1,0:T(8,128)(2,1)S(1)}, bf16[192,128]{1,0:T(8,128)(2,1)S(1)}, u32[]{:S(2)}, u32[]{:S(2)}) collective-permute-start(bf16[192,128]{1,0:T(8,128)(2,1)S(1)} %get-tuple-element.60), channel_id=1, source_target_pairs={{0,4},{4,0},{8,12},{12,8},{16,20},{20,16},{24,28},{28,24},{1,5},{5... | collective-permute-start | bytes 147464 | tf_op jit(solution)/shard_map/ppermute | solution.py:18
  3.5 14.6 %collective-permute-start = (s32[192]{0:T(256)S(1)}, s32[192]{0:T(256)S(1)}, u32[]{:S(2)}, u32[]{:S(2)}) collective-permute-start(s32[192]{0:T(256)S(1)} %broadcast_select_fusion.2), channel_id=1, source_target_pairs={{0,4},{4,0},{8,12},{12,8},{16,20},{20,16},{24,28},{28,24},{1,5},{5... | collective-permute-start | bytes 2312 | tf_op jit(solution)/shard_map/ppermute | solution.py:18
  3.7 8.7 %collective-permute-start.13 = (bf16[768,128]{1,0:T(8,128)(2,1)S(1)}, bf16[768,128]{1,0:T(8,128)(2,1)S(1)}, u32[]{:S(2)}, u32[]{:S(2)}) collective-permute-start(bf16[768,128]{1,0:T(8,128)(2,1)S(1)} %bitcast.138), channel_id=1, source_target_pairs={{0,8},{4,12},{8,0},{12,4},{16,24},{20,28},{24,16},{28,20},{1,9},{5... | collective-permute-start | bytes 589832 | tf_op jit(solution)/shard_map/ppermute | solution.py:18
  6.7 10.9 %collective-permute-start.14 = (bf16[768,128]{1,0:T(8,128)(2,1)S(1)}, bf16[768,128]{1,0:T(8,128)(2,1)S(1)}, u32[]{:S(2)}, u32[]{:S(2)}) collective-permute-start(bf16[768,128]{1,0:T(8,128)(2,1)S(1)} %bitcast.139), channel_id=1, source_target_pairs={{0,16},{4,20},{8,24},{12,28},{16,0},{20,4},{24,8},{28,12},{1,17},{... | collective-permute-start | bytes 589832 | tf_op jit(solution)/shard_map/ppermute | solution.py:18
  8.9 8.6 %collective-permute-start.15 = (bf16[768,128]{1,0:T(8,128)(2,1)}, bf16[768,128]{1,0:T(8,128)(2,1)S(1)}, u32[]{:S(2)}, u32[]{:S(2)}) collective-permute-start(bf16[768,128]{1,0:T(8,128)(2,1)} %bitcast.12), channel_id=1, source_target_pairs={{0,24},{4,28},{8,16},{12,20},{16,8},{20,12},{24,0},{28,4},{1,25},{... | collective-permute-start | bytes 589832 | tf_op jit(solution)/shard_map/ppermute | solution.py:18
  9.2 9.7 %collective-permute-start.16 = (bf16[768,128]{1,0:T(8,128)(2,1)S(1)}, bf16[768,128]{1,0:T(8,128)(2,1)S(1)}, u32[]{:S(2)}, u32[]{:S(2)}) collective-permute-start(bf16[768,128]{1,0:T(8,128)(2,1)S(1)} %bitcast.133), channel_id=1, source_target_pairs={{0,4},{4,0},{8,12},{12,8},{16,20},{20,16},{24,28},{28,24},{1,5},{5... | collective-permute-start | bytes 589832 | tf_op jit(solution)/shard_map/ppermute | solution.py:18
  12.4 7.9 %collective-permute-start.17 = (bf16[768,128]{1,0:T(8,128)(2,1)S(1)}, bf16[768,128]{1,0:T(8,128)(2,1)S(1)}, u32[]{:S(2)}, u32[]{:S(2)}) collective-permute-start(bf16[768,128]{1,0:T(8,128)(2,1)S(1)} %collective-permute-done.13.refs_1_), channel_id=1, source_target_pairs={{0,4},{4,0},{8,12},{12,8},{16,20},{20,16},{24,28},{28,24},{1,5},{5... | collective-permute-start | bytes 589832 | tf_op jit(solution)/shard_map/ppermute | solution.py:18
  17.5 4.2 %collective-permute-start.18 = (bf16[768,128]{1,0:T(8,128)(2,1)S(1)}, bf16[768,128]{1,0:T(8,128)(2,1)S(1)}, u32[]{:S(2)}, u32[]{:S(2)}) collective-permute-start(bf16[768,128]{1,0:T(8,128)(2,1)S(1)} %collective-permute-done.14.refs_2_), channel_id=1, source_target_pairs={{0,4},{4,0},{8,12},{12,8},{16,20},{20,16},{24,28},{28,24},{1,5},{5... | collective-permute-start | bytes 589832 | tf_op jit(solution)/shard_map/ppermute | solution.py:18
  17.5 4.8 %collective-permute-start.19 = (bf16[768,128]{1,0:T(8,128)(2,1)S(1)}, bf16[768,128]{1,0:T(8,128)(2,1)S(1)}, u32[]{:S(2)}, u32[]{:S(2)}) collective-permute-start(bf16[768,128]{1,0:T(8,128)(2,1)S(1)} %collective-permute-done.15.refs_3_), channel_id=1, source_target_pairs={{0,4},{4,0},{8,12},{12,8},{16,20},{20,16},{24,28},{28,24},{1,5},{5... | collective-permute-start | bytes 589832 | tf_op jit(solution)/shard_map/ppermute | solution.py:18
  18.1 6.0 %collective-permute-start.9 = (bf16[384,128]{1,0:T(8,128)(2,1)S(1)}, bf16[384,128]{1,0:T(8,128)(2,1)S(1)}, u32[]{:S(2)}, u32[]{:S(2)}) collective-permute-start(bf16[384,128]{1,0:T(8,128)(2,1)S(1)} %pad_maximum_fusion), channel_id=1, source_target_pairs={{0,8},{4,12},{8,0},{12,4},{16,24},{20,28},{24,16},{28,20},{1,9},{5... | collective-permute-start | bytes 294920 | tf_op jit(solution)/shard_map/ppermute | solution.py:18
  18.9 16.6 %collective-permute-start.1 = (bf16[768,128]{1,0:T(8,128)(2,1)S(1)}, bf16[768,128]{1,0:T(8,128)(2,1)S(1)}, u32[]{:S(2)}, u32[]{:S(2)}) collective-permute-start(bf16[768,128]{1,0:T(8,128)(2,1)S(1)} %bitcast.135), channel_id=1, source_target_pairs={{0,8},{4,12},{8,0},{12,4},{16,24},{20,28},{24,16},{28,20},{1,9},{5... | collective-permute-start | bytes 589832 | tf_op jit(solution)/shard_map/ppermute | solution.py:18
  20.2 15.2 %collective-permute-start.2 = (bf16[768,128]{1,0:T(8,128)(2,1)S(1)}, bf16[768,128]{1,0:T(8,128)(2,1)S(1)}, u32[]{:S(2)}, u32[]{:S(2)}) collective-permute-start(bf16[768,128]{1,0:T(8,128)(2,1)S(1)} %bitcast.136), channel_id=1, source_target_pairs={{0,16},{4,20},{8,24},{12,28},{16,0},{20,4},{24,8},{28,12},{1,17},{... | collective-permute-start | bytes 589832 | tf_op jit(solution)/shard_map/ppermute | solution.py:18
  21.8 14.2 %collective-permute-start.3 = (bf16[768,128]{1,0:T(8,128)(2,1)S(1)}, bf16[768,128]{1,0:T(8,128)(2,1)S(1)}, u32[]{:S(2)}, u32[]{:S(2)}) collective-permute-start(bf16[768,128]{1,0:T(8,128)(2,1)S(1)} %bitcast.137), channel_id=1, source_target_pairs={{0,24},{4,28},{8,16},{12,20},{16,8},{20,12},{24,0},{28,4},{1,25},{... | collective-permute-start | bytes 589832 | tf_op jit(solution)/shard_map/ppermute | solution.py:18
  22.4 20.7 %collective-permute-start.4 = (bf16[768,128]{1,0:T(8,128)(2,1)S(1)}, bf16[768,128]{1,0:T(8,128)(2,1)S(1)}, u32[]{:S(2)}, u32[]{:S(2)}) collective-permute-start(bf16[768,128]{1,0:T(8,128)(2,1)S(1)} %bitcast.131), channel_id=1, source_target_pairs={{0,4},{4,0},{8,12},{12,8},{16,20},{20,16},{24,28},{28,24},{1,5},{5... | collective-permute-start | bytes 589832 | tf_op jit(solution)/shard_map/ppermute | solution.py:18
  24.1 9.4 %collective-permute-start.10 = (bf16[384,128]{1,0:T(8,128)(2,1)S(1)}, bf16[384,128]{1,0:T(8,128)(2,1)S(1)}, u32[]{:S(2)}, u32[]{:S(2)}) collective-permute-start(bf16[384,128]{1,0:T(8,128)(2,1)S(1)} %pad_maximum_fusion), channel_id=1, source_target_pairs={{0,16},{4,20},{8,24},{12,28},{16,0},{20,4},{24,8},{28,12},{1,17},{... | collective-permute-start | bytes 294920 | tf_op jit(solution)/shard_map/ppermute | solution.py:18
  33.5 5.5 %collective-permute-start.11 = (bf16[384,128]{1,0:T(8,128)(2,1)S(1)}, bf16[384,128]{1,0:T(8,128)(2,1)S(1)}, u32[]{:S(2)}, u32[]{:S(2)}) collective-permute-start(bf16[384,128]{1,0:T(8,128)(2,1)S(1)} %pad_maximum_fusion), channel_id=1, source_target_pairs={{0,24},{4,28},{8,16},{12,20},{16,8},{20,12},{24,0},{28,4},{1,25},{... | collective-permute-start | bytes 294920 | tf_op jit(solution)/shard_map/ppermute | solution.py:18
  35.4 7.6 %collective-permute-start.5 = (bf16[768,128]{1,0:T(8,128)(2,1)S(1)}, bf16[768,128]{1,0:T(8,128)(2,1)S(1)}, u32[]{:S(2)}, u32[]{:S(2)}) collective-permute-start(bf16[768,128]{1,0:T(8,128)(2,1)S(1)} %collective-permute-done.1.refs_1_), channel_id=1, source_target_pairs={{0,4},{4,0},{8,12},{12,8},{16,20},{20,16},{24,28},{28,24},{1,5},{5... | collective-permute-start | bytes 589832 | tf_op jit(solution)/shard_map/ppermute | solution.py:18
  35.4 7.6 %collective-permute-start.6 = (bf16[768,128]{1,0:T(8,128)(2,1)S(1)}, bf16[768,128]{1,0:T(8,128)(2,1)S(1)}, u32[]{:S(2)}, u32[]{:S(2)}) collective-permute-start(bf16[768,128]{1,0:T(8,128)(2,1)S(1)} %collective-permute-done.2.refs_2_), channel_id=1, source_target_pairs={{0,4},{4,0},{8,12},{12,8},{16,20},{20,16},{24,28},{28,24},{1,5},{5... | collective-permute-start | bytes 589832 | tf_op jit(solution)/shard_map/ppermute | solution.py:18
  35.9 7.1 %collective-permute-start.7 = (bf16[768,128]{1,0:T(8,128)(2,1)S(1)}, bf16[768,128]{1,0:T(8,128)(2,1)S(1)}, u32[]{:S(2)}, u32[]{:S(2)}) collective-permute-start(bf16[768,128]{1,0:T(8,128)(2,1)S(1)} %collective-permute-done.3.refs_3_), channel_id=1, source_target_pairs={{0,4},{4,0},{8,12},{12,8},{16,20},{20,16},{24,28},{28,24},{1,5},{5... | collective-permute-start | bytes 589832 | tf_op jit(solution)/shard_map/ppermute | solution.py:18
  39.4 9.0 %collective-permute-start.21 = (bf16[384,128]{1,0:T(8,128)(2,1)S(1)}, bf16[384,128]{1,0:T(8,128)(2,1)S(1)}, u32[]{:S(2)}, u32[]{:S(2)}) collective-permute-start(bf16[384,128]{1,0:T(8,128)(2,1)S(1)} %get-tuple-element.58), channel_id=1, source_target_pairs={{0,3},{1,2},{2,1},{3,0},{4,7},{5,6},{6,5},{7,4},{8,11},{9,10},{10,... | collective-permute-start | bytes 294920 | tf_op jit(solution)/shard_map/ppermute | solution.py:18
  43.0 7.3 %collective-permute-start.20 = (bf16[384,128]{1,0:T(8,128)(2,1)S(1)}, bf16[384,128]{1,0:T(8,128)(2,1)S(1)}, u32[]{:S(2)}, u32[]{:S(2)}) collective-permute-start(bf16[384,128]{1,0:T(8,128)(2,1)S(1)} %get-tuple-element.57), channel_id=1, source_target_pairs={{0,2},{1,3},{2,0},{3,1},{4,6},{5,7},{6,4},{7,5},{8,10},{9,11},{10,... | collective-permute-start | bytes 294920 | tf_op jit(solution)/shard_map/ppermute | solution.py:18
  46.2 5.1 %collective-permute-start.12 = (bf16[384,128]{1,0:T(8,128)(2,1)S(1)}, bf16[384,128]{1,0:T(8,128)(2,1)S(1)}, u32[]{:S(2)}, u32[]{:S(2)}) collective-permute-start(bf16[384,128]{1,0:T(8,128)(2,1)S(1)} %slice.243), channel_id=1, source_target_pairs={{0,1},{1,0},{2,3},{3,2},{4,5},{5,4},{6,7},{7,6},{8,9},{9,8},{10,11... | collective-permute-start | bytes 294920 | tf_op jit(solution)/shard_map/ppermute | solution.py:18
  51.8 5.1 %collective-permute-start.22 = (bf16[384,128]{1,0:T(8,128)(2,1)S(1)}, bf16[384,128]{1,0:T(8,128)(2,1)S(1)}, u32[]{:S(2)}, u32[]{:S(2)}) collective-permute-start(bf16[384,128]{1,0:T(8,128)(2,1)S(1)} %get-tuple-element.43), channel_id=1, source_target_pairs={{0,8},{4,12},{8,0},{12,4},{16,24},{20,28},{24,16},{28,20},{1,9},{5... | collective-permute-start | bytes 294920 | tf_op jit(solution)/shard_map/ppermute | solution.py:18
  52.9 5.9 %collective-permute-start.23 = (bf16[384,128]{1,0:T(8,128)(2,1)S(1)}, bf16[384,128]{1,0:T(8,128)(2,1)S(1)}, u32[]{:S(2)}, u32[]{:S(2)}) collective-permute-start(bf16[384,128]{1,0:T(8,128)(2,1)S(1)} %get-tuple-element.43), channel_id=1, source_target_pairs={{0,16},{4,20},{8,24},{12,28},{16,0},{20,4},{24,8},{28,12},{1,17},{... | collective-permute-start | bytes 294920 | tf_op jit(solution)/shard_map/ppermute | solution.py:18
  55.1 5.5 %collective-permute-start.24 = (bf16[384,128]{1,0:T(8,128)(2,1)S(1)}, bf16[384,128]{1,0:T(8,128)(2,1)S(1)}, u32[]{:S(2)}, u32[]{:S(2)}) collective-permute-start(bf16[384,128]{1,0:T(8,128)(2,1)S(1)} %get-tuple-element.43), channel_id=1, source_target_pairs={{0,24},{4,28},{8,16},{12,20},{16,8},{20,12},{24,0},{28,4},{1,25},{... | collective-permute-start | bytes 294920 | tf_op jit(solution)/shard_map/ppermute | solution.py:18
  61.0 6.5 %collective-permute-start.27 = (bf16[384,128]{1,0:T(8,128)(2,1)S(1)}, bf16[384,128]{1,0:T(8,128)(2,1)S(1)}, u32[]{:S(2)}, u32[]{:S(2)}) collective-permute-start(bf16[384,128]{1,0:T(8,128)(2,1)S(1)} %get-tuple-element.56), channel_id=1, source_target_pairs={{0,3},{1,2},{2,1},{3,0},{4,7},{5,6},{6,5},{7,4},{8,11},{9,10},{10,... | collective-permute-start | bytes 294920 | tf_op jit(solution)/shard_map/ppermute | solution.py:18
  63.4 6.3 %collective-permute-start.26 = (bf16[384,128]{1,0:T(8,128)(2,1)S(1)}, bf16[384,128]{1,0:T(8,128)(2,1)S(1)}, u32[]{:S(2)}, u32[]{:S(2)}) collective-permute-start(bf16[384,128]{1,0:T(8,128)(2,1)S(1)} %get-tuple-element.55), channel_id=1, source_target_pairs={{0,2},{1,3},{2,0},{3,1},{4,6},{5,7},{6,4},{7,5},{8,10},{9,11},{10,... | collective-permute-start | bytes 294920 | tf_op jit(solution)/shard_map/ppermute | solution.py:18
  64.5 5.8 %collective-permute-start.25 = (bf16[384,128]{1,0:T(8,128)(2,1)S(1)}, bf16[384,128]{1,0:T(8,128)(2,1)S(1)}, u32[]{:S(2)}, u32[]{:S(2)}) collective-permute-start(bf16[384,128]{1,0:T(8,128)(2,1)S(1)} %slice.242), channel_id=1, source_target_pairs={{0,1},{1,0},{2,3},{3,2},{4,5},{5,4},{6,7},{7,6},{8,9},{9,8},{10,11... | collective-permute-start | bytes 294920 | tf_op jit(solution)/shard_map/ppermute | solution.py:18
  70.7 4.7 %collective-permute-start.28 = (bf16[384,128]{1,0:T(8,128)(2,1)S(1)}, bf16[384,128]{1,0:T(8,128)(2,1)S(1)}, u32[]{:S(2)}, u32[]{:S(2)}) collective-permute-start(bf16[384,128]{1,0:T(8,128)(2,1)S(1)} %get-tuple-element.41), channel_id=1, source_target_pairs={{0,8},{4,12},{8,0},{12,4},{16,24},{20,28},{24,16},{28,20},{1,9},{5... | collective-permute-start | bytes 294920 | tf_op jit(solution)/shard_map/ppermute | solution.py:18
  70.9 4.8 %collective-permute-start.29 = (bf16[384,128]{1,0:T(8,128)(2,1)S(1)}, bf16[384,128]{1,0:T(8,128)(2,1)S(1)}, u32[]{:S(2)}, u32[]{:S(2)}) collective-permute-start(bf16[384,128]{1,0:T(8,128)(2,1)S(1)} %get-tuple-element.41), channel_id=1, source_target_pairs={{0,16},{4,20},{8,24},{12,28},{16,0},{20,4},{24,8},{28,12},{1,17},{... | collective-permute-start | bytes 294920 | tf_op jit(solution)/shard_map/ppermute | solution.py:18
  72.2 5.5 %collective-permute-start.30 = (bf16[384,128]{1,0:T(8,128)(2,1)S(1)}, bf16[384,128]{1,0:T(8,128)(2,1)S(1)}, u32[]{:S(2)}, u32[]{:S(2)}) collective-permute-start(bf16[384,128]{1,0:T(8,128)(2,1)S(1)} %get-tuple-element.41), channel_id=1, source_target_pairs={{0,24},{4,28},{8,16},{12,20},{16,8},{20,12},{24,0},{28,4},{1,25},{... | collective-permute-start | bytes 294920 | tf_op jit(solution)/shard_map/ppermute | solution.py:18
  78.1 6.5 %collective-permute-start.33 = (bf16[384,128]{1,0:T(8,128)(2,1)S(1)}, bf16[384,128]{1,0:T(8,128)(2,1)S(1)}, u32[]{:S(2)}, u32[]{:S(2)}) collective-permute-start(bf16[384,128]{1,0:T(8,128)(2,1)S(1)} %get-tuple-element.54), channel_id=1, source_target_pairs={{0,3},{1,2},{2,1},{3,0},{4,7},{5,6},{6,5},{7,4},{8,11},{9,10},{10,... | collective-permute-start | bytes 294920 | tf_op jit(solution)/shard_map/ppermute | solution.py:18
  80.0 6.8 %collective-permute-start.32 = (bf16[384,128]{1,0:T(8,128)(2,1)S(1)}, bf16[384,128]{1,0:T(8,128)(2,1)S(1)}, u32[]{:S(2)}, u32[]{:S(2)}) collective-permute-start(bf16[384,128]{1,0:T(8,128)(2,1)S(1)} %get-tuple-element.53), channel_id=1, source_target_pairs={{0,2},{1,3},{2,0},{3,1},{4,6},{5,7},{6,4},{7,5},{8,10},{9,11},{10,... | collective-permute-start | bytes 294920 | tf_op jit(solution)/shard_map/ppermute | solution.py:18
  81.7 5.7 %collective-permute-start.31 = (bf16[384,128]{1,0:T(8,128)(2,1)S(1)}, bf16[384,128]{1,0:T(8,128)(2,1)S(1)}, u32[]{:S(2)}, u32[]{:S(2)}) collective-permute-start(bf16[384,128]{1,0:T(8,128)(2,1)S(1)} %slice.241), channel_id=1, source_target_pairs={{0,1},{1,0},{2,3},{3,2},{4,5},{5,4},{6,7},{7,6},{8,9},{9,8},{10,11... | collective-permute-start | bytes 294920 | tf_op jit(solution)/shard_map/ppermute | solution.py:18
  87.9 4.7 %collective-permute-start.34 = (bf16[384,128]{1,0:T(8,128)(2,1)S(1)}, bf16[384,128]{1,0:T(8,128)(2,1)S(1)}, u32[]{:S(2)}, u32[]{:S(2)}) collective-permute-start(bf16[384,128]{1,0:T(8,128)(2,1)S(1)} %get-tuple-element.39), channel_id=1, source_target_pairs={{0,8},{4,12},{8,0},{12,4},{16,24},{20,28},{24,16},{28,20},{1,9},{5... | collective-permute-start | bytes 294920 | tf_op jit(solution)/shard_map/ppermute | solution.py:18
  89.6 4.6 %collective-permute-start.35 = (bf16[384,128]{1,0:T(8,128)(2,1)S(1)}, bf16[384,128]{1,0:T(8,128)(2,1)S(1)}, u32[]{:S(2)}, u32[]{:S(2)}) collective-permute-start(bf16[384,128]{1,0:T(8,128)(2,1)S(1)} %get-tuple-element.39), channel_id=1, source_target_pairs={{0,16},{4,20},{8,24},{12,28},{16,0},{20,4},{24,8},{28,12},{1,17},{... | collective-permute-start | bytes 294920 | tf_op jit(solution)/shard_map/ppermute | solution.py:18
  90.7 5.5 %collective-permute-start.36 = (bf16[384,128]{1,0:T(8,128)(2,1)S(1)}, bf16[384,128]{1,0:T(8,128)(2,1)S(1)}, u32[]{:S(2)}, u32[]{:S(2)}) collective-permute-start(bf16[384,128]{1,0:T(8,128)(2,1)S(1)} %get-tuple-element.39), channel_id=1, source_target_pairs={{0,24},{4,28},{8,16},{12,20},{16,8},{20,12},{24,0},{28,4},{1,25},{... | collective-permute-start | bytes 294920 | tf_op jit(solution)/shard_map/ppermute | solution.py:18
  96.6 6.5 %collective-permute-start.39 = (bf16[384,128]{1,0:T(8,128)(2,1)S(1)}, bf16[384,128]{1,0:T(8,128)(2,1)S(1)}, u32[]{:S(2)}, u32[]{:S(2)}) collective-permute-start(bf16[384,128]{1,0:T(8,128)(2,1)S(1)} %get-tuple-element.52), channel_id=1, source_target_pairs={{0,3},{1,2},{2,1},{3,0},{4,7},{5,6},{6,5},{7,4},{8,11},{9,10},{10,... | collective-permute-start | bytes 294920 | tf_op jit(solution)/shard_map/ppermute | solution.py:18
  99.0 6.4 %collective-permute-start.38 = (bf16[384,128]{1,0:T(8,128)(2,1)S(1)}, bf16[384,128]{1,0:T(8,128)(2,1)S(1)}, u32[]{:S(2)}, u32[]{:S(2)}) collective-permute-start(bf16[384,128]{1,0:T(8,128)(2,1)S(1)} %get-tuple-element.51), channel_id=1, source_target_pairs={{0,2},{1,3},{2,0},{3,1},{4,6},{5,7},{6,4},{7,5},{8,10},{9,11},{10,... | collective-permute-start | bytes 294920 | tf_op jit(solution)/shard_map/ppermute | solution.py:18
  100.2 5.7 %collective-permute-start.37 = (bf16[384,128]{1,0:T(8,128)(2,1)S(1)}, bf16[384,128]{1,0:T(8,128)(2,1)S(1)}, u32[]{:S(2)}, u32[]{:S(2)}) collective-permute-start(bf16[384,128]{1,0:T(8,128)(2,1)S(1)} %slice.240), channel_id=1, source_target_pairs={{0,1},{1,0},{2,3},{3,2},{4,5},{5,4},{6,7},{7,6},{8,9},{9,8},{10,11... | collective-permute-start | bytes 294920 | tf_op jit(solution)/shard_map/ppermute | solution.py:18
  106.3 4.7 %collective-permute-start.40 = (bf16[384,128]{1,0:T(8,128)(2,1)S(1)}, bf16[384,128]{1,0:T(8,128)(2,1)S(1)}, u32[]{:S(2)}, u32[]{:S(2)}) collective-permute-start(bf16[384,128]{1,0:T(8,128)(2,1)S(1)} %get-tuple-element.37), channel_id=1, source_target_pairs={{0,8},{4,12},{8,0},{12,4},{16,24},{20,28},{24,16},{28,20},{1,9},{5... | collective-permute-start | bytes 294920 | tf_op jit(solution)/shard_map/ppermute | solution.py:18
  106.5 4.8 %collective-permute-start.41 = (bf16[384,128]{1,0:T(8,128)(2,1)S(1)}, bf16[384,128]{1,0:T(8,128)(2,1)S(1)}, u32[]{:S(2)}, u32[]{:S(2)}) collective-permute-start(bf16[384,128]{1,0:T(8,128)(2,1)S(1)} %get-tuple-element.37), channel_id=1, source_target_pairs={{0,16},{4,20},{8,24},{12,28},{16,0},{20,4},{24,8},{28,12},{1,17},{... | collective-permute-start | bytes 294920 | tf_op jit(solution)/shard_map/ppermute | solution.py:18
  107.7 5.5 %collective-permute-start.42 = (bf16[384,128]{1,0:T(8,128)(2,1)S(1)}, bf16[384,128]{1,0:T(8,128)(2,1)S(1)}, u32[]{:S(2)}, u32[]{:S(2)}) collective-permute-start(bf16[384,128]{1,0:T(8,128)(2,1)S(1)} %get-tuple-element.37), channel_id=1, source_target_pairs={{0,24},{4,28},{8,16},{12,20},{16,8},{20,12},{24,0},{28,4},{1,25},{... | collective-permute-start | bytes 294920 | tf_op jit(solution)/shard_map/ppermute | solution.py:18
  113.6 6.5 %collective-permute-start.45 = (bf16[384,128]{1,0:T(8,128)(2,1)S(1)}, bf16[384,128]{1,0:T(8,128)(2,1)S(1)}, u32[]{:S(2)}, u32[]{:S(2)}) collective-permute-start(bf16[384,128]{1,0:T(8,128)(2,1)S(1)} %get-tuple-element.50), channel_id=1, source_target_pairs={{0,3},{1,2},{2,1},{3,0},{4,7},{5,6},{6,5},{7,4},{8,11},{9,10},{10,... | collective-permute-start | bytes 294920 | tf_op jit(solution)/shard_map/ppermute | solution.py:18
  115.6 9.8 %collective-permute-start.44 = (bf16[384,128]{1,0:T(8,128)(2,1)S(1)}, bf16[384,128]{1,0:T(8,128)(2,1)S(1)}, u32[]{:S(2)}, u32[]{:S(2)}) collective-permute-start(bf16[384,128]{1,0:T(8,128)(2,1)S(1)} %get-tuple-element.49), channel_id=1, source_target_pairs={{0,2},{1,3},{2,0},{3,1},{4,6},{5,7},{6,4},{7,5},{8,10},{9,11},{10,... | collective-permute-start | bytes 294920 | tf_op jit(solution)/shard_map/ppermute | solution.py:18
  117.3 8.1 %collective-permute-start.43 = (bf16[384,128]{1,0:T(8,128)(2,1)S(1)}, bf16[384,128]{1,0:T(8,128)(2,1)S(1)}, u32[]{:S(2)}, u32[]{:S(2)}) collective-permute-start(bf16[384,128]{1,0:T(8,128)(2,1)S(1)} %slice.239), channel_id=1, source_target_pairs={{0,1},{1,0},{2,3},{3,2},{4,5},{5,4},{6,7},{7,6},{8,9},{9,8},{10,11... | collective-permute-start | bytes 294920 | tf_op jit(solution)/shard_map/ppermute | solution.py:18
  125.8 4.7 %collective-permute-start.46 = (bf16[384,128]{1,0:T(8,128)(2,1)S(1)}, bf16[384,128]{1,0:T(8,128)(2,1)S(1)}, u32[]{:S(2)}, u32[]{:S(2)}) collective-permute-start(bf16[384,128]{1,0:T(8,128)(2,1)S(1)} %get-tuple-element.35), channel_id=1, source_target_pairs={{0,8},{4,12},{8,0},{12,4},{16,24},{20,28},{24,16},{28,20},{1,9},{5... | collective-permute-start | bytes 294920 | tf_op jit(solution)/shard_map/ppermute | solution.py:18
  127.4 4.6 %collective-permute-start.47 = (bf16[384,128]{1,0:T(8,128)(2,1)S(1)}, bf16[384,128]{1,0:T(8,128)(2,1)S(1)}, u32[]{:S(2)}, u32[]{:S(2)}) collective-permute-start(bf16[384,128]{1,0:T(8,128)(2,1)S(1)} %get-tuple-element.35), channel_id=1, source_target_pairs={{0,16},{4,20},{8,24},{12,28},{16,0},{20,4},{24,8},{28,12},{1,17},{... | collective-permute-start | bytes 294920 | tf_op jit(solution)/shard_map/ppermute | solution.py:18
  128.9 5.5 %collective-permute-start.48 = (bf16[384,128]{1,0:T(8,128)(2,1)S(1)}, bf16[384,128]{1,0:T(8,128)(2,1)S(1)}, u32[]{:S(2)}, u32[]{:S(2)}) collective-permute-start(bf16[384,128]{1,0:T(8,128)(2,1)S(1)} %get-tuple-element.35), channel_id=1, source_target_pairs={{0,24},{4,28},{8,16},{12,20},{16,8},{20,12},{24,0},{28,4},{1,25},{... | collective-permute-start | bytes 294920 | tf_op jit(solution)/shard_map/ppermute | solution.py:18
  134.9 6.5 %collective-permute-start.51 = (bf16[384,128]{1,0:T(8,128)(2,1)S(1)}, bf16[384,128]{1,0:T(8,128)(2,1)S(1)}, u32[]{:S(2)}, u32[]{:S(2)}) collective-permute-start(bf16[384,128]{1,0:T(8,128)(2,1)S(1)} %get-tuple-element.48), channel_id=1, source_target_pairs={{0,3},{1,2},{2,1},{3,0},{4,7},{5,6},{6,5},{7,4},{8,11},{9,10},{10,... | collective-permute-start | bytes 294920 | tf_op jit(solution)/shard_map/ppermute | solution.py:18
  137.1 6.3 %collective-permute-start.50 = (bf16[384,128]{1,0:T(8,128)(2,1)S(1)}, bf16[384,128]{1,0:T(8,128)(2,1)S(1)}, u32[]{:S(2)}, u32[]{:S(2)}) collective-permute-start(bf16[384,128]{1,0:T(8,128)(2,1)S(1)} %get-tuple-element.47), channel_id=1, source_target_pairs={{0,2},{1,3},{2,0},{3,1},{4,6},{5,7},{6,4},{7,5},{8,10},{9,11},{10,... | collective-permute-start | bytes 294920 | tf_op jit(solution)/shard_map/ppermute | solution.py:18
  137.5 6.0 %collective-permute-start.49 = (bf16[384,128]{1,0:T(8,128)(2,1)S(1)}, bf16[384,128]{1,0:T(8,128)(2,1)S(1)}, u32[]{:S(2)}, u32[]{:S(2)}) collective-permute-start(bf16[384,128]{1,0:T(8,128)(2,1)S(1)} %slice.238), channel_id=1, source_target_pairs={{0,1},{1,0},{2,3},{3,2},{4,5},{5,4},{6,7},{7,6},{8,9},{9,8},{10,11... | collective-permute-start | bytes 294920 | tf_op jit(solution)/shard_map/ppermute | solution.py:18
  143.5 1.4 collective-permute-start.52
